TPU v7x, 32 devices: a whole 2x2x4 slice. The times are simulated.
32 devices in a mesh: rows: 16 (over z, x, core), seq: 2 (over y).
Axes of the slice: x: 2, y: 2, z: 4, core: 2. Of those that a mesh axis runs over, the one named last changes fastest.
Arguments:
- tokens: bfloat16 [16, 1888, 768], P('rows', 'seq'), may hold values from -6 to 6
- cotangent: bfloat16 [16, 1888, 768], P('rows', 'seq'), may hold values from -6 to 6
- segment_ids: int32 [16, 1888], P('rows'), may hold values from 0 to 3, as said below
- routing: int32 [16, 1888], P('rows'), may hold values from 0 to 943, as said below
- qkv_weight: bfloat16 [768, 2304], replicated, may hold values from -0.21875 to 0.21875
- query_bias: bfloat16 [768], replicated, may hold values from -1 to 1
- value_bias: bfloat16 [768], replicated, may hold values from -1 to 1
- out_weight: bfloat16 [768, 768], replicated, may hold values from -0.875 to 0.875
- out_bias: bfloat16 [768], replicated, may hold values from -1 to 1
- first_scale: bfloat16 [768], replicated, may hold values from 0.5 to 1.5
- first_offset: bfloat16 [768], replicated, may hold values from -1 to 1
- second_scale: bfloat16 [768], replicated, may hold values from 0.5 to 1.5
- second_offset: bfloat16 [768], replicated, may hold values from -1 to 1
- up_weight: bfloat16 [768, 3072], replicated, may hold values from -0.21875 to 0.21875
- up_bias: bfloat16 [3072], replicated, may hold values from -1 to 1
- down_weight: bfloat16 [3072, 768], replicated, may hold values from -0.109375 to 0.109375
- down_bias: bfloat16 [768], replicated, may hold values from -1 to 1
- router_weight: bfloat16 [768], replicated, may hold values from -0.21875 to 0.21875
Outputs:
- out_tokens: bfloat16 [16, 1888, 768], P('rows', 'seq')
- grad_tokens: bfloat16 [16, 1888, 768], P('rows', 'seq')
- grad_qkv_weight: float32 [768, 2304], replicated
- grad_query_bias: float32 [768], replicated
- grad_value_bias: float32 [768], replicated
- grad_out_weight: float32 [768, 768], replicated
- grad_out_bias: float32 [768], replicated
- grad_first_scale: float32 [768], replicated
- grad_first_offset: float32 [768], replicated
- grad_second_scale: float32 [768], replicated
- grad_second_offset: float32 [768], replicated
- grad_up_weight: float32 [768, 3072], replicated
- grad_up_bias: float32 [3072], replicated
- grad_down_weight: float32 [3072, 768], replicated
- grad_down_bias: float32 [768], replicated
- grad_router_weight: float32 [768], replicated
Inputs may be any that keep to these rules, and one draw needn't show every extreme that they name: `segment_ids`: in each row the ids start at 0 and rise by one at each new image; every image but a row's first and last has 577 slots, and the image that holds slot 944 also holds slot 943. `routing`: each aligned block of 944 entries of a row is an order of 0 to 943.
All inputs are finite; a program needn't handle non-finite values.
Results may differ from a plain program's by a relative error of at most 0.012.
Values may be sent and summed in bfloat16 or wider, within the bound.
No kernel may reach another device: no remote copies, remote signals or barrier semaphores. Data moves between devices by JAX's collectives and lax.ppermute only.
A program may use at most 192 MiB of HBM per device.

v0:
```python
import jax
import jax.numpy as jnp
from jax import lax
from jax.sharding import PartitionSpec as P

H = 12
HD = 64


def from_behind(block, axis, distance):
    devices = range(lax.axis_size(axis))
    route = [((i - distance) % len(devices), i) for i in devices]
    return lax.ppermute(block, axis, route)


def layer_norm(values, scaling, offset):
    center = values - jnp.mean(values, axis=-1, keepdims=True)
    inverse = lax.rsqrt(jnp.mean(center * center, axis=-1, keepdims=True) + 1e-06)
    return center * inverse * scaling + offset


def gelu_tanh(activation):
    return jax.nn.gelu(activation, approximate=True)


def pick_rows(source_rows, indices):
    return jnp.take_along_axis(source_rows, indices[:, :, None], axis=1)


def masked_scores(queries, key_rows, query_segment, key_segment):
    scores = jnp.einsum(
        "rqhd,rkhd->rhqk", queries, key_rows, preferred_element_type=jnp.float32
    ) * HD ** (-0.5)
    allowed = (query_segment[:, :, None] == key_segment[:, None, :])[:, None]
    return jnp.where(allowed, scores, -jnp.inf)


def padded_vector(members):
    joined = jnp.concatenate([member for member in members])
    return joined


def body(
    tokens,
    cotangent,
    segment_ids,
    routing,
    qkv_weight,
    query_bias,
    value_bias,
    out_weight,
    out_bias,
    first_scale,
    first_offset,
    second_scale,
    second_offset,
    up_weight,
    up_bias,
    down_weight,
    down_bias,
    router_weight,
):
    row_count, slot_count, model_width = tokens.shape
    hidden_width = up_weight.shape[1]
    routed_count = slot_count // 2
    head_shape = (row_count, routed_count, H, HD)
    flat_shape = (row_count, routed_count, model_width)
    position = lax.axis_index("seq")
    other_position = 1 - position
    own_route = lax.dynamic_slice_in_dim(routing, position * slot_count, slot_count, 1)
    other_route = lax.dynamic_slice_in_dim(routing, other_position * slot_count, slot_count, 1)
    own_groups = lax.dynamic_slice_in_dim(segment_ids, position * slot_count, slot_count, 1)
    other_groups = lax.dynamic_slice_in_dim(segment_ids, other_position * slot_count, slot_count, 1)
    chosen = own_route[:, :routed_count]
    query_segment = jnp.take_along_axis(own_groups, chosen, axis=1)
    remote_segment = jnp.take_along_axis(other_groups, other_route[:, :routed_count], axis=1)
    norm_one = (first_scale.astype(jnp.float32), first_offset.astype(jnp.float32))
    norm_two = (second_scale.astype(jnp.float32), second_offset.astype(jnp.float32))
    routed_in = pick_rows(tokens, chosen)
    routed_float = routed_in.astype(jnp.float32)
    router_logit = jnp.einsum(
        "rtd,d->rt", routed_in, router_weight, preferred_element_type=jnp.float32
    )
    gate_value = jax.nn.sigmoid(router_logit)
    first_norm = layer_norm(routed_float, norm_one[0], norm_one[1]).astype(jnp.bfloat16)
    projected = jnp.einsum(
        "rtd,de->rte", first_norm, qkv_weight, preferred_element_type=jnp.float32
    )
    queries = (projected[..., :model_width] + query_bias).astype(jnp.bfloat16).reshape(head_shape)
    key_rows = (
        projected[..., model_width : 2 * model_width].astype(jnp.bfloat16).reshape(head_shape)
    )
    values = (
        (projected[..., 2 * model_width :] + value_bias).astype(jnp.bfloat16).reshape(head_shape)
    )
    received = from_behind(jnp.stack([key_rows, values]), "seq", 1)
    remote_keys = received[0]
    remote_values = received[1]
    local_scores = masked_scores(queries, key_rows, query_segment, query_segment)
    remote_scores = masked_scores(queries, remote_keys, query_segment, remote_segment)
    row_top = jnp.maximum(
        jnp.max(local_scores, axis=-1, keepdims=True),
        jnp.max(remote_scores, axis=-1, keepdims=True),
    )
    row_total = jnp.sum(jnp.exp(local_scores - row_top), axis=-1, keepdims=True) + jnp.sum(
        jnp.exp(remote_scores - row_top), axis=-1, keepdims=True
    )
    log_total = row_top + jnp.log(row_total)
    local_low = jnp.exp(local_scores - log_total).astype(jnp.bfloat16)
    remote_low = jnp.exp(remote_scores - log_total).astype(jnp.bfloat16)
    attended = jnp.einsum("rhqk,rkhd->rqhd", local_low, values, preferred_element_type=jnp.float32)
    attended = attended + jnp.einsum(
        "rhqk,rkhd->rqhd", remote_low, remote_values, preferred_element_type=jnp.float32
    )
    attended_low = attended.reshape(flat_shape).astype(jnp.bfloat16)
    branch_attention = (
        jnp.einsum("rtd,de->rte", attended_low, out_weight, preferred_element_type=jnp.float32)
        + out_bias
    )
    mixed_sum = routed_float + branch_attention
    second_norm = layer_norm(mixed_sum, norm_two[0], norm_two[1]).astype(jnp.bfloat16)
    hidden_pre = (
        jnp.einsum("rtd,df->rtf", second_norm, up_weight, preferred_element_type=jnp.float32)
        + up_bias
    )
    hidden_act, gelu_back = jax.vjp(gelu_tanh, hidden_pre)
    hidden_low = hidden_act.astype(jnp.bfloat16)
    branch_feed = (
        jnp.einsum("rtf,fd->rtd", hidden_low, down_weight, preferred_element_type=jnp.float32)
        + down_bias
    )
    branch_total = branch_attention + branch_feed
    routed_out = routed_float + gate_value[..., None] * branch_total
    row_ids = jnp.arange(row_count, dtype=jnp.int32)[:, None]
    out_tokens = tokens.at[row_ids, chosen].set(routed_out.astype(jnp.bfloat16))
    grad_routed = pick_rows(cotangent, chosen).astype(jnp.float32)
    logit_grad = jnp.sum(grad_routed * branch_total, axis=-1) * gate_value * (1.0 - gate_value)
    grad_router = jnp.einsum("rtd,rt->d", routed_float, logit_grad, precision=lax.Precision.HIGHEST)
    grad_delta = gate_value[..., None] * grad_routed
    grad_feed_low = grad_delta.astype(jnp.bfloat16)
    grad_down = jnp.einsum(
        "rtf,rtd->fd", hidden_low, grad_feed_low, preferred_element_type=jnp.float32
    )
    grad_down_vec = jnp.sum(grad_feed_low.astype(jnp.float32), axis=(0, 1))
    grad_hidden = jnp.einsum(
        "rtd,fd->rtf", grad_feed_low, down_weight, preferred_element_type=jnp.float32
    )
    grad_pre_low = gelu_back(grad_hidden)[0].astype(jnp.bfloat16)
    grad_up = jnp.einsum(
        "rtd,rtf->df", second_norm, grad_pre_low, preferred_element_type=jnp.float32
    )
    grad_up_vec = jnp.sum(grad_pre_low.astype(jnp.float32), axis=(0, 1))
    grad_second = jnp.einsum(
        "rtf,df->rtd", grad_pre_low, up_weight, preferred_element_type=jnp.float32
    )
    _, second_back = jax.vjp(layer_norm, mixed_sum, norm_two[0], norm_two[1])
    grad_mixed, grad_second_gain, grad_second_shift = second_back(grad_second)
    feed_parts = (
        grad_up.reshape(-1),
        grad_down.reshape(-1),
        padded_vector([grad_up_vec, grad_down_vec, grad_second_gain, grad_second_shift]),
    )
    grad_attention_low = (grad_delta + grad_mixed).astype(jnp.bfloat16)
    grad_out = jnp.einsum(
        "rtd,rte->de", attended_low, grad_attention_low, preferred_element_type=jnp.float32
    )
    grad_out_vec = jnp.sum(grad_attention_low.astype(jnp.float32), axis=(0, 1))
    grad_attended = jnp.einsum(
        "rte,de->rtd", grad_attention_low, out_weight, preferred_element_type=jnp.float32
    )
    grad_attended = grad_attended.astype(jnp.bfloat16).reshape(head_shape)
    again = from_behind(jnp.stack([key_rows, values]), "seq", 1)
    back_keys = again[0]
    back_values = again[1]

    def block_grads(block_keys, block_values, key_segment):
        scores = masked_scores(queries, block_keys, query_segment, key_segment)
        block_weights = jnp.exp(scores - log_total)
        block_grad = jnp.einsum(
            "rqhd,rkhd->rhqk", grad_attended, block_values, preferred_element_type=jnp.float32
        )
        return (block_weights, block_grad)

    local_weights, local_grad = block_grads(key_rows, values, query_segment)
    remote_weights, remote_grad = block_grads(back_keys, back_values, remote_segment)
    row_dot = jnp.sum(local_weights * local_grad, axis=-1, keepdims=True) + jnp.sum(
        remote_weights * remote_grad, axis=-1, keepdims=True
    )
    local_dscore = (local_weights * (local_grad - row_dot)).astype(jnp.bfloat16)
    remote_dscore = (remote_weights * (remote_grad - row_dot)).astype(jnp.bfloat16)
    local_wlow = local_weights.astype(jnp.bfloat16)
    remote_wlow = remote_weights.astype(jnp.bfloat16)
    score_scale = HD ** (-0.5)
    grad_queries = score_scale * (
        jnp.einsum("rhqk,rkhd->rqhd", local_dscore, key_rows, preferred_element_type=jnp.float32)
        + jnp.einsum(
            "rhqk,rkhd->rqhd", remote_dscore, back_keys, preferred_element_type=jnp.float32
        )
    )
    remote_key_grad = score_scale * jnp.einsum(
        "rhqk,rqhd->rkhd", remote_dscore, queries, preferred_element_type=jnp.float32
    )
    remote_value_grad = jnp.einsum(
        "rhqk,rqhd->rkhd", remote_wlow, grad_attended, preferred_element_type=jnp.float32
    )
    returned = from_behind(jnp.stack([remote_key_grad, remote_value_grad]), "seq", -1)
    local_key_grad = score_scale * jnp.einsum(
        "rhqk,rqhd->rkhd", local_dscore, queries, preferred_element_type=jnp.float32
    )
    local_value_grad = jnp.einsum(
        "rhqk,rqhd->rkhd", local_wlow, grad_attended, preferred_element_type=jnp.float32
    )
    grad_query_low = grad_queries.reshape(flat_shape).astype(jnp.bfloat16)
    grad_key_low = (local_key_grad + returned[0]).reshape(flat_shape).astype(jnp.bfloat16)
    grad_value_low = (local_value_grad + returned[1]).reshape(flat_shape).astype(jnp.bfloat16)
    grad_projected = jnp.concatenate([grad_query_low, grad_key_low, grad_value_low], axis=-1)
    grad_qkv = jnp.einsum(
        "rtd,rte->de", first_norm, grad_projected, preferred_element_type=jnp.float32
    )
    grad_query_vec = jnp.sum(grad_query_low.astype(jnp.float32), axis=(0, 1))
    grad_value_vec = jnp.sum(grad_value_low.astype(jnp.float32), axis=(0, 1))
    grad_first = jnp.einsum(
        "rte,de->rtd", grad_projected, qkv_weight, preferred_element_type=jnp.float32
    )
    _, first_back = jax.vjp(layer_norm, routed_float, norm_one[0], norm_one[1])
    grad_from_norm, grad_first_gain, grad_first_shift = first_back(grad_first)
    grad_routed_in = (
        grad_routed
        + grad_mixed
        + grad_from_norm
        + logit_grad[..., None] * router_weight.astype(jnp.float32)
    )
    grad_tokens = cotangent.at[row_ids, chosen].set(grad_routed_in.astype(jnp.bfloat16))
    attention_parts = (
        grad_qkv.reshape(-1),
        grad_out.reshape(-1),
        padded_vector(
            [
                grad_query_vec,
                grad_value_vec,
                grad_out_vec,
                grad_first_gain,
                grad_first_shift,
                grad_router,
            ]
        ),
    )
    all_shares = (
        lax.psum_scatter(feed_parts[0], ("rows", "seq"), scatter_dimension=0, tiled=True),
        lax.psum_scatter(feed_parts[1], ("rows", "seq"), scatter_dimension=0, tiled=True),
        lax.psum_scatter(feed_parts[2], ("rows", "seq"), scatter_dimension=0, tiled=True),
        lax.psum_scatter(attention_parts[0], ("rows", "seq"), scatter_dimension=0, tiled=True),
        lax.psum_scatter(attention_parts[1], ("rows", "seq"), scatter_dimension=0, tiled=True),
        lax.psum_scatter(attention_parts[2], ("rows", "seq"), scatter_dimension=0, tiled=True),
    )
    feed_shares = all_shares[0:3]
    attention_shares = all_shares[3:6]
    summed = (
        lax.all_gather(feed_shares[0], ("rows", "seq"), axis=0, tiled=True),
        lax.all_gather(feed_shares[1], ("rows", "seq"), axis=0, tiled=True),
        lax.all_gather(feed_shares[2], ("rows", "seq"), axis=0, tiled=True),
        lax.all_gather(attention_shares[0], ("rows", "seq"), axis=0, tiled=True),
        lax.all_gather(attention_shares[1], ("rows", "seq"), axis=0, tiled=True),
        lax.all_gather(attention_shares[2], ("rows", "seq"), axis=0, tiled=True),
    )
    feed_small = summed[2]
    attention_small = summed[5]
    return (
        out_tokens,
        grad_tokens,
        summed[3].reshape(model_width, 3 * model_width),
        attention_small[0:model_width],
        attention_small[model_width : 2 * model_width],
        summed[4].reshape(model_width, model_width),
        attention_small[2 * model_width : 3 * model_width],
        attention_small[3 * model_width : 4 * model_width],
        attention_small[4 * model_width : 5 * model_width],
        feed_small[hidden_width + model_width : hidden_width + 2 * model_width],
        feed_small[hidden_width + 2 * model_width : hidden_width + 3 * model_width],
        summed[0].reshape(model_width, hidden_width),
        feed_small[0:hidden_width],
        summed[1].reshape(hidden_width, model_width),
        feed_small[hidden_width : hidden_width + model_width],
        attention_small[5 * model_width : 6 * model_width],
    )


def solution(mesh):
    return jax.shard_map(
        body,
        mesh=mesh,
        in_specs=(
            P("rows", "seq", None),
            P("rows", "seq", None),
            P("rows", None),
            P("rows", None),
            P(),
            P(),
            P(),
            P(),
            P(),
            P(),
            P(),
            P(),
            P(),
            P(),
            P(),
            P(),
            P(),
            P(),
        ),
        out_specs=(
            P("rows", "seq", None),
            P("rows", "seq", None),
            P(),
            P(),
            P(),
            P(),
            P(),
            P(),
            P(),
            P(),
            P(),
            P(),
            P(),
            P(),
            P(),
            P(),
        ),
        check_vma=False,
    )
```

profile of v0, /device:TPU:0, one launch (start us, length us, event | category | flops | bytes accessed | tf_op | source)
XLA Modules:
  0.0 1023.8 jit_solution(13722739931993220925)
XLA Ops:
  11.9 4.6 gather_fusion
  39.5 4.6 gather_fusion.3
  66.6 7.5 collective-permute-done
  77.4 5.5 exponential_reduce_fusion
  83.0 3.8 fusion.70
  86.9 4.6 add_convert_fusion
  96.6 7.7 convert_reduce_fusion
  115.1 8.5 convolution_bitcast_fusion.2
  123.7 5.9 fusion.98
  129.6 19.3 %multiply_reduce_fusion = (f32[12,472]{1,0:T(8,128)S(1)}, f32[12,472]{1,0:T(8,128)S(1)}, f32[12,472,472]{1,2,0:T(8,128)}) fusion(f32[12,472,472]{1,2,0:T(8,128)} %copy-done.2, f32[12,472]{1,0:T(8,128)S(1)} %copy-done.37, pred[472,472]{0,1:T(8,128)(4,1)S(1)} %copy-done.23, f32[12,472,472]{1,2,0:T(8,128)} %fusion.98, f32[12,472,472]{1,2,0:T(8,128)} %copy-done.1, ...), kind=kOutput, calls=%fused_computation.8 | convolution fusion | flops 368918976 | bytes 47518208 | tf_op jit(solution)/shard_map/rqhd,rkhd->rhqk/dot_general | solution.py:179
  148.9 19.7 %multiply_convert_fusion.1 = (bf16[12,472,472]{1,2,0:T(8,128)(2,1)}, bf16[12,472,472]{1,2,0:T(8,128)(2,1)S(1)}) fusion(f32[12,472,472]{1,2,0:T(8,128)} %fusion.98, f32[12,472,472]{1,2,0:T(8,128)} %copy-done.1, f32[12,472]{1,0:T(8,128)S(1)} %add.231, f32[12,472]{1,0:T(8,128)S(1)} %copy-done.37, pred[472,472]{0,1:T(8,128)(4,1)S(1)} %copy-done.20, ...), kind=kLoop, calls=%fused_computation.7 | loop fusion | flops 32080896 | bytes 53959040 | tf_op jit(solution)/shard_map/convert_element_type | solution.py:189
  180.3 5.2 convolution_bitcast_fusion.1
  185.6 5.9 copy.92
  191.5 10.0 fusion.51
  201.5 10.7 %reshape.731 = f32[2359296]{0:T(1024)} reshape(f32[3072,768]{1,0:T(8,128)} %fusion.51) | data formatting | bytes 18874368 | tf_op jit(solution)/shard_map/reshape | solution.py:160
  212.2 4.1 fusion.99
  216.4 4.4 convert_reduce_fusion.3
  220.9 21.9 %collective-permute-done.1 = f32[2,1,472,12,64]{2,4,3,1,0:T(8,128)} collective-permute-done((f32[2,1,472,12,64]{2,4,3,1,0:T(8,128)}, f32[2,1,472,12,64]{2,4,3,1,0:T(8,128)}, u32[]{:S(2)}, u32[]{:S(2)}) %collective-permute-start.1) | collective-permute-done | bytes 2900000 | tf_op jit(solution)/shard_map/ppermute | solution.py:13
  242.8 6.2 convert_reduce_fusion.2
  253.4 5.5 fusion.38
  258.9 7.9 reshape.725
  266.8 433.4 %all-reduce.14.cloned.1.call-done = (f32[1769472]{0:T(1024)}, f32[589824]{0:T(1024)}, f32[2359296]{0:T(1024)}, f32[2359296]{0:T(1024)}) async-done(((f32[1769472]{0:T(1024)}, f32[589824]{0:T(1024)}, f32[2359296]{0:T(1024)}, f32[2359296]{0:T(1024)}), (f32[1769472]{0:T(1024)}, f32[589824]{0:T(1024)}, f32[2359296]{0:T(1024)}, f32[2359296]{0:T(1024)})) %all-reduce.14.cloned.1.call-update) | async-done | bytes 28311568
  722.3 9.6 convert_reduce_fusion.4
  738.6 41.8 %all-reduce.10 = (f32[4608]{0:T(1024)}, f32[5376]{0:T(1024)}) all-reduce(f32[4608]{0:T(1024)} %constant_dynamic-update-slice_fusion, f32[5376]{0:T(1024)} %pad_maximum_fusion.2), channel_id=3, replica_groups=mesh['rows'=16,'seq'=2] {'rows','seq'}, use_global_device_ids=true, to_apply=%region_23.26.clone | all-reduce | flops 9984 | bytes 79872
  784.5 41.8 %all-reduce.9 = (f32[4608]{0:T(1024)}, f32[5376]{0:T(1024)}) all-reduce(f32[4608]{0:T(1024)} %dynamic-slice_dynamic-update-slice_fusion.1, f32[5376]{0:T(1024)} %dynamic-slice_dynamic-update-slice_fusion), channel_id=1, replica_groups=mesh['rows'=16,'seq'=2] {'rows','seq'}, use_global_device_ids=true, to_apply=%add.1 | all-reduce | flops 9984 | bytes 79872
  827.6 6.1 scatter_custom_fusion
  835.0 7.5 scatter_custom_fusion.1
  848.7 8.3 reshape.726
  857.0 65.0 %all-gather.9.cloned.1.call-done = f32[2359296]{0:T(1024)} async-done(((f32[73728]{0:T(1024)}), f32[2359296]{0:T(1024)}) %all-gather.9.cloned.1.call-update) | async-done | bytes 9437200 | tf_op jit(solution)/shard_map/all_gather | solution.py:259
  922.0 10.9 %reshape.730 = f32[768,3072]{1,0:T(8,128)} reshape(f32[2359296]{0:T(1024)} %all-gather.9.cloned.1.call-done) | data formatting | bytes 18874368 | tf_op jit(solution)/shard_map/reshape | solution.py:280
  932.9 72.9 %all-gather.11.cloned.1.call-done = f32[2359296]{0:T(1024)} async-done(((f32[73728]{0:T(1024)}), f32[2359296]{0:T(1024)}) %all-gather.11.cloned.1.call-update) | async-done | bytes 9437200 | tf_op jit(solution)/shard_map/all_gather | solution.py:260
  1005.8 11.3 %reshape.732 = f32[3072,768]{1,0:T(8,128)} reshape(f32[2359296]{0:T(1024)} %all-gather.11.cloned.1.call-done) | data formatting | bytes 18874368 | tf_op jit(solution)/shard_map/reshape | solution.py:282
  (280 shorter events, 126.3 us)
Async XLA Ops:
  7.2 16.5 %copy-start = (bf16[768,2304]{1,0:T(8,128)(2,1)S(1)}, bf16[768,2304]{1,0:T(8,128)(2,1)}, u32[]{:S(2)}) copy-start(bf16[768,2304]{1,0:T(8,128)(2,1)} %param.26) | copy-start | bytes 10616836
  7.2 693.1 %all-reduce.14.cloned.1.call-start = ((), (), s32[]{:S(2)}) async-start(), calls=%async_computation.4 | async-start | bytes 56623104
  11.9 11.8 %copy-start.42 = (pred[472]{0:T(512)(128)(4,1)}, pred[472]{0:T(512)(128)(4,1)S(1)}, u32[]{:S(2)}) copy-start(pred[472]{0:T(512)(128)(4,1)S(1)} %get-tuple-element.43) | copy-start | bytes 1420
  29.2 10.2 %copy-start.57 = (s32[1024]{0:T(1024)S(1)}, s32[1024]{0:T(1024)}, u32[]{:S(2)}) copy-start(s32[1024]{0:T(1024)} %copy-done.56) | copy-start | bytes 12292
  36.5 37.7 %collective-permute-start = (bf16[2,1,472,12,64]{2,4,3,1,0:T(8,128)(2,1)}, bf16[2,1,472,12,64]{2,4,3,1,0:T(8,128)(2,1)}, u32[]{:S(2)}, u32[]{:S(2)}) collective-permute-start(bf16[2,1,472,12,64]{2,4,3,1,0:T(8,128)(2,1)} %pad_maximum_fusion.1), channel_id=1, source_target_pairs={{1,0},{0,1},{3,2},{2,3},{5,4},{4,5},{7,6},{6,7},{9,8},{8,9},{11,10... | collective-permute-start | bytes 4349960 | tf_op jit(solution)/shard_map/ppermute | solution.py:13
  62.9 20.0 %copy-start.19 = (pred[472,472]{0,1:T(8,128)(4,1)}, pred[472,472]{0,1:T(8,128)(4,1)S(1)}, u32[]{:S(2)}) copy-start(pred[472,472]{0,1:T(8,128)(4,1)S(1)} %get-tuple-element.63) | copy-start | bytes 668356
  62.9 23.9 %copy-start.22 = (pred[472,472]{0,1:T(8,128)(4,1)}, pred[472,472]{0,1:T(8,128)(4,1)S(1)}, u32[]{:S(2)}) copy-start(pred[472,472]{0,1:T(8,128)(4,1)S(1)} %get-tuple-element.62) | copy-start | bytes 668356
  62.9 11.2 %copy-start.7 = (bf16[1,472,768]{1,2,0:T(8,128)(2,1)S(1)}, bf16[1,472,768]{1,2,0:T(8,128)(2,1)}, u32[]{:S(2)}) copy-start(bf16[1,472,768]{1,2,0:T(8,128)(2,1)} %copy.71) | copy-start | bytes 2174980
  66.6 16.3 %copy-start.1 = (f32[12,472,472]{1,2,0:T(8,128)}, f32[12,472,472]{1,2,0:T(8,128)S(1)}, u32[]{:S(2)}) copy-start(f32[12,472,472]{1,2,0:T(8,128)S(1)} %get-tuple-element.65) | copy-start | bytes 32080900
  77.4 9.4 copy-start.2
  83.0 10.9 %slice-start.5 = ((s8[4718592]{0:T(1024)(128)(4,1)}), s8[4194304]{0:T(1024)(128)(4,1)S(1)}, s32[]{:S(2)}) async-start(s8[4718592]{0:T(1024)(128)(4,1)} %bitcast.297), calls=%async_computation.10 | async-start | bytes 8388608
  93.5 14.0 %copy-start.11 = (f32[1,472,768]{2,1,0:T(8,128)}, f32[1,472,768]{2,1,0:T(8,128)S(1)}, u32[]{:S(2)}) copy-start(f32[1,472,768]{2,1,0:T(8,128)S(1)} %get-tuple-element.42) | copy-start | bytes 4349956
  93.9 13.7 %copy-start.63 = (f32[472]{0:T(512)}, f32[472]{0:T(512)S(1)}, u32[]{:S(2)}) copy-start(f32[472]{0:T(512)S(1)} %fusion.73) | copy-start | bytes 5668
  148.9 19.7 %copy-start.8 = (bf16[1,472,768]{1,2,0:T(8,128)(2,1)S(1)}, bf16[1,472,768]{1,2,0:T(8,128)(2,1)}, u32[]{:S(2)}) copy-start(bf16[1,472,768]{1,2,0:T(8,128)(2,1)} %copy.71) | copy-start | bytes 2174980
  173.2 69.6 %collective-permute-start.1 = (f32[2,1,472,12,64]{2,4,3,1,0:T(8,128)}, f32[2,1,472,12,64]{2,4,3,1,0:T(8,128)}, u32[]{:S(2)}, u32[]{:S(2)}) collective-permute-start(f32[2,1,472,12,64]{2,4,3,1,0:T(8,128)} %pad_maximum_fusion), channel_id=1, source_target_pairs={{1,0},{0,1},{3,2},{2,3},{5,4},{4,5},{7,6},{6,7},{9,8},{8,9},{11,10... | collective-permute-start | bytes 8699912 | tf_op jit(solution)/shard_map/ppermute | solution.py:13
  212.2 30.6 %slice-start = ((s8[11599872]{0:T(1024)(128)(4,1)}), s8[4194304]{0:T(1024)(128)(4,1)S(1)}, s32[]{:S(2)}) async-start(s8[11599872]{0:T(1024)(128)(4,1)} %bitcast.253), calls=%async_computation.5 | async-start | bytes 8388608
  212.2 30.6 %slice-start.1 = ((s8[11599872]{0:T(1024)(128)(4,1)}), s8[4194304]{0:T(1024)(128)(4,1)S(1)}, s32[]{:S(2)}) async-start(s8[11599872]{0:T(1024)(128)(4,1)} %bitcast.253), calls=%async_computation.6 | async-start | bytes 8388608
  216.4 26.4 %slice-start.2 = ((s8[11599872]{0:T(1024)(128)(4,1)}), s8[3211264]{0:T(1024)(128)(4,1)S(1)}, s32[]{:S(2)}) async-start(s8[11599872]{0:T(1024)(128)(4,1)} %bitcast.253), calls=%async_computation.7 | async-start | bytes 6422528
  216.4 26.4 %copy-start.15 = (bf16[472,768]{0,1:T(8,128)(2,1)S(1)}, bf16[472,768]{0,1:T(8,128)(2,1)}, u32[]{:S(2)}) copy-start(bf16[472,768]{0,1:T(8,128)(2,1)} %copy.77) | copy-start | bytes 2174980
  216.4 26.4 %copy-start.21 = (pred[472,472]{0,1:T(8,128)(4,1)S(1)}, pred[472,472]{0,1:T(8,128)(4,1)}, u32[]{:S(2)}) copy-start(pred[472,472]{0,1:T(8,128)(4,1)} %copy-done.19) | copy-start | bytes 668356
  216.4 26.4 %copy-start.38 = (f32[12,472]{1,0:T(8,128)S(1)}, f32[12,472]{1,0:T(8,128)}, u32[]{:S(2)}) copy-start(f32[12,472]{1,0:T(8,128)} %copy-done.36) | copy-start | bytes 67972
  216.4 32.6 %slice-start.3 = ((s8[5799936]{0:T(1024)(128)(4,1)}), s8[4194304]{0:T(1024)(128)(4,1)S(1)}, s32[]{:S(2)}) async-start(s8[5799936]{0:T(1024)(128)(4,1)} %bitcast.255), calls=%async_computation.8 | async-start | bytes 8388608
  220.8 31.6 %copy-start.34 = (bf16[12,64,472]{2,1,0:T(8,128)(2,1)}, bf16[12,64,472]{2,1,0:T(8,128)(2,1)S(1)}, u32[]{:S(2)}) copy-start(bf16[12,64,472]{2,1,0:T(8,128)(2,1)S(1)} %get-tuple-element.73) | copy-start | bytes 2174980
  220.9 28.2 %slice-start.4 = ((s8[5799936]{0:T(1024)(128)(4,1)}), s8[1605632]{0:T(1024)(128)(4,1)S(1)}, s32[]{:S(2)}) async-start(s8[5799936]{0:T(1024)(128)(4,1)} %bitcast.255), calls=%async_computation.9 | async-start | bytes 3211264
  220.9 28.2 %copy-start.9 = (bf16[1,472,768]{1,2,0:T(8,128)(2,1)S(1)}, bf16[1,472,768]{1,2,0:T(8,128)(2,1)}, u32[]{:S(2)}) copy-start(bf16[1,472,768]{1,2,0:T(8,128)(2,1)} %copy.71) | copy-start | bytes 2174980
  266.8 578.5 %all-gather.7.cloned.1.call-start = ((), (), s32[]{:S(2)}) async-start(), calls=%async_computation.1 | async-start | bytes 2433024 | tf_op jit(solution)/shard_map/all_gather | solution.py:263
  701.8 146.9 %all-gather.5.cloned.1.call-start = ((), (), s32[]{:S(2)}) async-start(), calls=%async_computation | async-start | bytes 7299072 | tf_op jit(solution)/shard_map/all_gather | solution.py:262
  703.5 218.4 %all-gather.9.cloned.1.call-start = ((), (), s32[]{:S(2)}) async-start(), calls=%async_computation.2 | async-start | bytes 9732096 | tf_op jit(solution)/shard_map/all_gather | solution.py:259
  705.3 300.5 %all-gather.11.cloned.1.call-start = ((), (), s32[]{:S(2)}) async-start(), calls=%async_computation.3 | async-start | bytes 9732096 | tf_op jit(solution)/shard_map/all_gather | solution.py:260
  722.2 9.8 copy-start.25
  722.3 9.7 copy-start.51
  722.3 13.8 %copy-start.67 = (f32[1,472]{1,0:T(1,128)S(1)}, f32[1,472]{1,0:T(1,128)}, u32[]{:S(2)}) copy-start(f32[1,472]{1,0:T(1,128)} %copy-done.66) | copy-start | bytes 5668
  (62 other events, 263.5 us)
Sparse Core Ops, SparseCore 0:
  266.9 433.3 all-reduce.13
  703.6 57.4 all-gather.6
  765.1 72.6 all-gather.4
  841.5 80.3 all-gather.8
  925.1 80.6 all-gather.10
where the time goes:
time: 1040 us; the launch traced here: 1020 us
  waiting for transfers between devices  601 us (58%)
  matrix products  128 us (12%)
  local copies, waits for them, and re-layouts  122 us (12%)
  blocking collectives  83.6 us (8%)
  other arithmetic  69.9 us (7%)
  between operations  15.1 us (1%)
    unnamed x6, waiting for transfers between devices  434 us
    unnamed x2, blocking collectives  83.6 us
    all_gather x1, waiting for transfers between devices, body(): lax.all_gather(feed_shares[1], ('rows', 'seq'), axis=0, tiled=True)  72.9 us
    all_gather x1, waiting for transfers between devices, body(): lax.all_gather(feed_shares[0], ('rows', 'seq'), axis=0, tiled=True)  65 us
    unnamed x191, local copies, waits for them, and re-layouts  31.5 us
    ppermute x2, waiting for transfers between devices, from_behind(): return lax.ppermute(block, axis, route)  29.4 us
    dot_general x2, matrix products, block_grads(): jnp.einsum('rqhd,rkhd->rhqk', grad_attended, block_values, preferred_elem...  25.2 us
  transfers between devices with their start and end apart: 7, of which 5 were waited for; matrix products, arithmetic and copies ran while one was open for 15% of the time, Pallas kernels for 0%

commit v1 on v0

v1 whole, which is shorter than its diff:
```python
import functools

import jax
import jax.numpy as jnp
from jax import lax
from jax.experimental import pallas as pl
from jax.experimental.pallas import tpu as pltpu
from jax.sharding import PartitionSpec as P

H = 12
HD = 64
PAIR = 2 * HD
TILE = 128
NEG = -1e30
SCALE = HD ** (-0.5)
UNIT = 100000
WEIGHT = {
    "pick_rows": 6 * UNIT,
    "near_attention": 16 * UNIT,
    "far_attention": 16 * UNIT,
    "feed_blocks": 13 * UNIT,
    "feed_grads": 7 * UNIT,
    "middle": 8 * UNIT,
    "own_back": 9 * UNIT,
    "other_back": 9 * UNIT,
    "last_grads": 8 * UNIT,
    "token_out": 7 * UNIT,
    "token_grad": 9 * UNIT,
}
F32 = jnp.float32
BF16 = jnp.bfloat16
I32 = jnp.int32
VMEM = pltpu.VMEM
SMEM = pltpu.SMEM


def nn(a, b):
    return lax.dot_general(a, b, (((1,), (0,)), ((), ())), preferred_element_type=F32)


def nt(a, b):
    return lax.dot_general(a, b, (((1,), (1,)), ((), ())), preferred_element_type=F32)


def tn(a, b):
    return lax.dot_general(a, b, (((0,), (0,)), ((), ())), preferred_element_type=F32)


def shape_of(shape, kind):
    return jax.ShapeDtypeStruct(shape, kind)


class Fetch:
    def __init__(self, source, target, sem):
        self.copy = pltpu.make_async_copy(source, target, sem)
        self.target, self.ready = target, False
        self.copy.start()

    def __call__(self):
        if not self.ready:
            self.copy.wait()
            self.ready = True
        return self.target


class Send:
    def __init__(self, buffer, target, sem):
        self.ref, self.target, self.sem = buffer, target, sem
        self.copy = pltpu.make_async_copy(buffer, target, sem)
        self.begun = False

    def go(self):
        self.copy.start()
        self.begun = True


def streamed(name, kernel, scalars, small, large, outs, scratch=(), scalar_outs=(), room=62):
    parts = []
    arrays = []
    for array, part, extent in large:
        at = next((i for i, a in enumerate(arrays) if a is array), None)
        if at is None:
            at = len(arrays)
            arrays.append(array)
        parts.append((at, part, extent))

    def wrapped(*refs):
        refs = list(refs)

        def take(count):
            head = refs[:count]
            del refs[:count]
            return head

        scalar_refs = take(len(scalars))
        small_refs = take(len(small))
        array_refs = take(len(arrays))
        out_refs = take(len(outs))
        scalar_out_refs = take(len(scalar_outs))
        landing = take(len(parts))
        staging = take(len(outs))
        in_sems, out_sems = take(2)
        fetches = []
        for i, (at, part, _) in enumerate(parts):
            source = array_refs[at] if part is None else part(array_refs[at], scalar_refs)
            fetches.append(Fetch(source, landing[i], in_sems.at[i]))
        sends = [Send(staging[i], out_refs[i], out_sems.at[i]) for i in range(len(outs))]
        kernel(scalar_refs, small_refs, fetches, sends, refs, scalar_out_refs)
        for fetch in fetches:
            fetch()
        for send in sends:
            if not send.begun:
                send.go()
        for send in sends:
            send.copy.wait()

    hbm = pl.BlockSpec(memory_space=pltpu.HBM)
    result = pl.pallas_call(
        wrapped,
        out_shape=tuple(outs) + tuple(scalar_outs),
        in_specs=[pl.BlockSpec(memory_space=SMEM)] * len(scalars)
        + [pl.BlockSpec(memory_space=VMEM)] * len(small)
        + [hbm] * len(arrays),
        out_specs=tuple([hbm] * len(outs) + [pl.BlockSpec(memory_space=SMEM)] * len(scalar_outs)),
        scratch_shapes=[VMEM(extent, arrays[at].dtype) for at, _, extent in parts]
        + [VMEM(o.shape, o.dtype) for o in outs]
        + [pltpu.SemaphoreType.DMA((len(parts),)), pltpu.SemaphoreType.DMA((len(outs),))]
        + list(scratch),
        compiler_params=pltpu.CompilerParams(vmem_limit_bytes=room << 20),
        cost_estimate=pl.CostEstimate(flops=0, bytes_accessed=WEIGHT[name], transcendentals=0),
        name=name,
    )(*scalars, *small, *arrays)
    return result


def full(array):
    return (array, None, array.shape)


def row_of(array, index):
    return (array, lambda ref, scalars: ref.at[index], array.shape[1:])


def head_rows(array, count):
    return (array, lambda ref, scalars: ref.at[0:count], (count,) + array.shape[1:])


def columns(array, start, count):
    return (array, lambda ref, scalars: ref.at[:, start : start + count], (array.shape[0], count))


def wide(ref):
    return ref[...].astype(F32)


def normalize(values):
    center = values - jnp.mean(values, axis=-1, keepdims=True)
    inverse = lax.rsqrt(jnp.mean(center * center, axis=-1, keepdims=True) + 1e-06)
    return center * inverse, inverse


def norm_back(grad, scale, unit, inverse):
    scaled = grad * scale
    first = jnp.mean(scaled, axis=-1, keepdims=True)
    second = jnp.mean(scaled * unit, axis=-1, keepdims=True)
    return inverse * (scaled - first - unit * second)


def tile_spans(line, count, out_ref):
    width = line.shape[1]
    lane = lax.broadcasted_iota(I32, (1, width), 1)
    tiles = width // TILE
    for i in range(tiles):
        inside = (lane >= i * TILE) & (lane < min((i + 1) * TILE, count))
        out_ref[i] = jnp.min(jnp.where(inside, line, 1e9)).astype(I32)
        out_ref[tiles + i] = jnp.max(jnp.where(inside, line, -1e9)).astype(I32)


def pick_rows(pos, routes, segs, tokens, cotangent, count, width):
    slots, depth = tokens.shape

    def kernel(scalars, small, fetches, sends, scratch, scalar_outs):
        route, seg, tok, cot = fetches
        routed, grad, hot_out = sends
        lane = lax.broadcasted_iota(I32, (slots, width), 1)
        slot = lax.broadcasted_iota(I32, (slots, width), 0)
        chosen = (slot == route()[:, :width]) & (lane < count)
        taken = jnp.max(jnp.where(chosen, 1.0, 0.0), axis=-1, keepdims=True)
        before = lax.broadcasted_iota(I32, (slots, slots), 0) < lax.broadcasted_iota(I32, (slots, slots), 1)
        before = jnp.where(before, 1.0, 0.0).astype(BF16)
        rank = tn(before, jnp.broadcast_to(taken, (slots, TILE)).astype(BF16))[:, 0:1]
        rank = jnp.where(taken > 0.0, rank, -1.0)
        hot = jnp.where(lane.astype(F32) == rank, 1.0, 0.0).astype(BF16)
        hot_out.ref[...] = hot
        hot_out.go()
        groups = jnp.broadcast_to(seg()[...].astype(F32), (8, slots)).astype(BF16)
        line = nn(groups, hot)
        line = jnp.where(lax.broadcasted_iota(I32, (8, width), 1) < count, line, -1.0)
        routed.ref[0:width] = tn(hot, tok()[...]).astype(BF16)
        routed.ref[width:] = jnp.zeros_like(routed.ref[width:])
        routed.ref[width : width + 8, 0:width] = line.astype(BF16)
        routed.go()
        grad.ref[...] = tn(hot, cot()[...]).astype(BF16)
        tile_spans(line[0:1], count, scalar_outs[0])

    return streamed(
        "pick_rows", kernel, [pos], [],
        [
            (routes, lambda ref, scalars: ref.at[scalars[0][0]], routes.shape[1:]),
            (segs, lambda ref, scalars: ref.at[scalars[0][0]], segs.shape[1:]),
            full(tokens), full(cotangent),
        ],
        [shape_of((width + 16, depth), BF16), shape_of((width, depth), BF16), shape_of((slots, width), BF16)],
        scalar_outs=[shape_of((2 * (width // TILE),), I32)],
    )


def key_span(keys, queries, j, tiles):
    low, high = queries[j], queries[tiles + j]
    first, last = jnp.int32(tiles), jnp.int32(-1)
    for t in range(tiles):
        meets = (keys[tiles + t] >= low) & (keys[t] <= high)
        first = jnp.where(meets & (first == tiles), t, first)
        last = jnp.where(meets, t, last)
    return jnp.minimum(first, tiles - 1), jnp.maximum(last - first + 1, 0)


def store_spans(ref, keys, queries, tiles):
    for j in range(tiles):
        first, many = key_span(keys, queries, j, tiles)
        ref[j] = first
        ref[tiles + j] = many


def fill_bias(bias_ref, key_line, query_line, key_pad):
    keys = jnp.where(key_line < 0.0, key_pad, key_line).T[:, 0:1]
    bias_ref[...] = jnp.where(keys == query_line[0:1], 0.0, NEG)


def stacked_heads(block):
    lane = lax.broadcasted_iota(I32, (1, PAIR), 1)
    zero = jnp.zeros_like(block)
    return jnp.concatenate([jnp.where(lane < HD, block, zero), jnp.where(lane >= HD, block, zero)], axis=0)


def own_blocks(block):
    return jnp.concatenate([block[0:HD, 0:TILE], block[HD:PAIR, TILE : 2 * TILE]], axis=0)


def twice(block):
    return jnp.concatenate([block, block], axis=1)


def over_tiles(span, tiles, pairs, lowest, work, group=3):
    def tile_step(j, carry):
        for n in range(lowest, tiles + 1):

            def branch(n=n):
                def group_step(i, inner):
                    for p in range(group):
                        work(n, j, i * group + p)
                    return inner

                lax.fori_loop(0, pairs // group, group_step, 0)

            pl.when(span[tiles + j] == n)(branch)
        return carry

    lax.fori_loop(0, tiles, tile_step, 0)


def project(normed, weights, qb, vb, q_ref, k_ref, v_ref, turned_ref, sends=None):
    depth = normed.shape[1]
    step = 256
    for part, (ref, weight) in enumerate(zip((k_ref, q_ref, v_ref), (weights[1], weights[0], weights[2]))):
        weight_ref = weight()
        for at in range(0, depth, step):
            value = nn(normed, weight_ref[:, at : at + step])
            if part == 1:
                value = value + qb[:, at : at + step]
            elif part == 2:
                value = value + vb[:, at : at + step]
            value = value.astype(BF16)
            ref[:, at : at + step] = value
            if part == 2:
                turned_ref[at : at + step, :] = value.T
        if sends is not None:
            sends[part].go()


def near_attention(spans, routed, qkv_weight, query_bias, value_bias, scale, offset, router):
    depth = routed.shape[1]
    width = routed.shape[0] - 16
    tiles = width // TILE
    pairs = depth // PAIR

    def kernel(scalars, small, fetches, sends, scratch, scalar_outs):
        qb, vb, scale_ref, offset_ref, router_ref = small
        q, k, v, normed, gate, acc, stat = sends
        bias, turned, span = scratch
        x_ref = fetches[0]()
        x = x_ref[0:width].astype(F32)
        unit, _ = normalize(x)
        low = (unit * wide(scale_ref) + wide(offset_ref)).astype(BF16)
        normed.ref[...] = low
        normed.go()
        logit = jnp.sum(x * wide(router_ref), axis=-1, keepdims=True)
        gate.ref[...] = jnp.broadcast_to(1.0 / (1.0 + jnp.exp(-logit)), gate.ref.shape)
        gate.go()
        project(low, fetches[1:4], wide(qb), wide(vb), q.ref, k.ref, v.ref, turned, (k, q, v))
        line = x_ref[width : width + 8, 0:width].astype(F32)
        fill_bias(bias, line, line, -1.0)
        store_spans(span, scalars[0], scalars[0], tiles)

        def work(n, j, pair):
            at = pl.multiple_of(pair * PAIR, PAIR)
            rows = pl.ds(pl.multiple_of(j * TILE, TILE), TILE)
            some = pl.ds(pl.multiple_of(span[j] * TILE, TILE), n * TILE)
            index = pair * tiles + j
            query = stacked_heads(q.ref[rows, pl.ds(at, PAIR)]) * SCALE
            scores = nt(k.ref[some, pl.ds(at, PAIR)], query) + twice(bias[some, rows])
            top = jnp.max(scores, axis=0, keepdims=True)
            weights = jnp.exp(scores - top)
            stat.ref[0, pl.ds(index, 1)] = top
            stat.ref[1, pl.ds(index, 1)] = jnp.sum(weights, axis=0, keepdims=True)
            acc.ref[index] = own_blocks(nn(turned[pl.ds(at, PAIR), some], weights.astype(BF16)))

        over_tiles(span, tiles, pairs, 1, work)

    low = shape_of((width, depth), BF16)
    return streamed(
        "near_attention", kernel, [spans], [query_bias, value_bias, scale, offset, router],
        [full(routed)] + [columns(qkv_weight, i * depth, depth) for i in range(3)],
        [
            low, low, low, low,
            shape_of((width, TILE), F32),
            shape_of((pairs * tiles, PAIR, TILE), F32),
            shape_of((2, pairs * tiles, 2 * TILE), F32),
        ],
        scratch=[VMEM((width, width), F32), VMEM((depth, width), BF16), SMEM((2 * tiles,), I32)],
    )


def far_attention(far, spans, routed, qkv_weight, query_bias, value_bias, scale, offset, count,
                  queries, acc, stat, out_weight, out_bias, scale2, offset2, gate, grad_routed, normed):
    depth = routed.shape[1]
    width = routed.shape[0] - 16
    tiles = width // TILE
    pairs = depth // PAIR

    def kernel(scalars, small, fetches, sends, scratch, scalar_outs):
        qb, vb, scale_ref, offset_ref, ob, scale2_ref, offset2_ref = small
        far_in, x_in, weight_q, weight_k, weight_v, q_in, acc_in, stat_in, ow, gate_in, grad_in, normed_in = fetches
        fq, fk, fv, pack, lse, branch_out, turned_out, lines = sends
        bias, turned, span, attended = scratch
        far_ref = far_in()
        far_line = far_ref[width : width + 8, 0:width].astype(F32)
        tile_spans(far_line[0:1], count, scalar_outs[0])
        unit, _ = normalize(far_ref[0:width].astype(F32))
        low = (unit * wide(scale_ref) + wide(offset_ref)).astype(BF16)
        project(low, (weight_q, weight_k, weight_v), wide(qb), wide(vb), fq.ref, fk.ref, fv.ref, turned,
                (fk, fq, fv))
        x_ref = x_in()
        line = x_ref[width : width + 8, 0:width].astype(F32)
        fill_bias(bias, far_line, line, -2.0)
        lines.ref[0] = line
        lines.ref[1] = jnp.where(far_line < 0.0, -2.0, far_line)
        lines.go()
        store_spans(span, scalar_outs[0], scalars[0], tiles)
        q_ref, acc_ref, stat_ref = q_in(), acc_in(), stat_in()

        def work(n, j, pair):
            at = pl.multiple_of(pair * PAIR, PAIR)
            rows = pl.ds(pl.multiple_of(j * TILE, TILE), TILE)
            index = pair * tiles + j
            one = pl.ds(index, 1)
            near, top, total = acc_ref[index], stat_ref[0, one], stat_ref[1, one]
            if n > 0:
                query = stacked_heads(q_ref[rows, pl.ds(at, PAIR)]) * SCALE
                some = pl.ds(pl.multiple_of(span[j] * TILE, TILE), n * TILE)
                scores = nt(fk.ref[some, pl.ds(at, PAIR)], query) + twice(bias[some, rows])
                near_top = top
                top = jnp.maximum(jnp.max(scores, axis=0, keepdims=True), near_top)
                weights = jnp.exp(scores - top)
                shrink = jnp.exp(near_top - top)
                total = jnp.sum(weights, axis=0, keepdims=True) + shrink * total
                value = own_blocks(nn(turned[pl.ds(at, PAIR), some], weights.astype(BF16)))
                near = value + jnp.concatenate(
                    [near[0:HD] * shrink[:, 0:TILE], near[HD:PAIR] * shrink[:, TILE:]], axis=0
                )
            part = jnp.concatenate([near[0:HD] / total[:, 0:TILE], near[HD:PAIR] / total[:, TILE:]], axis=0)
            attended[rows, pl.ds(at, PAIR)] = part.T.astype(BF16)
            lse.ref[one] = top + jnp.log(total)

        over_tiles(span, tiles, pairs, 0, work)
        pack.ref[2] = attended[...]
        pack.ref[3] = normed_in()[...]
        pack.ref[1] = (gate_in()[:, 0:1] * wide(grad_in())).astype(BF16)
        branch = nn(attended[...], ow()[...]) + wide(ob)
        branch_out.ref[...] = branch
        branch_out.go()
        unit, _ = normalize(x_ref[0:width].astype(F32) + branch)
        second = (unit * wide(scale2_ref) + wide(offset2_ref)).astype(BF16)
        pack.ref[0] = second
        pack.go()
        turned_out.ref[...] = second.T

    low = shape_of((width, depth), BF16)
    return streamed(
        "far_attention", kernel, [spans], [query_bias, value_bias, scale, offset, out_bias, scale2, offset2],
        [full(far), full(routed)] + [columns(qkv_weight, i * depth, depth) for i in range(3)]
        + [full(a) for a in (queries, acc, stat, out_weight, gate, grad_routed, normed)],
        [
            low, low, low,
            shape_of((4, width, depth), BF16),
            shape_of((pairs * tiles, 2 * TILE), F32),
            shape_of((width, depth), F32),
            shape_of((depth, width), BF16),
            shape_of((2, 8, width), F32),
        ],
        scratch=[
            VMEM((width, width), F32), VMEM((depth, width), BF16), SMEM((2 * tiles,), I32),
            VMEM((width, depth), BF16),
        ],
        scalar_outs=[shape_of((2 * tiles,), I32)],
    )


def feed_blocks(core, pack, up_weight, up_bias, down_weight, carried, pair):
    width, depth = pack.shape[1:]
    first = carried is None
    step = 256
    tiles = depth // step

    def block_of(which, scalars):
        other = 1 - scalars[0][0]
        return 2 * pair + (other if which == 0 else 1 - other)

    def up_part(which, i):
        def part(ref, scalars):
            start = pl.multiple_of(block_of(which, scalars) * depth + i * step, step)
            return ref.at[:, pl.ds(start, step)]
        return (up_weight, part, (depth, step))

    def down_part(which):
        def part(ref, scalars):
            return ref.at[pl.ds(pl.multiple_of(block_of(which, scalars) * depth, step), depth)]
        return (down_weight, part, (depth, depth))

    def kernel(scalars, small, fetches, sends, scratch, scalar_outs):
        second = fetches[0]
        gfl = fetches[1]
        ups = (fetches[2 : 2 + tiles], fetches[3 + tiles : 3 + 2 * tiles])
        downs = (fetches[2 + tiles], fetches[3 + 2 * tiles])
        rest = fetches[4 + 2 * tiles :]
        send, own, back_out, feed_out, vec_out = sends
        if first:
            vec_out.ref[...] = jnp.zeros_like(vec_out.ref)
            vec_out.ref[4:5, :] = jnp.sum(wide(gfl()), axis=0, keepdims=True)
        else:
            vec_out.ref[...] = rest[2]()[...]
        for which, out in enumerate((send, own)):
            block = block_of(which, scalars)
            down_ref = None
            for i in range(tiles):
                cols = slice(i * step, (i + 1) * step)
                start = pl.multiple_of(block * depth + i * step, step)
                pre = nn(second()[...], ups[which][i]()[...])
                pre = pre + small[0][:, pl.ds(start, step)].astype(F32)
                squared = pre * pre
                inner = pre * (0.7978845608028654 + 0.035677408136300125 * squared)
                tanh = jnp.tanh(inner)
                half = 0.5 + 0.5 * tanh
                out.ref[0, :, cols] = (pre * half).astype(BF16)
                slope = half + pre * (0.5 * (1.0 - tanh * tanh)) * (
                    0.7978845608028654 + 0.10703222440890037 * squared
                )
                if down_ref is None:
                    down_ref = downs[which]()
                grad = (nt(gfl()[...], down_ref[cols, :]) * slope).astype(BF16)
                out.ref[1, :, cols] = grad
                vec_out.ref[pl.ds(block, 1), cols] = jnp.sum(grad.astype(F32), axis=0, keepdims=True)
            out.go()
        for at in range(0, depth, step):
            cols = slice(at, at + step)
            value = nn(send.ref[0], downs[0]()[:, cols]) + nn(own.ref[0], downs[1]()[:, cols])
            if not first:
                value = value + rest[1]()[:, cols]
            feed_out.ref[:, cols] = value
        feed_out.go()
        value = None
        for which, out in enumerate((send, own)):
            for i in range(tiles):
                part = nt(out.ref[1, :, i * step : (i + 1) * step], ups[which][i]()[...])
                if value is None:
                    value = part if first else part + rest[0]()[...]
                else:
                    value = value + part
        back_out.ref[...] = value

    acts = shape_of((2, width, depth), BF16)
    total = shape_of((width, depth), F32)
    return streamed(
        "feed_blocks", kernel, [core], [up_bias],
        [row_of(pack, 0), row_of(pack, 1)]
        + [up_part(0, i) for i in range(tiles)] + [down_part(0)]
        + [up_part(1, i) for i in range(tiles)] + [down_part(1)]
        + ([] if first else [full(c) for c in carried]),
        [acts, acts, total, total, shape_of((16, depth), F32)],
    )


def feed_grads(got, bit, turned, pack, far_pack, own):
    depth, width = turned.shape
    step = 256

    def kernel(scalars, small, fetches, sends, scratch, scalar_outs):
        turned_in, far_second, own_grad, got_grad, gfl, far_gfl, own_hidden, got_hidden = fetches
        send, keep = sends
        both = scratch[0]
        bit = scalars[0][0]
        for at in range(0, depth, step):
            cols = slice(at, at + step)
            value = nn(turned_in()[...], own_grad()[:, cols]) + tn(far_second()[...], got_grad()[:, cols])
            both[bit, :, cols] = value.astype(BF16)
        for at in range(0, depth, step):
            rows = slice(at, at + step)
            value = tn(own_hidden()[:, rows], gfl()[...]) + tn(got_hidden()[:, rows], far_gfl()[...])
            both[1 - bit, rows, :] = value.astype(BF16)
        keep.copy = pltpu.make_async_copy(both.at[0], keep.target, keep.sem)
        send.copy = pltpu.make_async_copy(both.at[1], send.target, send.sem)
        keep.go()
        send.go()

    half = shape_of((depth, depth), BF16)
    return streamed(
        "feed_grads", kernel, [jnp.reshape(bit, (1,)).astype(I32)], [],
        [full(turned), row_of(far_pack, 0), row_of(own, 1), row_of(got, 1),
         row_of(pack, 1), row_of(far_pack, 1), row_of(own, 0), row_of(got, 0)],
        [half, half],
        scratch=[VMEM((2, depth, depth), BF16)],
    )


def three_parts(value):
    high = value.astype(BF16)
    rest = value - high.astype(F32)
    middle_part = rest.astype(BF16)
    return high, middle_part, (rest - middle_part.astype(F32)).astype(BF16)


def middle(back, routed, branch, scale2, gate, grad_routed, out_weight, pack, lse, vec):
    width, depth = branch.shape
    tiles = width // TILE
    lots = lse.shape[0]
    extra = -(-lots // 16) * 16

    def kernel(scalars, small, fetches, sends, scratch, scalar_outs):
        back_in, x_in, branch_in, gate_in, grad_in, ow, att, lse_in, vec_in = fetches
        gout, mixed_out, low_out, delta_out, vec_out = sends
        back = back_in()[...]
        unit, inverse = normalize(wide(x_in()) + branch_in()[...])
        vec_out.ref[...] = vec_in()[...]
        vec_out.ref[5:6, :] = jnp.sum(back * unit, axis=0, keepdims=True)
        vec_out.ref[6:7, :] = jnp.sum(back, axis=0, keepdims=True)
        mixed = norm_back(back, wide(small[0]), unit, inverse)
        mixed_out.ref[...] = mixed
        mixed_out.go()
        low = (gate_in()[:, 0:1] * wide(grad_in()) + mixed).astype(BF16)
        low_out.ref[...] = low
        low_out.go()
        vec_out.ref[7:8, :] = jnp.sum(low.astype(F32), axis=0, keepdims=True)
        value = nt(low, ow()[...]).astype(BF16)
        gout.ref[0:width] = value
        product = value.astype(F32) * wide(att())
        high = product.astype(BF16)
        rest = (product - high.astype(F32)).astype(BF16)
        member = lax.broadcasted_iota(I32, (16, depth), 1) // HD
        ones = jnp.where(member == lax.broadcasted_iota(I32, (16, depth), 0), 1.0, 0.0).astype(BF16)
        delta = nt(ones, high) + nt(ones, rest)
        for head in range(H):
            for j in range(tiles):
                lot = (head // 2) * tiles + j
                at = (head % 2) * TILE
                delta_out.ref[lot : lot + 1, at : at + TILE] = delta[head : head + 1, j * TILE : (j + 1) * TILE]
        gout.ref[width:] = jnp.zeros_like(gout.ref[width:])
        for i, part in enumerate(three_parts(lse_in()[...])):
            gout.ref[width : width + lots, i * 2 * TILE : (i + 1) * 2 * TILE] = part
        for i, part in enumerate(three_parts(delta_out.ref[...])):
            gout.ref[width + extra : width + extra + lots, i * 2 * TILE : (i + 1) * 2 * TILE] = part

    low = shape_of((width, depth), BF16)
    return streamed(
        "middle", kernel, [], [scale2],
        [full(back), head_rows(routed, width)]
        + [full(a) for a in (branch, gate, grad_routed, out_weight)] + [row_of(pack, 2)]
        + [full(lse), full(vec)],
        [
            shape_of((width + 2 * extra, depth), BF16),
            shape_of((width, depth), F32),
            low,
            shape_of(lse.shape, F32),
            shape_of((16, depth), F32),
        ],
    )


def own_back(part, parts, q, k, v, gout, lse, delta, fk, fv, lines, spans, far_spans):
    width, depth = q.shape
    tiles = width // TILE
    some = depth // parts
    pairs = some // PAIR
    base = part * pairs * tiles

    def kernel(scalars, small, fetches, sends, scratch, scalar_outs):
        q_in, k_in, v_in, g_in, fk_in, fv_in, lse_in, delta_in, lines_in = fetches
        dq, dk, dv = sends
        bias, far_bias, turned, far_turned, span, far_span, dq_turned = scratch
        lines_ref = lines_in()
        fill_bias(bias, lines_ref[0], lines_ref[0], -1.0)
        fill_bias(far_bias, lines_ref[1], lines_ref[0], -2.0)
        store_spans(span, scalars[0], scalars[0], tiles)
        store_spans(far_span, scalars[1], scalars[0], tiles)
        k_ref, fk_ref, q_ref, g_ref, v_ref, fv_ref = k_in(), fk_in(), q_in(), g_in(), v_in(), fv_in()
        lse_ref, delta_ref = lse_in(), delta_in()
        turned[...] = k_ref[...].T
        far_turned[...] = fk_ref[...].T
        dk.ref[...] = jnp.zeros_like(dk.ref)
        dv.ref[...] = jnp.zeros_like(dv.ref)

        def pieces(j, pair):
            cols = pl.ds(pl.multiple_of(pair * PAIR, PAIR), PAIR)
            rows = pl.ds(pl.multiple_of(j * TILE, TILE), TILE)
            query = stacked_heads(q_ref[rows, cols]) * SCALE
            grad = stacked_heads(g_ref[rows, cols])
            one = pl.ds(base + pair * tiles + j, 1)
            return cols, rows, query, grad, lse_ref[one], delta_ref[one]

        def local(n, j, pair):
            cols, rows, query, grad, top, delta = pieces(j, pair)
            near = pl.ds(pl.multiple_of(span[j] * TILE, TILE), n * TILE)
            weights = jnp.exp(nt(k_ref[near, cols], query) + twice(bias[near, rows]) - top)
            dscore = (weights * (nt(v_ref[near, cols], grad) - delta)).astype(BF16)
            dk.ref[near, cols] += nn(dscore, query)
            dv.ref[near, cols] += nn(weights.astype(BF16), grad)
            dq_turned[cols, rows] = own_blocks(nn(turned[cols, near], dscore))

        def remote(n, j, pair):
            cols, rows, query, grad, top, delta = pieces(j, pair)
            far = pl.ds(pl.multiple_of(far_span[j] * TILE, TILE), n * TILE)
            weights = jnp.exp(nt(fk_ref[far, cols], query) + twice(far_bias[far, rows]) - top)
            dscore = (weights * (nt(fv_ref[far, cols], grad) - delta)).astype(BF16)
            dq_turned[cols, rows] += own_blocks(nn(far_turned[cols, far], dscore))

        over_tiles(span, tiles, pairs, 1, local)
        over_tiles(far_span, tiles, pairs, 1, remote)
        dq.ref[...] = (dq_turned[...].T * SCALE).astype(BF16)

    total = shape_of((width, some), F32)
    return streamed(
        "own_back", kernel, [spans, far_spans], [],
        [columns(a, part * some, some) for a in (q, k, v)]
        + [(gout, lambda ref, scalars: ref.at[0:width, part * some : (part + 1) * some], (width, some))]
        + [columns(a, part * some, some) for a in (fk, fv)]
        + [full(lse), full(delta), full(lines)],
        [shape_of((width, some), BF16), total, total],
        scratch=[
            VMEM((width, width), F32), VMEM((width, width), F32),
            VMEM((some, width), BF16), VMEM((some, width), BF16),
            SMEM((2 * tiles,), I32), SMEM((2 * tiles,), I32), VMEM((some, width), F32),
        ],
    )


def other_back(fgout, core, spans, far_spans, fq, k, v, lines, grads, low, vec):
    width, depth = k.shape
    tiles = width // TILE
    parts = len(grads)
    some = depth // parts
    pairs = some // PAIR
    lots = depth // PAIR * tiles
    extra = -(-lots // 16) * 16
    half = depth // 2

    def kernel(scalars, small, fetches, sends, scratch, scalar_outs):
        g_in, fq_in, k_in, v_in, lines_in, low_in, vec_in = fetches[:7]
        pieces = fetches[7:]
        halves = sends[:4]
        dq, dk, dv, vec_out = sends[4:]
        bias, span, stat, dk_sum, dv_sum = scratch
        lines_ref = lines_in()
        fill_bias(bias, lines_ref[0], lines_ref[1], -1.0)
        store_spans(span, scalars[1], scalars[2], tiles)
        g_ref = g_in()
        for i in range(2):
            block = g_ref[width + i * extra : width + i * extra + lots]
            stat[i] = (
                block[:, 0 : 2 * TILE].astype(F32)
                + block[:, 2 * TILE : 4 * TILE].astype(F32)
                + block[:, 4 * TILE : 6 * TILE].astype(F32)
            )
        fq_ref, k_ref, v_ref = fq_in(), k_in(), v_in()
        for part in range(parts):
            place = slice(part * some, (part + 1) * some)
            dq.ref[:, place] = pieces[3 * part]()[...]
            dk_sum[:, place] = pieces[3 * part + 1]()[...]
            dv_sum[:, place] = pieces[3 * part + 2]()[...]

        def work(n, j, pair):
            cols = pl.ds(pl.multiple_of(pair * PAIR, PAIR), PAIR)
            rows = pl.ds(pl.multiple_of(j * TILE, TILE), TILE)
            one = pl.ds(pair * tiles + j, 1)
            query = stacked_heads(fq_ref[rows, cols]) * SCALE
            grad = stacked_heads(g_ref[rows, cols])
            near = pl.ds(pl.multiple_of(span[j] * TILE, TILE), n * TILE)
            scores = nt(k_ref[near, cols], query) + twice(bias[near, rows])
            weights = jnp.exp(scores - stat[0, one])
            dscore = (weights * (nt(v_ref[near, cols], grad) - stat[1, one])).astype(BF16)
            dk_sum[near, cols] += nn(dscore, query)
            dv_sum[near, cols] += nn(weights.astype(BF16), grad)

        over_tiles(span, tiles, depth // PAIR, 1, work)
        dk.ref[...] = dk_sum[...].astype(BF16)
        dv.ref[...] = dv_sum[...].astype(BF16)
        low_ref = low_in()
        cols = pl.ds(pl.multiple_of((1 - scalars[0][0]) * half, TILE), half)
        for out, ref in zip(halves, (dq.ref, dk.ref, dv.ref, low_ref)):
            out.ref[...] = ref[:, cols]
            out.go()
        vec_out.ref[...] = vec_in()[...]
        vec_out.ref[8:9, :] = jnp.sum(wide(dq.ref), axis=0, keepdims=True)
        vec_out.ref[9:10, :] = jnp.sum(wide(dv.ref), axis=0, keepdims=True)

    flat = [piece for grad in grads for piece in grad]
    low_shape = shape_of((width, depth), BF16)
    return streamed(
        "other_back", kernel, [core, spans, far_spans], [],
        [full(a) for a in (fgout, fq, k, v, lines, low, vec)] + [full(a) for a in flat],
        [shape_of((width, half), BF16)] * 4 + [low_shape] * 3 + [shape_of((16, depth), F32)],
        scratch=[
            VMEM((width, width), F32), SMEM((2 * tiles,), I32), VMEM((2, lots, 2 * TILE), F32),
            VMEM((width, depth), F32), VMEM((width, depth), F32),
        ],
    )


def last_grads(core, bit, pack, far_pack, dq, dk, dv, low, got):
    width, depth = dq.shape
    half = depth // 2

    def kernel(scalars, small, fetches, sends, scratch, scalar_outs):
        normed, far_normed, att, far_att, dq_in, dk_in, dv_in, low_in = fetches[:8]
        gots = fetches[8:]
        send, keep = sends
        turned = scratch[0]
        cols = pl.ds(pl.multiple_of(scalars[0][0] * half, TILE), half)
        for i, ref in enumerate((normed, far_normed, att, far_att)):
            turned[i // 2, :, (i % 2) * width : (i % 2 + 1) * width] = ref()[...].T
        for out, which in ((send, 1 - scalars[1][0]), (keep, scalars[1][0])):
            rows = pl.ds(pl.multiple_of(which * half, TILE), half)
            for i, part in enumerate((dq_in, dk_in, dv_in, low_in)):
                place = slice(i * half, (i + 1) * half)
                side = 0 if i < 3 else 1
                value = nn(turned[side, rows, 0:width], part()[:, cols])
                value = value + nn(turned[side, rows, width : 2 * width], gots[i]()[...])
                out.ref[:, place] = value.astype(BF16)
            out.go()

    shape = shape_of((half, 2 * depth), BF16)
    return streamed(
        "last_grads", kernel, [core, jnp.reshape(bit, (1,)).astype(I32)], [],
        [row_of(pack, 3), row_of(far_pack, 3), row_of(pack, 2), row_of(far_pack, 2)]
        + [full(a) for a in (dq, dk, dv, low) + tuple(got)],
        [shape, shape],
        scratch=[VMEM((2, depth, 2 * width), BF16)],
    )


def scatter(hot_ref, rows, slots_ref):
    hot = hot_ref[...]
    taken = jnp.max(hot.astype(F32), axis=-1, keepdims=True) > 0.0
    return jnp.where(taken, nn(hot, rows).astype(BF16), slots_ref[...])


def token_out(hot, tokens, routed, gate, branch, feed, down_bias, grad_routed, router, mixed, vec):
    slots, depth = tokens.shape
    width = branch.shape[0]

    def kernel(scalars, small, fetches, sends, scratch, scalar_outs):
        branch_in, feed_in, x_in, gate_in, grad_in, mixed_in, vec_in, hot_in, tok_in = fetches
        out, base, vec_out = sends
        total = branch_in()[...] + feed_in()[...] + wide(small[0])
        x = wide(x_in())
        gate = gate_in()[:, 0:1]
        grad = wide(grad_in())
        logit = jnp.sum(grad * total, axis=-1, keepdims=True) * gate * (1.0 - gate)
        base.ref[...] = grad + mixed_in()[...] + logit * wide(small[1])
        base.go()
        vec_out.ref[...] = vec_in()[...]
        vec_out.ref[12:13, :] = jnp.sum(x * logit, axis=0, keepdims=True)
        out.ref[...] = scatter(hot_in(), (x + gate * total).astype(BF16), tok_in())

    return streamed(
        "token_out", kernel, [], [down_bias, router],
        [full(branch), full(feed), head_rows(routed, width)]
        + [full(a) for a in (gate, grad_routed, mixed, vec, hot, tokens)],
        [shape_of((slots, depth), BF16), shape_of((width, depth), F32), shape_of((16, depth), F32)],
    )


def token_grad(dq, dk, dv, hot, cotangent, routed, base, scale, qkv_weight, vec):
    slots, depth = cotangent.shape
    width = base.shape[0]

    def kernel(scalars, small, fetches, sends, scratch, scalar_outs):
        dq_in, weight_q, dk_in, weight_k, dv_in, weight_v, x_in, base_in, vec_in, hot_in, cot_in = fetches
        out, vec_out = sends
        back = nt(dq_in()[...], weight_q()[...]) + nt(dk_in()[...], weight_k()[...])
        back = back + nt(dv_in()[...], weight_v()[...])
        unit, inverse = normalize(wide(x_in()))
        vec_out.ref[...] = vec_in()[...]
        vec_out.ref[10:11, :] = jnp.sum(back * unit, axis=0, keepdims=True)
        vec_out.ref[11:12, :] = jnp.sum(back, axis=0, keepdims=True)
        vec_out.go()
        rows = (base_in()[...] + norm_back(back, wide(small[0]), unit, inverse)).astype(BF16)
        out.ref[...] = scatter(hot_in(), rows, cot_in())

    return streamed(
        "token_grad", kernel, [], [scale],
        [
            full(dq), columns(qkv_weight, 0, depth), full(dk), columns(qkv_weight, depth, depth),
            full(dv), columns(qkv_weight, 2 * depth, depth), head_rows(routed, width),
            full(base), full(vec), full(hot), full(cotangent),
        ],
        [shape_of((slots, depth), BF16), shape_of((16, depth), F32)],
    )


AXES = ("rows", "seq")
SHIFT = {"c": 0, "x": 1, "z1": 2, "z2": 3}
BLOCK = 16
XY_FIRST = (("x", "y"), ("y", "x"), ("z1", "z1"), ("z2", "z2"))
Z_FIRST = (("z1", "z1"), ("x", "y"), ("y", "x"), ("z2", "z2"))
X_FIRST = (("x", "x"), ("y", "y"), ("z1", "z1"), ("z2", "z2"))


def swap(block, axes):
    route = []
    for row in range(lax.axis_size("rows")):
        axis = axes[row & 1]
        for seq in range(2):
            if axis == "y":
                other = row * 2 + (seq ^ 1)
            else:
                other = (row ^ (1 << SHIFT[axis])) * 2 + seq
            route.append((row * 2 + seq, other))
    return lax.ppermute(block, AXES, route)


def own_bit(axis):
    if axis == "y":
        return lax.axis_index("seq")
    return (lax.axis_index("rows") >> SHIFT[axis]) & 1


def stage_bit(axes, core):
    if axes[0] == axes[1]:
        return own_bit(axes[0])
    return jnp.where(core == 0, own_bit(axes[0]), own_bit(axes[1]))


def half_of(block, which):
    half = block.shape[0] // 2
    return lax.dynamic_slice_in_dim(block, which * half, half, 0)


def add_low(left, right):
    return (left.astype(F32) + right.astype(F32)).astype(BF16)


def after(value, *others):
    return lax.optimization_barrier((value, *others))[0]


def over_blocks(total):
    extra = BLOCK
    size = lax.axis_size("rows")
    while extra < size:
        route = [(i * 2 + j, (i ^ extra) * 2 + j) for i in range(size) for j in range(2)]
        got = lax.ppermute(total, AXES, route)
        total = (total.astype(F32) + got.astype(F32)).astype(total.dtype)
        extra *= 2
    return total


class Order:
    def __init__(self):
        self.tail = None

    def run(self, call, lead, *args):
        if self.tail is not None:
            lead = after(lead, self.tail)
        result = call(lead, *args)
        self.tail = jax.tree.leaves(result)[-1]
        return result


class Sum:
    def __init__(self, order, send, keep, stages):
        self.order, self.keep, self.stages, self.at = order, keep, stages, 1
        self.got = swap(send, stages[0])

    def reduce(self):
        if self.at == len(self.stages):
            self.keep = over_blocks(self.order.run(add_low, self.got, self.keep))
            self.got = swap(self.keep, self.stages[-1])
            return
        axes = self.stages[self.at]
        bit = stage_bit(axes, own_bit("c"))
        send = self.order.run(lambda got, keep: add_low(half_of(keep, 1 - bit), half_of(got, 1 - bit)), self.got, self.keep)
        got = swap(send, axes)
        self.keep = self.order.run(lambda got, keep: add_low(half_of(keep, bit), half_of(got, bit)), self.got, self.keep)
        self.got = got
        self.at += 1

    def gather(self):
        self.at -= 1
        self.keep = self.order.run(lambda got, keep: jnp.concatenate([keep, got]), self.got, self.keep)
        self.got = swap(self.keep, self.stages[self.at - 1] if self.at else ("c", "c"))


class SmallSum:
    def __init__(self, order, block):
        self.order, self.block, self.left = order, block, ["c", "x", "y", "z1", "z2"]
        self.send()

    def send(self):
        axis = self.left.pop(0)
        self.got = swap(self.block, (axis, axis))

    def step(self):
        self.block = self.order.run(lambda got, block: got + block, self.got, self.block)
        if self.left:
            self.send()

    def total(self):
        return over_blocks(self.block)


def shard_of(stages, core):
    index = jnp.int32(0)
    for axes in stages:
        index = index * 2 + stage_bit(axes, core)
    return index


SHARDS = 16


def place_kernel(split, info_ref, block_ref, *rest):
    first_ref, second_ref, low, full, sems = rest[-5:]
    rows = block_ref.shape[0] // SHARDS
    own = info_ref[0]
    lot = info_ref[1]
    depth = block_ref.shape[1]

    def pull(s):
        src = pl.ds(pl.multiple_of((s ^ own) * rows, rows), rows)
        dst = pl.ds(s * rows, rows)
        return pltpu.make_async_copy(block_ref.at[src], low.at[dst], sems.at[0, s])

    def push(s):
        src = pl.ds(s * rows, rows)
        if split == "feed":
            per = SHARDS // 2
            if s < per:
                to = first_ref.at[pl.ds(s * rows, rows), pl.ds(pl.multiple_of(lot * depth, 128), depth)]
            else:
                to = second_ref.at[pl.ds(pl.multiple_of(lot * depth + (s - per) * rows, rows), rows)]
            return [pltpu.make_async_copy(full.at[src], to, sems.at[1, s])]
        part = depth // 4
        copies = []
        for t in range(4):
            target = first_ref if t < 3 else second_ref
            at = (2 * t + lot) * part if t < 3 else lot * part
            copies.append(
                pltpu.make_async_copy(
                    full.at[src, pl.ds(t * part, part)],
                    target.at[pl.ds(s * rows, rows), pl.ds(pl.multiple_of(at, 128), part)],
                    sems.at[1 + t, s],
                )
            )
        return copies

    for s in range(SHARDS):
        pull(s).start()
    for s in range(SHARDS):
        pull(s).wait()
        dst = slice(s * rows, (s + 1) * rows)
        full[dst] = low[dst].astype(F32)
        for copy in push(s):
            copy.start()
    for s in range(SHARDS):
        for copy in push(s):
            copy.wait()


def place(split, info, block, targets, shapes):
    hbm = pl.BlockSpec(memory_space=pl.ANY)
    targets = targets or ()
    return pl.pallas_call(
        functools.partial(place_kernel, split),
        out_shape=tuple(jax.ShapeDtypeStruct(s, F32) for s in shapes),
        in_specs=[pl.BlockSpec(memory_space=pltpu.SMEM), hbm] + [hbm] * len(targets),
        out_specs=(hbm, hbm),
        scratch_shapes=[
            VMEM(block.shape, BF16),
            VMEM(block.shape, F32),
            pltpu.SemaphoreType.DMA((5, SHARDS)),
        ],
        input_output_aliases={2: 0, 3: 1} if targets else {},
        compiler_params=pltpu.CompilerParams(vmem_limit_bytes=16 << 20),
        cost_estimate=pl.CostEstimate(flops=0, bytes_accessed=0, transcendentals=0),
        name="place",
    )(info, block, *targets)


def body(
    tokens,
    cotangent,
    segment_ids,
    routing,
    qkv_weight,
    query_bias,
    value_bias,
    out_weight,
    out_bias,
    first_scale,
    first_offset,
    second_scale,
    second_offset,
    up_weight,
    up_bias,
    down_weight,
    down_bias,
    router_weight,
):
    row_count, slots, depth = tokens.shape
    hidden = up_weight.shape[1]
    count = slots // 2
    width = -(-count // 128) * 128
    core = own_bit("c")
    seat = jnp.reshape(core, (1,)).astype(jnp.int32)
    pos = jnp.reshape(lax.axis_index("seq"), (1,)).astype(jnp.int32)
    tokens = tokens.reshape(slots, depth)
    cotangent = cotangent.reshape(slots, depth)
    routes = routing.reshape(2, 1, slots)
    segs = segment_ids.reshape(2, 1, slots)
    qb, vb, ob, s1, o1, s2, o2, db, rw = (
        v.reshape(1, depth)
        for v in (query_bias, value_bias, out_bias, first_scale, first_offset, second_scale,
                  second_offset, down_bias, router_weight)
    )
    ub = up_bias.reshape(1, hidden)

    order = Order()
    routed, grad_routed, hot, spans = pick_rows(pos, routes, segs, tokens, cotangent, count, width)
    far = swap(routed, ("y", "y"))
    q, k, v, normed, gate, acc, stat = near_attention(spans, routed, qkv_weight, qb, vb, s1, o1, rw)
    fq, fk, fv, pack, lse, branch, turned, lines, far_spans = order.run(
        far_attention, far, spans, routed, qkv_weight, qb, vb, s1, o1, count, q, acc, stat,
        out_weight, ob, s2, o2, gate, grad_routed, normed
    )
    far_pack = swap(pack, ("c", "c"))

    plans = (Z_FIRST, X_FIRST, XY_FIRST)
    first_bits = [stage_bit(plan[0], core) for plan in plans]
    gots, owns = [], []
    carried = None
    for pair in range(2):
        send, own, *carried = order.run(feed_blocks, seat, pack, up_weight, ub, down_weight, carried, pair)
        gots.append(swap(send, ("c", "c")))
        owns.append(own)
    back, feed_sum, vec = carried

    def feed_sums(pair):
        send, keep = order.run(
            feed_grads, gots[pair], first_bits[pair], turned, pack, far_pack, owns[pair]
        )
        return Sum(order, send, keep, plans[pair])

    one = feed_sums(0)
    two = feed_sums(1)
    gout, mixed, low, delta, vec = order.run(
        middle, back, routed, branch, s2, gate, grad_routed, out_weight, pack, lse, vec
    )
    fgout = swap(gout, ("y", "y"))
    grads = [
        order.run(
            lambda q, part=part: own_back(part, 2, q, k, v, gout, lse, delta, fk, fv, lines, spans, far_spans), q
        )
        for part in range(2)
    ]
    one.reduce()
    out_tokens, base, vec = order.run(
        token_out, hot, tokens, routed, gate, branch, feed_sum, db, grad_routed, rw, mixed, vec
    )
    two.reduce()
    *last_sends, dq, dk, dv, vec = order.run(
        other_back, fgout, seat, spans, far_spans, fq, k, v, lines, grads, low, vec
    )
    gots = [swap(send, ("c", "c")) for send in last_sends]
    one.reduce()
    two.reduce()
    grad_tokens, vec = order.run(token_grad, dq, dk, dv, hot, cotangent, routed, base, s1, qkv_weight, vec)
    one.reduce()
    two.reduce()
    send, keep = order.run(
        lambda got, *rest: last_grads(seat, first_bits[2], pack, far_pack, dq, dk, dv, low, (got,) + rest), *gots
    )
    three = Sum(order, send, keep, plans[2])
    small = SmallSum(order, vec)
    one.reduce()
    two.reduce()
    three.reduce()
    small.step()
    one.gather()
    two.gather()
    three.reduce()
    small.step()
    one.gather()
    two.gather()
    three.reduce()
    small.step()
    one.gather()
    two.gather()
    three.reduce()
    small.step()
    three.gather()
    small.step()
    three.gather()
    one.gather()
    two.gather()
    three.gather()
    vec = small.total()

    def put(part, index, targets):
        plan = plans[index]
        shapes, kind = ((depth, hidden), (hidden, depth)), "feed"
        if index == 2:
            shapes, kind = ((depth, 3 * depth), (depth, depth)), "last"
        for block, owner in ((part.keep, core), (part.got, 1 - core)):
            lot = owner if index == 2 else 2 * index + owner
            info = jnp.stack([shard_of(plan, owner), lot]).astype(jnp.int32)
            targets = order.run(lambda info, *rest: place(kind, info, *rest), info, block, targets, shapes)
        return targets

    pair_grads = put(one, 0, None)
    three.gather()
    grad_qkv, grad_out = put(three, 2, None)
    grad_up, grad_down = put(two, 1, pair_grads)
    return (
        out_tokens.reshape(row_count, slots, depth),
        grad_tokens.reshape(row_count, slots, depth),
        grad_qkv,
        vec[8],
        vec[9],
        grad_out,
        vec[7],
        vec[10],
        vec[11],
        vec[5],
        vec[6],
        grad_up,
        vec[0:4].reshape(hidden),
        grad_down,
        vec[4],
        vec[12],
    )


def solution(mesh):
    split = P("rows", "seq", None)
    return jax.shard_map(
        body,
        mesh=mesh,
        in_specs=(split, split, P("rows", None), P("rows", None)) + (P(),) * 14,
        out_specs=(split, split) + (P(),) * 14,
        check_vma=False,
    )
```

time: 1040 us -> 366 us (0.35)
  waiting for transfers between devices: 601 us -> 85.5 us
  Pallas kernels: 0 us -> 175 us
  matrix products: 128 us -> 0 us
  local copies, waits for them, and re-layouts: 122 us -> 21.8 us
  blocking collectives: 83.6 us -> 0 us
  starting transfers between devices: 4.92 us -> 43.7 us
  other arithmetic: 69.9 us -> 32 us
  between operations: 15.1 us -> 1.59 us
    unnamed x6 -> x0, waiting for transfers between devices: 434 us -> none
    pallas_call x0 -> x20, Pallas kernels: none -> 175 us  [the longest x14 147 us: streamed(): pl.pallas_call(wrapped, out_shape=tuple(outs) + tuple(scalar_outs), in_sp...]
    all_gather x4 -> x0, waiting for transfers between devices: 138 us -> none  [the longest x1 72.9 us: body(): lax.all_gather(feed_shares[1], ('rows', 'seq'), axis=0, tiled=True)]
    dot_general x26 -> x0, matrix products: 128 us -> none  [the longest x2 25.2 us: block_grads(): jnp.einsum('rqhd,rkhd->rhqk', grad_attended, block_values, preferred_elem...]
    unnamed x2 -> x0, blocking collectives: 83.6 us -> none
    ppermute x2 -> x41, waiting for transfers between devices: 29.4 us -> 85.5 us  [swap(): return lax.ppermute(block, AXES, route)]
    reshape x7 -> x13, local copies, waits for them, and re-layouts: 55.7 us -> 7.81 us  [the longest x9 5.23 us: body(): v.reshape(1, depth)]
    ppermute x2 -> x41, starting transfers between devices: 4.71 us -> 43.7 us  [swap(): return lax.ppermute(block, AXES, route)]
  transfers between devices with their start and end apart: 7 -> 41, of which waited for: 5 -> 12; matrix products, arithmetic and copies ran while one was open for 15% -> 12% of each run, Pallas kernels for 0% -> 39%
where the time goes in v1:
time: 366 us; the launch traced here: 360 us
  Pallas kernels  175 us (48%)
  waiting for transfers between devices  85.5 us (23%)
  starting transfers between devices  43.7 us (12%)
  other arithmetic  32 us (9%)
  local copies, waits for them, and re-layouts  21.8 us (6%)
    pallas_call x14, Pallas kernels, streamed(): pl.pallas_call(wrapped, out_shape=tuple(outs) + tuple(scalar_outs), in_sp...  147 us
    ppermute x41, waiting for transfers between devices, swap(): return lax.ppermute(block, AXES, route)  85.5 us
    ppermute x41, starting transfers between devices, swap(): return lax.ppermute(block, AXES, route)  43.7 us
    pallas_call x6, Pallas kernels, place(): pl.pallas_call(functools.partial(place_kernel, split), out_shape=tuple((j...  28.3 us
    convert_element_type x18, other arithmetic, add_low(): return (left.astype(F32) + right.astype(F32)).astype(BF16)  24 us
    unnamed x59, local copies, waits for them, and re-layouts  9.74 us
  transfers between devices with their start and end apart: 41, of which 12 were waited for; matrix products, arithmetic and copies ran while one was open for 12% of the time, Pallas kernels for 39%

profile of v1, /device:TPU:0, one launch (start us, length us, event | category | flops | bytes accessed | tf_op | source)
XLA Modules:
  0.0 359.7 jit_solution(2258627999108284689)
XLA Ops:
  3.6 6.2 %pick_rows.1 = (bf16[528,768]{1,0:T(8,128)(2,1)}, bf16[512,768]{1,0:T(8,128)(2,1)}, bf16[944,512]{1,0:T(8,128)(2,1)}, s32[8]{0:T(128)}) custom-call(s32[1]{0:T(128)} %bitcast.refs_0_, s32[2,1,944]{2,1,0:T(1,128)} %reshape.101.refs_1_, s32[2,1,944]{2,1,0:T(1,128)} %reshape.102.refs_2_, bf16[944,768]{1,0:T(8,128)(2,1)} %bitcast.17, bf16[944,768]{1,0:T(8,128)(2,1)} %bitcast.19), custom_call_target="tpu_custom_call" | custom-call | bytes 600000 | tf_op jit(solution)/shard_map/pick_rows/pallas_call | solution.py:118
  9.8 3.0 collective-permute-start
  17.5 16.7 %near_attention.1 = (bf16[512,768]{1,0:T(8,128)(2,1)}, bf16[512,768]{1,0:T(8,128)(2,1)}, bf16[512,768]{1,0:T(8,128)(2,1)}, bf16[512,768]{1,0:T(8,128)(2,1)}, f32...) custom-call(s32[8]{0:T(128)} %get-tuple-element.143.refs_0_.refs_1_, ...), custom_call_target="tpu_custom_call" | custom-call | bytes 1600000 | tf_op jit(solution)/shard_map/near_attention/pallas_call | solution.py:118
  35.1 15.6 %far_attention.1 = (bf16[512,768]{1,0:T(8,128)(2,1)}, bf16[512,768]{1,0:T(8,128)(2,1)}, bf16[512,768]{1,0:T(8,128)(2,1)}, bf16[4,512,768]{2,1,0:T(8,128)(2,1)}, ...) custom-call(s32[8]{0:T(128)} %get-tuple-element.143.refs_0_.refs_1_, ...), custom_call_target="tpu_custom_call" | custom-call | bytes 1600000 | tf_op jit(solution)/shard_map/far_attention/pallas_call | solution.py:118
  51.4 13.1 %feed_blocks.2 = (bf16[2,512,768]{2,1,0:T(8,128)(2,1)}, bf16[2,512,768]{2,1,0:T(8,128)(2,1)}, f32[512,768]{1,0:T(8,128)}, f32[512,768]{1,0:T(8,128)}, f32[16,768]{1,0:T(8,128)}) custom-call(s32[1]{0:T(128)} %bitcast.3.refs_0_, bf16[1,3072]{1,0:T(2,128)(2,1)} %reshape.113.refs_1_, bf16[4,512,768]{2,1,0:T(8,128)(2,1)} %get-tuple-element.154.refs_2_.refs_5_.refs_7_, ...), custom_call_target="tpu_custom_call" | custom-call | bytes 1300000 | tf_op jit(solution)/shard_map/feed_blocks/pallas_call | solution.py:118
  65.0 17.0 %feed_blocks.3 = (bf16[2,512,768]{2,1,0:T(8,128)(2,1)}, bf16[2,512,768]{2,1,0:T(8,128)(2,1)}, f32[512,768]{1,0:T(8,128)}, f32[512,768]{1,0:T(8,128)}, f32[16,768]{1,0:T(8,128)}) custom-call(s32[1]{0:T(128)} %bitcast.3.refs_0_, bf16[1,3072]{1,0:T(2,128)(2,1)} %reshape.113.refs_1_, bf16[4,512,768]{2,1,0:T(8,128)(2,1)} %get-tuple-element.154.refs_2_.refs_5_.refs_7_, ...), custom_call_target="tpu_custom_call" | custom-call | bytes 1300000 | tf_op jit(solution)/shard_map/feed_blocks/pallas_call | solution.py:118
  82.1 7.0 %feed_grads.2 = (bf16[768,768]{1,0:T(8,128)(2,1)}, bf16[768,768]{1,0:T(8,128)(2,1)}) custom-call(s32[1]{0:T(128)} %bitcast.5.refs_0_, bf16[768,512]{1,0:T(8,128)(2,1)} %get-tuple-element.161.refs_1_, bf16[4,512,768]{2,1,0:T(8,128)(2,1)} %collective-permute-done.1.refs_2_.refs_3_, bf16[2,512,768]{2,1,0:T(8,128)(2,1)} %get-tuple-element.164.refs_3_, ...), custom_call_target="tpu_custom_call" | custom-call | bytes 700000 | tf_op jit(solution)/shard_map/feed_grads/pallas_call | solution.py:118
  90.6 7.0 %feed_grads.3 = (bf16[768,768]{1,0:T(8,128)(2,1)}, bf16[768,768]{1,0:T(8,128)(2,1)}) custom-call(s32[1]{0:T(128)} %bitcast.4.refs_0_, bf16[768,512]{1,0:T(8,128)(2,1)} %get-tuple-element.161.refs_1_, bf16[4,512,768]{2,1,0:T(8,128)(2,1)} %collective-permute-done.1.refs_2_.refs_3_, bf16[2,512,768]{2,1,0:T(8,128)(2,1)} %get-tuple-element.162.refs_3_, ...), custom_call_target="tpu_custom_call" | custom-call | bytes 700000 | tf_op jit(solution)/shard_map/feed_grads/pallas_call | solution.py:118
  97.6 2.9 collective-permute-start.6
  100.5 8.0 %middle.1 = (bf16[576,768]{1,0:T(8,128)(2,1)}, f32[512,768]{1,0:T(8,128)}, bf16[512,768]{1,0:T(8,128)(2,1)}, f32[24,256]{1,0:T(8,128)}, f32[16,768]{1,0:T(8,128)}) custom-call(bf16[1,768]{1,0:T(2,128)(2,1)} %reshape.110.refs_6_.refs_0_, f32[512,768]{1,0:T(8,128)} %get-tuple-element.171.refs_1_, ...), custom_call_target="tpu_custom_call" | custom-call | bytes 800000 | tf_op jit(solution)/shard_map/middle/pallas_call | solution.py:118
  109.7 10.7 %own_back.2 = (bf16[512,384]{1,0:T(8,128)(2,1)}, f32[512,384]{1,0:T(8,128)}, f32[512,384]{1,0:T(8,128)}) custom-call(s32[8]{0:T(128)} %get-tuple-element.143.refs_0_.refs_1_, s32[8]{0:T(128)} %get-tuple-element.152.refs_1_.refs_2_, bf16[512,768]{1,0:T(8,128)(2,1)} %get-tuple-element.186.refs_11_.refs_2_, ...), custom_call_target="tpu_custom_call" | custom-call | bytes 900000 | tf_op jit(solution)/shard_map/own_back/pallas_call | solution.py:118
  120.4 11.1 %own_back.3 = (bf16[512,384]{1,0:T(8,128)(2,1)}, f32[512,384]{1,0:T(8,128)}, f32[512,384]{1,0:T(8,128)}) custom-call(s32[8]{0:T(128)} %get-tuple-element.143.refs_0_.refs_1_, s32[8]{0:T(128)} %get-tuple-element.152.refs_1_.refs_2_, bf16[512,768]{1,0:T(8,128)(2,1)} %get-tuple-element.186.refs_11_.refs_2_, ...), custom_call_target="tpu_custom_call" | custom-call | bytes 900000 | tf_op jit(solution)/shard_map/own_back/pallas_call | solution.py:118
  134.8 6.6 %token_out.1 = (bf16[944,768]{1,0:T(8,128)(2,1)}, f32[512,768]{1,0:T(8,128)}, f32[16,768]{1,0:T(8,128)}) custom-call(bf16[1,768]{1,0:T(2,128)(2,1)} %reshape.98.refs_0_, bf16[1,768]{1,0:T(2,128)(2,1)} %reshape.99.refs_5_.refs_1_, f32[512,768]{1,0:T(8,128)} %get-tuple-element.151.refs_3_.refs_2_, f32[512,768]{1,0:T(8,128)} %get-tuple-element.159.refs_3_, ...), custom_call_target="tpu_custom_call" | custom-call | bytes 700000 | tf_op jit(solution)/shard_map/token_out/pallas_call | solution.py:118
  146.2 10.2 %other_back.1 = (bf16[512,384]{1,0:T(8,128)(2,1)}, bf16[512,384]{1,0:T(8,128)(2,1)}, bf16[512,384]{1,0:T(8,128)(2,1)}, bf16[512,384]{1,0:T(8,128)(2,1)}, bf16[51...) custom-call(s32[1]{0:T(128)} %bitcast.3.refs_0_, ...), custom_call_target="tpu_custom_call" | custom-call | bytes 900000 | tf_op jit(solution)/shard_map/other_back/pallas_call | solution.py:118
  163.2 9.6 %token_grad.1 = (bf16[944,768]{1,0:T(8,128)(2,1)}, f32[16,768]{1,0:T(8,128)}) custom-call(bf16[1,768]{1,0:T(2,128)(2,1)} %reshape.107.refs_3_.refs_0_, bf16[512,768]{1,0:T(8,128)(2,1)} %get-tuple-element.209.refs_1_.refs_4_, bf16[768,2304]{1,0:T(8,128)(2,1)} %refs_2_.1, bf16[512,768]{1,0:T(8,128)(2,1)} %get-tuple-element.210.refs_3_.refs_5_, ...), custom_call_target="tpu_custom_call" | custom-call | bytes 900000 | tf_op jit(solution)/shard_map/token_grad/pallas_call | solution.py:118
  179.2 8.2 %last_grads.1 = (bf16[384,1536]{1,0:T(8,128)(2,1)}, bf16[384,1536]{1,0:T(8,128)(2,1)}) custom-call(s32[1]{0:T(128)} %bitcast.3.refs_0_, s32[1]{0:T(128)} %bitcast.11.refs_1_, bf16[4,512,768]{2,1,0:T(8,128)(2,1)} %get-tuple-element.154.refs_2_.refs_5_.refs_7_, bf16[4,512,768]{2,1,0:T(8,128)(2,1)} %collective-permute-done.1.refs_2_.refs_3_, ...), custom_call_target="tpu_custom_call" | custom-call | bytes 800000 | tf_op jit(solution)/shard_map/last_grads/pallas_call | solution.py:118
  187.9 3.0 collective-permute-start.17
  191.0 11.0 %collective-permute-done.17 = bf16[96,768]{1,0:T(8,128)(2,1)S(1)} collective-permute-done((bf16[96,768]{1,0:T(8,128)(2,1)S(1)}, bf16[96,768]{1,0:T(8,128)(2,1)S(1)}, u32[]{:S(2)}, u32[]{:S(2)}) %collective-permute-start.17) | collective-permute-done | bytes 147488 | tf_op jit(solution)/shard_map/ppermute | solution.py:857
  212.4 8.2 %collective-permute-done.20 = bf16[96,768]{1,0:T(8,128)(2,1)S(1)} collective-permute-done((bf16[96,768]{1,0:T(8,128)(2,1)S(1)}, bf16[96,768]{1,0:T(8,128)(2,1)S(1)}, u32[]{:S(2)}, u32[]{:S(2)}) %collective-permute-start.20) | collective-permute-done | bytes 147488 | tf_op jit(solution)/shard_map/ppermute | solution.py:857
  235.2 4.5 %collective-permute-done.22 = bf16[96,1536]{1,0:T(8,128)(2,1)} collective-permute-done((bf16[96,1536]{1,0:T(8,128)(2,1)}, bf16[96,1536]{1,0:T(8,128)(2,1)}, u32[]{:S(2)}, u32[]{:S(2)}) %collective-permute-start.22) | collective-permute-done | bytes 294944 | tf_op jit(solution)/shard_map/ppermute | solution.py:857
  246.4 4.3 %collective-permute-done.27 = bf16[384,768]{1,0:T(8,128)(2,1)S(1)} collective-permute-done((bf16[384,768]{1,0:T(8,128)(2,1)S(1)}, bf16[384,768]{1,0:T(8,128)(2,1)S(1)}, u32[]{:S(2)}, u32[]{:S(2)}) %collective-permute-start.27) | collective-permute-done | bytes 589856 | tf_op jit(solution)/shard_map/ppermute | solution.py:857
  254.5 24.5 %collective-permute-done.31 = f32[16,768]{1,0:T(8,128)S(1)} collective-permute-done((f32[16,768]{1,0:T(8,128)S(1)}, f32[16,768]{1,0:T(8,128)S(1)}, u32[]{:S(2)}, u32[]{:S(2)}) %collective-permute-start.31) | collective-permute-done | bytes 49184 | tf_op jit(solution)/shard_map/ppermute | solution.py:857
  280.6 3.3 collective-permute-start.33
  290.8 22.0 %collective-permute-done.35 = bf16[768,768]{1,0:T(8,128)(2,1)S(1)} collective-permute-done((bf16[768,768]{1,0:T(8,128)(2,1)S(1)}, bf16[768,768]{1,0:T(8,128)(2,1)S(1)}, u32[]{:S(2)}, u32[]{:S(2)}) %collective-permute-start.35) | collective-permute-done | bytes 1179680 | tf_op jit(solution)/shard_map/ppermute | solution.py:857
  318.3 4.4 %place.6 = (f32[768,3072]{1,0:T(8,128)}, f32[3072,768]{1,0:T(8,128)}) custom-call(s32[2]{0:T(128)S(1)} %get-tuple-element.251.info_ref, bf16[1536,768]{1,0:T(8,128)(2,1)} %constant_dynamic-update-slice_fusion.block_ref), custom_call_target="tpu_custom_call" | custom-call | tf_op jit(solution)/shard_map/place/pallas_call | solution.py:1011
  323.5 4.4 %place.7 = (f32[768,3072]{1,0:T(8,128)}, f32[3072,768]{1,0:T(8,128)}) custom-call(s32[2]{0:T(128)S(1)} %get-tuple-element.253.info_ref, bf16[1536,768]{1,0:T(8,128)(2,1)} %collective-permute-done.38.block_ref, f32[768,3072]{1,0:T(8,128)} %get-tuple-element.254.rest_0_, ...), custom_call_target="tpu_custom_call", output_to_operand_aliasing={{0}: (2, {}), {1}: (3, {})} | custom-call | tf_op jit(solution)/shard_map/place/pallas_call | solution.py:1011
  327.9 2.7 collective-permute-done.37
  333.0 3.4 collective-permute-start.39
  337.8 4.3 %place.8 = (f32[768,2304]{1,0:T(8,128)}, f32[768,768]{1,0:T(8,128)}) custom-call(s32[2]{0:T(128)S(1)} %get-tuple-element.257.info_ref, bf16[768,1536]{1,0:T(8,128)(2,1)} %constant_dynamic-update-slice_fusion.10.block_ref), custom_call_target="tpu_custom_call" | custom-call | tf_op jit(solution)/shard_map/place/pallas_call | solution.py:1011
  344.2 4.3 %place.9 = (f32[768,2304]{1,0:T(8,128)}, f32[768,768]{1,0:T(8,128)}) custom-call(s32[2]{0:T(128)S(1)} %get-tuple-element.259.info_ref, bf16[768,1536]{1,0:T(8,128)(2,1)} %collective-permute-done.39.block_ref, f32[768,2304]{1,0:T(8,128)} %get-tuple-element.260.rest_0_, ...), custom_call_target="tpu_custom_call", output_to_operand_aliasing={{0}: (2, {}), {1}: (3, {})} | custom-call | tf_op jit(solution)/shard_map/place/pallas_call | solution.py:1011
  348.6 6.5 %place.10 = (f32[768,3072]{1,0:T(8,128)}, f32[3072,768]{1,0:T(8,128)}) custom-call(s32[2]{0:T(128)S(1)} %pad_add_fusion.5.info_ref, bf16[1536,768]{1,0:T(8,128)(2,1)S(1)} %constant_dynamic-update-slice_fusion.5.block_ref, f32[768,3072]{1,0:T(8,128)} %get-tuple-element.264.rest_0_, ...), custom_call_target="tpu_custom_call", output_to_operand_aliasing={{0}: (2, {}), {1}: (3, {})} | custom-call | tf_op jit(solution)/shard_map/place/pallas_call | solution.py:1011
  355.1 4.4 %place.11 = (f32[768,3072]{1,0:T(8,128)}, f32[3072,768]{1,0:T(8,128)}) custom-call(s32[2]{0:T(128)S(1)} %pad_add_fusion.4.info_ref, bf16[1536,768]{1,0:T(8,128)(2,1)} %collective-permute-done.40.block_ref, f32[768,3072]{1,0:T(8,128)} %get-tuple-element.267.rest_0_, f32[3072,768]{1,0:T(8,128)} %get-tuple-element.265.rest_1_), custom_call_target="tpu_custom_call", output_to_operand_aliasing={{0}: (2, {}), {1}: (3, {})} | custom-call | tf_op jit(solution)/shard_map/place/pallas_call | solution.py:1011
  (188 shorter events, 90.2 us)
Async XLA Ops:
  9.8 24.4 %collective-permute-start = (bf16[528,768]{1,0:T(8,128)(2,1)}, bf16[528,768]{1,0:T(8,128)(2,1)S(1)}, u32[]{:S(2)}, u32[]{:S(2)}) collective-permute-start(bf16[528,768]{1,0:T(8,128)(2,1)} %get-tuple-element.144.refs_6_.refs_9_.refs_2_.refs_4_.refs_5_), channel_id=1, source_target_pairs={{0,1},{1,0},{2,3},{3,2},{4,5},{5,4},{6,7},{7,6},{8,9},{9,8},{10,11... | collective-permute-start | bytes 2433032 | tf_op jit(solution)/shard_map/ppermute | solution.py:857
  50.7 31.4 %collective-permute-start.1 = (bf16[4,512,768]{2,1,0:T(8,128)(2,1)}, bf16[4,512,768]{2,1,0:T(8,128)(2,1)}, u32[]{:S(2)}, u32[]{:S(2)}) collective-permute-start(bf16[4,512,768]{2,1,0:T(8,128)(2,1)} %get-tuple-element.154.refs_2_.refs_5_.refs_7_), channel_id=1, source_target_pairs={{0,2},{1,3},{2,0},{3,1},{4,6},{5,7},{6,4},{7,5},{8,10},{9,11},{10,... | collective-permute-start | bytes 9437192 | tf_op jit(solution)/shard_map/ppermute | solution.py:857
  64.5 17.6 %collective-permute-start.3 = (bf16[2,512,768]{2,1,0:T(8,128)(2,1)}, bf16[2,512,768]{2,1,0:T(8,128)(2,1)}, u32[]{:S(2)}, u32[]{:S(2)}) collective-permute-start(bf16[2,512,768]{2,1,0:T(8,128)(2,1)} %get-tuple-element.165), channel_id=1, source_target_pairs={{0,2},{1,3},{2,0},{3,1},{4,6},{5,7},{6,4},{7,5},{8,10},{9,11},{10,... | collective-permute-start | bytes 4718600 | tf_op jit(solution)/shard_map/ppermute | solution.py:857
  89.1 42.4 %collective-permute-start.4 = (bf16[768,768]{1,0:T(8,128)(2,1)}, bf16[768,768]{1,0:T(8,128)(2,1)}, u32[]{:S(2)}, u32[]{:S(2)}) collective-permute-start(bf16[768,768]{1,0:T(8,128)(2,1)} %get-tuple-element.176), channel_id=1, source_target_pairs={{0,8},{1,9},{2,10},{3,11},{4,12},{5,13},{6,14},{7,15},{8,0},{9,1},... | collective-permute-start | bytes 3538952 | tf_op jit(solution)/shard_map/ppermute | solution.py:857
  97.6 43.8 %collective-permute-start.6 = (bf16[768,768]{1,0:T(8,128)(2,1)}, bf16[768,768]{1,0:T(8,128)(2,1)}, u32[]{:S(2)}, u32[]{:S(2)}) collective-permute-start(bf16[768,768]{1,0:T(8,128)(2,1)} %get-tuple-element.192), channel_id=1, source_target_pairs={{0,4},{1,5},{2,6},{3,7},{4,0},{5,1},{6,2},{7,3},{8,12},{9,13},{10,... | collective-permute-start | bytes 3538952 | tf_op jit(solution)/shard_map/ppermute | solution.py:857
  108.5 37.7 %collective-permute-start.5 = (bf16[576,768]{1,0:T(8,128)(2,1)}, bf16[576,768]{1,0:T(8,128)(2,1)}, u32[]{:S(2)}, u32[]{:S(2)}) collective-permute-start(bf16[576,768]{1,0:T(8,128)(2,1)} %get-tuple-element.180.refs_5_), channel_id=1, source_target_pairs={{0,1},{1,0},{2,3},{3,2},{4,5},{5,4},{6,7},{7,6},{8,9},{9,8},{10,11... | collective-permute-start | bytes 2654216 | tf_op jit(solution)/shard_map/ppermute | solution.py:857
  133.6 23.5 %collective-permute-start.8 = (bf16[384,768]{1,0:T(8,128)(2,1)}, bf16[384,768]{1,0:T(8,128)(2,1)}, u32[]{:S(2)}, u32[]{:S(2)}) collective-permute-start(bf16[384,768]{1,0:T(8,128)(2,1)} %add_convert_fusion.5), channel_id=1, source_target_pairs={{0,4},{1,5},{2,3},{3,2},{4,0},{5,1},{6,7},{7,6},{8,12},{9,13},{10,... | collective-permute-start | bytes 1769480 | tf_op jit(solution)/shard_map/ppermute | solution.py:857
  143.5 16.9 %collective-permute-start.7 = (bf16[384,768]{1,0:T(8,128)(2,1)}, bf16[384,768]{1,0:T(8,128)(2,1)}, u32[]{:S(2)}, u32[]{:S(2)}) collective-permute-start(bf16[384,768]{1,0:T(8,128)(2,1)} %add_convert_fusion.3), channel_id=1, source_target_pairs={{0,1},{1,0},{2,3},{3,2},{4,5},{5,4},{6,7},{7,6},{8,9},{9,8},{10,11... | collective-permute-start | bytes 1769480 | tf_op jit(solution)/shard_map/ppermute | solution.py:857
  156.4 21.9 %collective-permute-start.9 = (bf16[512,384]{1,0:T(8,128)(2,1)}, bf16[512,384]{1,0:T(8,128)(2,1)S(1)}, u32[]{:S(2)}, u32[]{:S(2)}) collective-permute-start(bf16[512,384]{1,0:T(8,128)(2,1)} %get-tuple-element.214), channel_id=1, source_target_pairs={{0,2},{1,3},{2,0},{3,1},{4,6},{5,7},{6,4},{7,5},{8,10},{9,11},{10,... | collective-permute-start | bytes 1179656 | tf_op jit(solution)/shard_map/ppermute | solution.py:857
  156.5 21.9 %collective-permute-start.12 = (bf16[512,384]{1,0:T(8,128)(2,1)}, bf16[512,384]{1,0:T(8,128)(2,1)}, u32[]{:S(2)}, u32[]{:S(2)}) collective-permute-start(bf16[512,384]{1,0:T(8,128)(2,1)} %get-tuple-element.221), channel_id=1, source_target_pairs={{0,2},{1,3},{2,0},{3,1},{4,6},{5,7},{6,4},{7,5},{8,10},{9,11},{10,... | collective-permute-start | bytes 1179656 | tf_op jit(solution)/shard_map/ppermute | solution.py:857
  157.0 21.4 %collective-permute-start.13 = (bf16[512,384]{1,0:T(8,128)(2,1)}, bf16[512,384]{1,0:T(8,128)(2,1)}, u32[]{:S(2)}, u32[]{:S(2)}) collective-permute-start(bf16[512,384]{1,0:T(8,128)(2,1)} %get-tuple-element.222), channel_id=1, source_target_pairs={{0,2},{1,3},{2,0},{3,1},{4,6},{5,7},{6,4},{7,5},{8,10},{9,11},{10,... | collective-permute-start | bytes 1179656 | tf_op jit(solution)/shard_map/ppermute | solution.py:857
  158.8 13.9 %collective-permute-start.11 = (bf16[192,768]{1,0:T(8,128)(2,1)}, bf16[192,768]{1,0:T(8,128)(2,1)}, u32[]{:S(2)}, u32[]{:S(2)}) collective-permute-start(bf16[192,768]{1,0:T(8,128)(2,1)} %add_convert_fusion.11), channel_id=1, source_target_pairs={{0,1},{1,0},{2,6},{3,7},{4,5},{5,4},{6,2},{7,3},{8,9},{9,8},{10,14... | collective-permute-start | bytes 884744 | tf_op jit(solution)/shard_map/ppermute | solution.py:857
  162.1 14.3 %collective-permute-start.10 = (bf16[192,768]{1,0:T(8,128)(2,1)}, bf16[192,768]{1,0:T(8,128)(2,1)}, u32[]{:S(2)}, u32[]{:S(2)}) collective-permute-start(bf16[192,768]{1,0:T(8,128)(2,1)} %add_convert_fusion.9), channel_id=1, source_target_pairs={{0,8},{1,9},{2,10},{3,11},{4,12},{5,13},{6,14},{7,15},{8,0},{9,1},... | collective-permute-start | bytes 884744 | tf_op jit(solution)/shard_map/ppermute | solution.py:857
  187.5 16.8 %collective-permute-start.15 = (bf16[384,1536]{1,0:T(8,128)(2,1)}, bf16[384,1536]{1,0:T(8,128)(2,1)S(1)}, u32[]{:S(2)}, u32[]{:S(2)}) collective-permute-start(bf16[384,1536]{1,0:T(8,128)(2,1)} %get-tuple-element.225), channel_id=1, source_target_pairs={{0,4},{1,5},{2,3},{3,2},{4,0},{5,1},{6,7},{7,6},{8,12},{9,13},{10,... | collective-permute-start | bytes 3538952 | tf_op jit(solution)/shard_map/ppermute | solution.py:857
  187.9 14.0 %collective-permute-start.17 = (bf16[96,768]{1,0:T(8,128)(2,1)S(1)}, bf16[96,768]{1,0:T(8,128)(2,1)S(1)}, u32[]{:S(2)}, u32[]{:S(2)}) collective-permute-start(bf16[96,768]{1,0:T(8,128)(2,1)S(1)} %add_convert_fusion.20), channel_id=1, source_target_pairs={{0,16},{1,17},{2,18},{3,19},{4,20},{5,21},{6,22},{7,23},{8,24},{9,... | collective-permute-start | bytes 442376 | tf_op jit(solution)/shard_map/ppermute | solution.py:857
  190.9 13.3 %collective-permute-start.16 = (bf16[96,768]{1,0:T(8,128)(2,1)S(1)}, bf16[96,768]{1,0:T(8,128)(2,1)S(1)}, u32[]{:S(2)}, u32[]{:S(2)}) collective-permute-start(bf16[96,768]{1,0:T(8,128)(2,1)S(1)} %add_convert_fusion.18), channel_id=1, source_target_pairs={{0,16},{1,17},{2,18},{3,19},{4,20},{5,21},{6,22},{7,23},{8,24},{9,... | collective-permute-start | bytes 442376 | tf_op jit(solution)/shard_map/ppermute | solution.py:857
  205.5 18.7 %collective-permute-start.18 = (bf16[192,1536]{1,0:T(8,128)(2,1)}, bf16[192,1536]{1,0:T(8,128)(2,1)}, u32[]{:S(2)}, u32[]{:S(2)}) collective-permute-start(bf16[192,1536]{1,0:T(8,128)(2,1)} %add_convert_fusion.1), channel_id=1, source_target_pairs={{0,1},{1,0},{2,6},{3,7},{4,5},{5,4},{6,2},{7,3},{8,9},{9,8},{10,14... | collective-permute-start | bytes 1769480 | tf_op jit(solution)/shard_map/ppermute | solution.py:857
  206.9 13.7 %collective-permute-start.20 = (bf16[96,768]{1,0:T(8,128)(2,1)S(1)}, bf16[96,768]{1,0:T(8,128)(2,1)S(1)}, u32[]{:S(2)}, u32[]{:S(2)}) collective-permute-start(bf16[96,768]{1,0:T(8,128)(2,1)S(1)} %get-tuple-element.280), channel_id=1, source_target_pairs={{0,16},{1,17},{2,18},{3,19},{4,20},{5,21},{6,22},{7,23},{8,24},{9,... | collective-permute-start | bytes 442376 | tf_op jit(solution)/shard_map/ppermute | solution.py:857
  208.4 15.0 %collective-permute-start.19 = (bf16[96,768]{1,0:T(8,128)(2,1)S(1)}, bf16[96,768]{1,0:T(8,128)(2,1)S(1)}, u32[]{:S(2)}, u32[]{:S(2)}) collective-permute-start(bf16[96,768]{1,0:T(8,128)(2,1)S(1)} %get-tuple-element.282), channel_id=1, source_target_pairs={{0,16},{1,17},{2,18},{3,19},{4,20},{5,21},{6,22},{7,23},{8,24},{9,... | collective-permute-start | bytes 442376 | tf_op jit(solution)/shard_map/ppermute | solution.py:857
  211.2 18.6 %collective-permute-start.25 = (f32[16,768]{1,0:T(8,128)S(1)}, f32[16,768]{1,0:T(8,128)S(1)}, u32[]{:S(2)}, u32[]{:S(2)}) collective-permute-start(f32[16,768]{1,0:T(8,128)S(1)} %add.231), channel_id=1, source_target_pairs={{0,4},{1,5},{2,6},{3,7},{4,0},{5,1},{6,2},{7,3},{8,12},{9,13},{10,... | collective-permute-start | bytes 147464 | tf_op jit(solution)/shard_map/ppermute | solution.py:857
  226.0 13.7 %collective-permute-start.22 = (bf16[96,1536]{1,0:T(8,128)(2,1)}, bf16[96,1536]{1,0:T(8,128)(2,1)}, u32[]{:S(2)}, u32[]{:S(2)}) collective-permute-start(bf16[96,1536]{1,0:T(8,128)(2,1)} %add_convert_fusion.7), channel_id=1, source_target_pairs={{0,8},{1,9},{2,10},{3,11},{4,12},{5,13},{6,14},{7,15},{8,0},{9,1},... | collective-permute-start | bytes 884744 | tf_op jit(solution)/shard_map/ppermute | solution.py:857
  231.2 12.2 %collective-permute-start.28 = (bf16[384,768]{1,0:T(8,128)(2,1)}, bf16[384,768]{1,0:T(8,128)(2,1)}, u32[]{:S(2)}, u32[]{:S(2)}) collective-permute-start(bf16[384,768]{1,0:T(8,128)(2,1)} %pad_maximum_fusion.3), channel_id=1, source_target_pairs={{0,4},{1,5},{2,3},{3,2},{4,0},{5,1},{6,7},{7,6},{8,12},{9,13},{10,... | collective-permute-start | bytes 1769480 | tf_op jit(solution)/shard_map/ppermute | solution.py:857
  234.4 16.3 %collective-permute-start.27 = (bf16[384,768]{1,0:T(8,128)(2,1)S(1)}, bf16[384,768]{1,0:T(8,128)(2,1)S(1)}, u32[]{:S(2)}, u32[]{:S(2)}) collective-permute-start(bf16[384,768]{1,0:T(8,128)(2,1)S(1)} %pad_maximum_fusion.4), channel_id=1, source_target_pairs={{0,1},{1,0},{2,3},{3,2},{4,5},{5,4},{6,7},{7,6},{8,9},{9,8},{10,11... | collective-permute-start | bytes 1769480 | tf_op jit(solution)/shard_map/ppermute | solution.py:857
  244.6 44.6 %collective-permute-start.36 = (bf16[768,768]{1,0:T(8,128)(2,1)S(1)}, bf16[768,768]{1,0:T(8,128)(2,1)S(1)}, u32[]{:S(2)}, u32[]{:S(2)}) collective-permute-start(bf16[768,768]{1,0:T(8,128)(2,1)S(1)} %pad_maximum_fusion), channel_id=1, source_target_pairs={{0,8},{1,9},{2,10},{3,11},{4,12},{5,13},{6,14},{7,15},{8,0},{9,1},... | collective-permute-start | bytes 3538952 | tf_op jit(solution)/shard_map/ppermute | solution.py:857
  251.5 27.6 %collective-permute-start.30 = (bf16[48,1536]{1,0:T(8,128)(2,1)S(1)}, bf16[48,1536]{1,0:T(8,128)(2,1)S(1)}, u32[]{:S(2)}, u32[]{:S(2)}) collective-permute-start(bf16[48,1536]{1,0:T(8,128)(2,1)S(1)} %get-tuple-element.284), channel_id=1, source_target_pairs={{0,16},{1,17},{2,18},{3,19},{4,20},{5,21},{6,22},{7,23},{8,24},{9,... | collective-permute-start | bytes 442376 | tf_op jit(solution)/shard_map/ppermute | solution.py:857
  252.5 26.6 %collective-permute-start.31 = (f32[16,768]{1,0:T(8,128)S(1)}, f32[16,768]{1,0:T(8,128)S(1)}, u32[]{:S(2)}, u32[]{:S(2)}) collective-permute-start(f32[16,768]{1,0:T(8,128)S(1)} %add.239), channel_id=1, source_target_pairs={{0,8},{1,9},{2,10},{3,11},{4,12},{5,13},{6,14},{7,15},{8,0},{9,1},... | collective-permute-start | bytes 147464 | tf_op jit(solution)/shard_map/ppermute | solution.py:857
  283.9 28.9 %collective-permute-start.35 = (bf16[768,768]{1,0:T(8,128)(2,1)S(1)}, bf16[768,768]{1,0:T(8,128)(2,1)S(1)}, u32[]{:S(2)}, u32[]{:S(2)}) collective-permute-start(bf16[768,768]{1,0:T(8,128)(2,1)S(1)} %pad_maximum_fusion.1), channel_id=1, source_target_pairs={{0,4},{1,5},{2,6},{3,7},{4,0},{5,1},{6,2},{7,3},{8,12},{9,13},{10,... | collective-permute-start | bytes 3538952 | tf_op jit(solution)/shard_map/ppermute | solution.py:857
  290.3 33.2 %collective-permute-start.38 = (bf16[1536,768]{1,0:T(8,128)(2,1)}, bf16[1536,768]{1,0:T(8,128)(2,1)}, u32[]{:S(2)}, u32[]{:S(2)}) collective-permute-start(bf16[1536,768]{1,0:T(8,128)(2,1)} %constant_dynamic-update-slice_fusion.block_ref), channel_id=1, source_target_pairs={{0,2},{1,3},{2,0},{3,1},{4,6},{5,7},{6,4},{7,5},{8,10},{9,11},{10,... | collective-permute-start | bytes 7077896 | tf_op jit(solution)/shard_map/ppermute | solution.py:857
  290.3 22.5 %collective-permute-start.34 = (bf16[192,1536]{1,0:T(8,128)(2,1)S(1)}, bf16[192,1536]{1,0:T(8,128)(2,1)S(1)}, u32[]{:S(2)}, u32[]{:S(2)}) collective-permute-start(bf16[192,1536]{1,0:T(8,128)(2,1)S(1)} %pad_maximum_fusion.5), channel_id=1, source_target_pairs={{0,1},{1,0},{2,6},{3,7},{4,5},{5,4},{6,2},{7,3},{8,9},{9,8},{10,14... | collective-permute-start | bytes 1769480 | tf_op jit(solution)/shard_map/ppermute | solution.py:857
  314.1 16.5 %collective-permute-start.37 = (bf16[384,1536]{1,0:T(8,128)(2,1)}, bf16[384,1536]{1,0:T(8,128)(2,1)}, u32[]{:S(2)}, u32[]{:S(2)}) collective-permute-start(bf16[384,1536]{1,0:T(8,128)(2,1)} %pad_maximum_fusion.2), channel_id=1, source_target_pairs={{0,4},{1,5},{2,3},{3,2},{4,0},{5,1},{6,7},{7,6},{8,12},{9,13},{10,... | collective-permute-start | bytes 3538952 | tf_op jit(solution)/shard_map/ppermute | solution.py:857
  333.0 11.3 %collective-permute-start.39 = (bf16[768,1536]{1,0:T(8,128)(2,1)}, bf16[768,1536]{1,0:T(8,128)(2,1)}, u32[]{:S(2)}, u32[]{:S(2)}) collective-permute-start(bf16[768,1536]{1,0:T(8,128)(2,1)} %constant_dynamic-update-slice_fusion.10.block_ref), channel_id=1, source_target_pairs={{0,2},{1,3},{2,0},{3,1},{4,6},{5,7},{6,4},{7,5},{8,10},{9,11},{10,... | collective-permute-start | bytes 7077896 | tf_op jit(solution)/shard_map/ppermute | solution.py:857
  336.4 18.7 %collective-permute-start.40 = (bf16[1536,768]{1,0:T(8,128)(2,1)S(1)}, bf16[1536,768]{1,0:T(8,128)(2,1)}, u32[]{:S(2)}, u32[]{:S(2)}) collective-permute-start(bf16[1536,768]{1,0:T(8,128)(2,1)S(1)} %constant_dynamic-update-slice_fusion.5.block_ref), channel_id=1, source_target_pairs={{0,2},{1,3},{2,0},{3,1},{4,6},{5,7},{6,4},{7,5},{8,10},{9,11},{10,... | collective-permute-start | bytes 7077896 | tf_op jit(solution)/shard_map/ppermute | solution.py:857
  (34 other events, 338.0 us)

commit v2 on v1

v2 whole, which is shorter than its diff:
```python
import functools

import jax
import jax.numpy as jnp
from jax import lax
from jax.experimental import pallas as pl
from jax.experimental.pallas import tpu as pltpu
from jax.sharding import PartitionSpec as P

H = 12
HD = 64
PAIR = 2 * HD
TILE = 128
NEG = -1e30
SCALE = HD ** (-0.5)
RATE = 1.15e9
LENGTH = {
    "pick_rows": 6.0,
    "near_attention": 14.0,
    "far_and_feed": 36.0,
    "feed_grads": 3.0,
    "own_back": 5.0,
    "other_back": 1.0,
    "token_out": 1.0,
    "last_grads": 8.0,
    "token_grad": 14.0,
    "place": 1.0,
}
F32 = jnp.float32
BF16 = jnp.bfloat16
I32 = jnp.int32
VMEM = pltpu.VMEM
SMEM = pltpu.SMEM


def nn(a, b):
    return lax.dot_general(a, b, (((1,), (0,)), ((), ())), preferred_element_type=F32)


def nt(a, b):
    return lax.dot_general(a, b, (((1,), (1,)), ((), ())), preferred_element_type=F32)


def tn(a, b):
    return lax.dot_general(a, b, (((0,), (0,)), ((), ())), preferred_element_type=F32)


def shape_of(shape, kind):
    return jax.ShapeDtypeStruct(shape, kind)


class Fetch:
    def __init__(self, copies, target):
        self.copies, self.target = copies, target
        self.waiting = set(range(len(copies)))
        for copy in copies:
            copy.start()

    def __call__(self, piece=None):
        for i in sorted(self.waiting) if piece is None else [piece]:
            if i in self.waiting:
                self.copies[i].wait()
                self.waiting.discard(i)
        return self.target


class Send:
    def __init__(self, buffer, target, sems, pieces):
        self.ref, self.target, self.sem, self.copies = buffer, target, sems, []
        for i in range(pieces):
            source, to = (buffer, target) if pieces == 1 else (buffer.at[i], target.at[i])
            self.copies.append(pltpu.make_async_copy(source, to, sems.at[i]))
        self.left = set(range(pieces))

    def go(self, piece=None):
        for i in sorted(self.left) if piece is None else [piece]:
            if i in self.left:
                self.copies[i].start()
                self.left.discard(i)

    def wait(self):
        self.go()
        for copy in self.copies:
            copy.wait()


def streamed(name, kernel, scalars, small, large, outs, scratch=(), scalar_outs=(), room=62, split=()):
    arrays, plans = [], []
    for array, parts, extent in large:
        at = next((i for i, a in enumerate(arrays) if a is array), None)
        if at is None:
            at = len(arrays)
            arrays.append(array)
        if parts is None or callable(parts):
            parts = [(parts, None)]
        plans.append((at, parts, extent))
    most_in = max(len(p) for _, p, _ in plans)
    counts = [o.shape[0] if i in split else 1 for i, o in enumerate(outs)]

    def wrapped(*refs):
        refs = list(refs)

        def take(count):
            head = refs[:count]
            del refs[:count]
            return head

        scalar_refs = take(len(scalars))
        small_refs = take(len(small))
        array_refs = take(len(arrays))
        out_refs = take(len(outs))
        scalar_out_refs = take(len(scalar_outs))
        landing = take(len(plans))
        staging = take(len(outs))
        in_sems, out_sems = take(2)
        fetches = []
        for i, (at, parts, _) in enumerate(plans):
            copies = []
            for j, (source, place) in enumerate(parts):
                start = array_refs[at] if source is None else source(array_refs[at], scalar_refs)
                to = landing[i] if place is None else place(landing[i])
                copies.append(pltpu.make_async_copy(start, to, in_sems.at[i, j]))
            fetches.append(Fetch(copies, landing[i]))
        sends = [Send(staging[i], out_refs[i], out_sems.at[i], counts[i]) for i in range(len(outs))]
        kernel(scalar_refs, small_refs, fetches, sends, refs, scalar_out_refs)
        for fetch in fetches:
            fetch()
        for send in sends:
            send.go()
        for send in sends:
            send.wait()

    hbm = pl.BlockSpec(memory_space=pltpu.HBM)
    return pl.pallas_call(
        wrapped,
        out_shape=tuple(outs) + tuple(scalar_outs),
        in_specs=[pl.BlockSpec(memory_space=SMEM)] * len(scalars)
        + [pl.BlockSpec(memory_space=VMEM)] * len(small)
        + [hbm] * len(arrays),
        out_specs=tuple([hbm] * len(outs) + [pl.BlockSpec(memory_space=SMEM)] * len(scalar_outs)),
        scratch_shapes=[VMEM(extent, arrays[at].dtype) for at, _, extent in plans]
        + [VMEM(o.shape, o.dtype) for o in outs]
        + [pltpu.SemaphoreType.DMA((len(plans), most_in)), pltpu.SemaphoreType.DMA((len(outs), max(counts)))]
        + list(scratch),
        compiler_params=pltpu.CompilerParams(vmem_limit_bytes=room << 20),
        cost_estimate=pl.CostEstimate(flops=int(LENGTH[name] * RATE), bytes_accessed=0, transcendentals=0),
        name=name,
    )(*scalars, *small, *arrays)


def full(array):
    return (array, None, array.shape)


def row_of(array, index):
    return (array, lambda ref, scalars: ref.at[index], array.shape[1:])


def head_rows(array, count):
    return (array, lambda ref, scalars: ref.at[0:count], (count,) + array.shape[1:])


def columns(array, start, count):
    return (array, lambda ref, scalars: ref.at[:, start : start + count], (array.shape[0], count))


def wide(ref):
    return ref[...].astype(F32)


def normalize(values):
    center = values - jnp.mean(values, axis=-1, keepdims=True)
    inverse = lax.rsqrt(jnp.mean(center * center, axis=-1, keepdims=True) + 1e-06)
    return center * inverse, inverse


def norm_back(grad, scale, unit, inverse):
    scaled = grad * scale
    first = jnp.mean(scaled, axis=-1, keepdims=True)
    second = jnp.mean(scaled * unit, axis=-1, keepdims=True)
    return inverse * (scaled - first - unit * second)


def tile_spans(line, count, out_ref):
    width = line.shape[1]
    lane = lax.broadcasted_iota(I32, (1, width), 1)
    tiles = width // TILE
    for i in range(tiles):
        inside = (lane >= i * TILE) & (lane < min((i + 1) * TILE, count))
        out_ref[i] = jnp.min(jnp.where(inside, line, 1e9)).astype(I32)
        out_ref[tiles + i] = jnp.max(jnp.where(inside, line, -1e9)).astype(I32)


def pick_rows(pos, routes, segs, tokens, cotangent, count, width):
    slots, depth = tokens.shape

    def kernel(scalars, small, fetches, sends, scratch, scalar_outs):
        route, seg, tok, cot = fetches
        routed, grad, hot_out = sends
        lane = lax.broadcasted_iota(I32, (slots, width), 1)
        slot = lax.broadcasted_iota(I32, (slots, width), 0)
        chosen = (slot == route()[:, :width]) & (lane < count)
        taken = jnp.max(jnp.where(chosen, 1.0, 0.0), axis=-1, keepdims=True)
        before = lax.broadcasted_iota(I32, (slots, slots), 0) < lax.broadcasted_iota(I32, (slots, slots), 1)
        before = jnp.where(before, 1.0, 0.0).astype(BF16)
        rank = tn(before, jnp.broadcast_to(taken, (slots, TILE)).astype(BF16))[:, 0:1]
        rank = jnp.where(taken > 0.0, rank, -1.0)
        hot = jnp.where(lane.astype(F32) == rank, 1.0, 0.0).astype(BF16)
        hot_out.ref[...] = hot
        hot_out.go()
        groups = jnp.broadcast_to(seg()[...].astype(F32), (8, slots)).astype(BF16)
        line = nn(groups, hot)
        line = jnp.where(lax.broadcasted_iota(I32, (8, width), 1) < count, line, -1.0)
        routed.ref[0:width] = tn(hot, tok()[...]).astype(BF16)
        routed.ref[width:] = jnp.zeros_like(routed.ref[width:])
        routed.ref[width : width + 8, 0:width] = line.astype(BF16)
        routed.go()
        grad.ref[...] = tn(hot, cot()[...]).astype(BF16)
        tile_spans(line[0:1], count, scalar_outs[0])

    return streamed(
        "pick_rows", kernel, [pos], [],
        [
            (routes, lambda ref, scalars: ref.at[scalars[0][0]], routes.shape[1:]),
            (segs, lambda ref, scalars: ref.at[scalars[0][0]], segs.shape[1:]),
            full(tokens), full(cotangent),
        ],
        [shape_of((width + 16, depth), BF16), shape_of((width, depth), BF16), shape_of((slots, width), BF16)],
        scalar_outs=[shape_of((2 * (width // TILE),), I32)],
    )


def key_span(keys, queries, j, tiles):
    low, high = queries[j], queries[tiles + j]
    first, last = jnp.int32(tiles), jnp.int32(-1)
    for t in range(tiles):
        meets = (keys[tiles + t] >= low) & (keys[t] <= high)
        first = jnp.where(meets & (first == tiles), t, first)
        last = jnp.where(meets, t, last)
    return jnp.minimum(first, tiles - 1), jnp.maximum(last - first + 1, 0)


def store_spans(ref, keys, queries, tiles):
    for j in range(tiles):
        first, many = key_span(keys, queries, j, tiles)
        ref[j] = first
        ref[tiles + j] = many


def fill_bias(bias_ref, key_line, query_line, key_pad):
    keys = jnp.where(key_line < 0.0, key_pad, key_line).T[:, 0:1]
    bias_ref[...] = jnp.where(keys == query_line[0:1], 0.0, NEG)


def fill_row_bias(bias_ref, key_line, query_line, key_pad):
    keys = jnp.where(key_line < 0.0, key_pad, key_line)[0:1]
    bias_ref[...] = jnp.where(query_line.T[:, 0:1] == keys, 0.0, NEG)


def first_head():
    return lax.broadcasted_iota(I32, (1, PAIR), 1) < HD


def attend_rows(query, keys, values, bias):
    first = first_head()
    zero = jnp.zeros_like(query)
    wide_values = jnp.concatenate([values, jnp.ones_like(values)], axis=1)
    sums, tops = [], []
    for head in range(2):
        some = jnp.where(first if head == 0 else jnp.logical_not(first), query, zero) * SCALE
        scores = nt(some, keys) + bias
        top = jnp.max(scores, axis=1, keepdims=True)
        sums.append(nn(jnp.exp(scores - top).astype(BF16), wide_values))
        tops.append(top)
    value = jnp.where(first, sums[0][:, 0:PAIR], sums[1][:, 0:PAIR])
    total = jnp.where(first, sums[0][:, PAIR:], sums[1][:, PAIR:])
    return value, total, jnp.where(first, tops[0], tops[1])


def stacked_heads(block):
    lane = lax.broadcasted_iota(I32, (1, PAIR), 1)
    zero = jnp.zeros_like(block)
    return jnp.concatenate([jnp.where(lane < HD, block, zero), jnp.where(lane >= HD, block, zero)], axis=0)


def own_blocks(block):
    return jnp.concatenate([block[0:HD, 0:TILE], block[HD:PAIR, TILE : 2 * TILE]], axis=0)


def twice(block):
    return jnp.concatenate([block, block], axis=1)


def over_tiles(span, tiles, pairs, lowest, work, group=3):
    def tile_step(j, carry):
        for n in range(lowest, tiles + 1):

            def branch(n=n):
                def group_step(i, inner):
                    for p in range(group):
                        work(n, j, i * group + p)
                    return inner

                lax.fori_loop(0, pairs // group, group_step, 0)

            pl.when(span[tiles + j] == n)(branch)
        return carry

    lax.fori_loop(0, tiles, tile_step, 0)


def project(normed, weights, qb, vb, q_ref, k_ref, v_ref, sends):
    depth = normed.shape[1]
    step = 256
    for part, (ref, weight) in enumerate(zip((k_ref, q_ref, v_ref), (weights[1], weights[0], weights[2]))):
        weight_ref = weight()
        for at in range(0, depth, step):
            value = nn(normed, weight_ref[:, at : at + step])
            if part == 1:
                value = value + qb[:, at : at + step]
            elif part == 2:
                value = value + vb[:, at : at + step]
            ref[:, at : at + step] = value.astype(BF16)
        sends[part].go()


def near_attention(spans, routed, qkv_weight, query_bias, value_bias, scale, offset, router):
    depth = routed.shape[1]
    width = routed.shape[0] - 16
    tiles = width // TILE
    pairs = depth // PAIR

    def kernel(scalars, small, fetches, sends, scratch, scalar_outs):
        qb, vb, scale_ref, offset_ref, router_ref = small
        q, k, v, normed, gate, acc, lse = sends
        bias, span = scratch
        x_ref = fetches[0]()
        x = x_ref[0:width].astype(F32)
        unit, _ = normalize(x)
        low = (unit * wide(scale_ref) + wide(offset_ref)).astype(BF16)
        normed.ref[...] = low
        normed.go()
        project(low, fetches[1:4], wide(qb), wide(vb), q.ref, k.ref, v.ref, (k, q, v))
        logit = jnp.sum(x * wide(router_ref), axis=-1, keepdims=True)
        gate.ref[...] = jnp.broadcast_to(1.0 / (1.0 + jnp.exp(-logit)), gate.ref.shape)
        gate.go()
        line = x_ref[width : width + 8, 0:width].astype(F32)
        fill_row_bias(bias, line, line, -1.0)
        store_spans(span, scalars[0], scalars[0], tiles)

        def work(n, j, pair):
            cols = pl.ds(pl.multiple_of(pair * PAIR, PAIR), PAIR)
            rows = pl.ds(pl.multiple_of(j * TILE, TILE), TILE)
            some = pl.ds(pl.multiple_of(span[j] * TILE, TILE), n * TILE)
            value, total, top = attend_rows(q.ref[rows, cols], k.ref[some, cols], v.ref[some, cols], bias[rows, some])
            acc.ref[rows, cols] = value / total
            lse.ref[rows, cols] = top + jnp.log(total)

        over_tiles(span, tiles, pairs, 1, work)

    low = shape_of((width, depth), BF16)
    total = shape_of((width, depth), F32)
    return streamed(
        "near_attention", kernel, [spans], [query_bias, value_bias, scale, offset, router],
        [full(routed)] + [columns(qkv_weight, i * depth, depth) for i in range(3)],
        [low, low, low, low, shape_of((width, TILE), F32), total, total],
        scratch=[VMEM((width, width), F32), SMEM((2 * tiles,), I32)],
    )


def three_parts(value):
    high = value.astype(BF16)
    rest = value - high.astype(F32)
    middle_part = rest.astype(BF16)
    return high, middle_part, (rest - middle_part.astype(F32)).astype(BF16)


def far_and_feed(far, spans, core, routed, qkv_weight, query_bias, value_bias, scale, offset, count,
                 queries, acc, near_lse, out_weight, out_bias, scale2, offset2, gate, grad_routed,
                 up_weight, up_bias, down_weight):
    depth = routed.shape[1]
    width = routed.shape[0] - 16
    tiles = width // TILE
    pairs = depth // PAIR
    lots = pairs * tiles
    extra = -(-lots // 16) * 16
    step = 256
    steps = depth // step
    blocks = up_weight.shape[1] // depth

    def block_of(at, scalars):
        own = scalars[1][0]
        return at // 2 * 2 + (1 - own if at % 2 == 0 else own)

    def up_part(at):
        def piece(i):
            def source(ref, scalars):
                start = pl.multiple_of(block_of(at, scalars) * depth + i * step, step)
                return ref.at[:, pl.ds(start, step)]
            return source, lambda ref: ref.at[:, i * step : (i + 1) * step]
        return (up_weight, [piece(i) for i in range(steps)], (depth, depth))

    def down_part(at):
        def part(ref, scalars):
            return ref.at[pl.ds(pl.multiple_of(block_of(at, scalars) * depth, step), depth)]
        return (down_weight, part, (depth, depth))

    def kernel(scalars, small, fetches, sends, scratch, scalar_outs):
        qb, vb, scale_ref, offset_ref, ob, scale2_ref, offset2_ref, ub = small
        far_in, weight_q, weight_k, weight_v, x_in, q_in, acc_in, lse_in, gate_in, grad_in, ow = fetches[:11]
        ups, downs = fetches[11::2], fetches[12::2]
        fq, fk, fv, pack, lse, branch_out, lines = sends[:7]
        acts = sends[7 : 7 + blocks]
        feed_out, gout, mixed_out, low_out, delta_out, vec_out = sends[7 + blocks :]
        bias, span, attended, back = scratch
        far_ref = far_in()
        far_line = far_ref[width : width + 8, 0:width].astype(F32)
        tile_spans(far_line[0:1], count, scalar_outs[0])
        unit, _ = normalize(far_ref[0:width].astype(F32))
        low = (unit * wide(scale_ref) + wide(offset_ref)).astype(BF16)
        project(low, (weight_q, weight_k, weight_v), wide(qb), wide(vb), fq.ref, fk.ref, fv.ref, (fk, fq, fv))
        x_ref = x_in()
        line = x_ref[width : width + 8, 0:width].astype(F32)
        fill_row_bias(bias, far_line, line, -2.0)
        lines.ref[0] = line
        lines.ref[1] = jnp.where(far_line < 0.0, -2.0, far_line)
        lines.go()
        grad_delta = gate_in()[:, 0:1] * wide(grad_in())
        pack.ref[1] = grad_delta.astype(BF16)
        pack.go(1)
        vec_out.ref[...] = jnp.zeros_like(vec_out.ref)
        vec_out.ref[4:5, :] = jnp.sum(wide(pack.ref.at[1]), axis=0, keepdims=True)
        store_spans(span, scalar_outs[0], scalars[0], tiles)
        q_ref, acc_ref, lse_ref = q_in(), acc_in(), lse_in()

        def work(n, j, pair):
            cols = pl.ds(pl.multiple_of(pair * PAIR, PAIR), PAIR)
            rows = pl.ds(pl.multiple_of(j * TILE, TILE), TILE)
            part, log_total = acc_ref[rows, cols], lse_ref[rows, cols]
            if n > 0:
                some = pl.ds(pl.multiple_of(span[j] * TILE, TILE), n * TILE)
                value, total, top = attend_rows(
                    q_ref[rows, cols], fk.ref[some, cols], fv.ref[some, cols], bias[rows, some]
                )
                most = jnp.maximum(top, log_total)
                far_part = jnp.exp(top - most)
                near_part = jnp.exp(log_total - most)
                total = far_part * total + near_part
                part = (part * near_part + value * far_part) / total
                log_total = most + jnp.log(total)
            attended[rows, cols] = part.astype(BF16)
            turned = log_total.T
            lse.ref[pl.ds(pair * tiles + j, 1)] = jnp.concatenate([turned[0:1], turned[HD : HD + 1]], axis=1)

        over_tiles(span, tiles, pairs, 0, work)
        pack.ref[2] = attended[...]
        pack.go(2)
        branch = nn(attended[...], ow()[...]) + wide(ob)
        branch_out.ref[...] = branch
        branch_out.go()
        unit, _ = normalize(x_ref[0:width].astype(F32) + branch)
        pack.ref[0] = (unit * wide(scale2_ref) + wide(offset2_ref)).astype(BF16)
        pack.go(0)

        second, gfl = pack.ref.at[0], pack.ref.at[1]
        for at, out in enumerate(acts):
            block = block_of(at, scalars)
            for i in range(steps):
                cols = slice(i * step, (i + 1) * step)
                start = pl.multiple_of(block * depth + i * step, step)
                pre = nn(second[...], ups[at](i)[:, cols])
                pre = pre + ub[:, pl.ds(start, step)].astype(F32)
                squared = pre * pre
                inner = pre * (0.7978845608028654 + 0.035677408136300125 * squared)
                tanh = jnp.tanh(inner)
                half = 0.5 + 0.5 * tanh
                out.ref[0, :, cols] = (pre * half).astype(BF16)
                slope = half + pre * (0.5 * (1.0 - tanh * tanh)) * (
                    0.7978845608028654 + 0.10703222440890037 * squared
                )
                grad = (nt(gfl[...], downs[at]()[cols, :]) * slope).astype(BF16)
                out.ref[1, :, cols] = grad
                vec_out.ref[pl.ds(block, 1), cols] = jnp.sum(grad.astype(F32), axis=0, keepdims=True)
            out.go()
        for start in range(0, depth, step):
            cols = slice(start, start + step)
            value = nt(acts[0].ref[1], ups[0]()[cols, :])
            for at in range(1, blocks):
                value = value + nt(acts[at].ref[1], ups[at]()[cols, :])
            back[:, cols] = value

        unit, inverse = normalize(x_ref[0:width].astype(F32) + branch_out.ref[...])
        vec_out.ref[5:6, :] = jnp.sum(back[...] * unit, axis=0, keepdims=True)
        vec_out.ref[6:7, :] = jnp.sum(back[...], axis=0, keepdims=True)
        mixed = norm_back(back[...], wide(scale2_ref), unit, inverse)
        mixed_out.ref[...] = mixed
        mixed_out.go()
        low = (gate_in()[:, 0:1] * wide(grad_in()) + mixed).astype(BF16)
        low_out.ref[...] = low
        low_out.go()
        vec_out.ref[7:8, :] = jnp.sum(low.astype(F32), axis=0, keepdims=True)
        value = nt(low, ow()[...]).astype(BF16)
        gout.ref[0:width] = value
        product = value.astype(F32) * wide(attended)
        high = product.astype(BF16)
        rest = (product - high.astype(F32)).astype(BF16)
        member = lax.broadcasted_iota(I32, (16, depth), 1) // HD
        ones = jnp.where(member == lax.broadcasted_iota(I32, (16, depth), 0), 1.0, 0.0).astype(BF16)
        delta = nt(ones, high) + nt(ones, rest)
        for head in range(H):
            for j in range(tiles):
                lot = (head // 2) * tiles + j
                at = (head % 2) * TILE
                delta_out.ref[lot : lot + 1, at : at + TILE] = delta[head : head + 1, j * TILE : (j + 1) * TILE]
        gout.ref[width:] = jnp.zeros_like(gout.ref[width:])
        for i, part in enumerate(three_parts(lse.ref[...])):
            gout.ref[width : width + lots, i * 2 * TILE : (i + 1) * 2 * TILE] = part
        for i, part in enumerate(three_parts(delta_out.ref[...])):
            gout.ref[width + extra : width + extra + lots, i * 2 * TILE : (i + 1) * 2 * TILE] = part
        gout.go()
        for start in range(0, depth, step):
            cols = slice(start, start + step)
            value = nn(acts[0].ref[0], downs[0]()[:, cols])
            for at in range(1, blocks):
                value = value + nn(acts[at].ref[0], downs[at]()[:, cols])
            feed_out.ref[:, cols] = value

    low = shape_of((width, depth), BF16)
    total = shape_of((width, depth), F32)
    stats = shape_of((lots, 2 * TILE), F32)
    return streamed(
        "far_and_feed", kernel, [spans, core],
        [query_bias, value_bias, scale, offset, out_bias, scale2, offset2, up_bias],
        [full(far)] + [columns(qkv_weight, i * depth, depth) for i in range(3)]
        + [full(a) for a in (routed, queries, acc, near_lse, gate, grad_routed, out_weight)]
        + [part(at) for at in range(blocks) for part in (up_part, down_part)],
        [low, low, low, shape_of((3, width, depth), BF16), stats, total, shape_of((2, 8, width), F32)]
        + [shape_of((2, width, depth), BF16)] * blocks
        + [total, shape_of((width + 2 * extra, depth), BF16), total, low, stats, shape_of((16, depth), F32)],
        scratch=[
            VMEM((width, width), F32), SMEM((2 * tiles,), I32), VMEM((width, depth), BF16),
            VMEM((width, depth), F32),
        ],
        scalar_outs=[shape_of((2 * tiles,), I32)],
        split=(3,),
    )


def feed_grads(got, bit, pack, far_pack, own):
    width, depth = pack.shape[1:]
    step = 256

    def kernel(scalars, small, fetches, sends, scratch, scalar_outs):
        second, own_grad, far_second, got_grad, gfl, far_gfl, own_hidden, got_hidden = fetches
        send, keep = sends
        bit = scalars[0][0]

        def up(ref):
            for at in range(0, depth, step):
                cols = slice(at, at + step)
                value = tn(second()[...], own_grad()[:, cols]) + tn(far_second()[...], got_grad()[:, cols])
                ref[:, cols] = value.astype(BF16)

        def down(ref):
            for at in range(0, depth, step):
                rows = slice(at, at + step)
                value = tn(own_hidden()[:, rows], gfl()[...]) + tn(got_hidden()[:, rows], far_gfl()[...])
                ref[rows, :] = value.astype(BF16)

        up(scratch[0].at[bit])
        down(scratch[0].at[1 - bit])
        for send_out, side in ((keep, 0), (send, 1)):
            send_out.copies = [pltpu.make_async_copy(scratch[0].at[side], send_out.target, send_out.sem.at[0])]
            send_out.go()

    half = shape_of((depth, depth), BF16)
    return streamed(
        "feed_grads", kernel, [jnp.reshape(bit, (1,)).astype(I32)], [],
        [row_of(pack, 0), row_of(own, 1), row_of(far_pack, 0), row_of(got, 1),
         row_of(pack, 1), row_of(far_pack, 1), row_of(own, 0), row_of(got, 0)],
        [half, half],
        scratch=[VMEM((2, depth, depth), BF16)],
    )


def own_back(part, parts, q, k, v, gout, lse, delta, fk, fv, lines, spans, far_spans):
    width, depth = q.shape
    tiles = width // TILE
    some = depth // parts
    pairs = some // PAIR
    base = part * pairs * tiles

    def kernel(scalars, small, fetches, sends, scratch, scalar_outs):
        q_in, k_in, v_in, g_in, fk_in, fv_in, lse_in, delta_in, lines_in = fetches
        dq, dk, dv = sends
        bias, far_bias, turned, far_turned, span, far_span, dq_turned = scratch
        lines_ref = lines_in()
        fill_bias(bias, lines_ref[0], lines_ref[0], -1.0)
        fill_bias(far_bias, lines_ref[1], lines_ref[0], -2.0)
        store_spans(span, scalars[0], scalars[0], tiles)
        store_spans(far_span, scalars[1], scalars[0], tiles)
        k_ref, fk_ref, q_ref, g_ref, v_ref, fv_ref = k_in(), fk_in(), q_in(), g_in(), v_in(), fv_in()
        lse_ref, delta_ref = lse_in(), delta_in()
        turned[...] = k_ref[...].T
        far_turned[...] = fk_ref[...].T
        dk.ref[...] = jnp.zeros_like(dk.ref)
        dv.ref[...] = jnp.zeros_like(dv.ref)

        def pieces(j, pair):
            cols = pl.ds(pl.multiple_of(pair * PAIR, PAIR), PAIR)
            rows = pl.ds(pl.multiple_of(j * TILE, TILE), TILE)
            query = stacked_heads(q_ref[rows, cols]) * SCALE
            grad = stacked_heads(g_ref[rows, cols])
            one = pl.ds(base + pair * tiles + j, 1)
            return cols, rows, query, grad, lse_ref[one], delta_ref[one]

        def local(n, j, pair):
            cols, rows, query, grad, top, delta = pieces(j, pair)
            near = pl.ds(pl.multiple_of(span[j] * TILE, TILE), n * TILE)
            weights = jnp.exp(nt(k_ref[near, cols], query) + twice(bias[near, rows]) - top)
            dscore = (weights * (nt(v_ref[near, cols], grad) - delta)).astype(BF16)
            dk.ref[near, cols] += nn(dscore, query)
            dv.ref[near, cols] += nn(weights.astype(BF16), grad)
            dq_turned[cols, rows] = own_blocks(nn(turned[cols, near], dscore))

        def remote(n, j, pair):
            cols, rows, query, grad, top, delta = pieces(j, pair)
            far = pl.ds(pl.multiple_of(far_span[j] * TILE, TILE), n * TILE)
            weights = jnp.exp(nt(fk_ref[far, cols], query) + twice(far_bias[far, rows]) - top)
            dscore = (weights * (nt(fv_ref[far, cols], grad) - delta)).astype(BF16)
            dq_turned[cols, rows] += own_blocks(nn(far_turned[cols, far], dscore))

        over_tiles(span, tiles, pairs, 1, local)
        over_tiles(far_span, tiles, pairs, 1, remote)
        dq.ref[...] = (dq_turned[...].T * SCALE).astype(BF16)

    total = shape_of((width, some), F32)
    return streamed(
        "own_back", kernel, [spans, far_spans], [],
        [columns(a, part * some, some) for a in (q, k, v)]
        + [(gout, lambda ref, scalars: ref.at[0:width, part * some : (part + 1) * some], (width, some))]
        + [columns(a, part * some, some) for a in (fk, fv)]
        + [full(lse), full(delta), full(lines)],
        [shape_of((width, some), BF16), total, total],
        scratch=[
            VMEM((width, width), F32), VMEM((width, width), F32),
            VMEM((some, width), BF16), VMEM((some, width), BF16),
            SMEM((2 * tiles,), I32), SMEM((2 * tiles,), I32), VMEM((some, width), F32),
        ],
    )


def other_back(fgout, core, spans, far_spans, fq, k, v, lines, grads, low, vec):
    width, depth = k.shape
    tiles = width // TILE
    parts = len(grads)
    some = depth // parts
    pairs = some // PAIR
    lots = depth // PAIR * tiles
    extra = -(-lots // 16) * 16
    half = depth // 2

    def kernel(scalars, small, fetches, sends, scratch, scalar_outs):
        g_in, fq_in, k_in, v_in, lines_in, low_in, vec_in = fetches[:7]
        pieces = fetches[7:]
        halves = sends[:4]
        dq, dk, dv, vec_out = sends[4:]
        bias, span, stat, dk_sum, dv_sum = scratch
        lines_ref = lines_in()
        fill_bias(bias, lines_ref[0], lines_ref[1], -1.0)
        store_spans(span, scalars[1], scalars[2], tiles)
        g_ref = g_in()
        for i in range(2):
            block = g_ref[width + i * extra : width + i * extra + lots]
            stat[i] = (
                block[:, 0 : 2 * TILE].astype(F32)
                + block[:, 2 * TILE : 4 * TILE].astype(F32)
                + block[:, 4 * TILE : 6 * TILE].astype(F32)
            )
        fq_ref, k_ref, v_ref = fq_in(), k_in(), v_in()
        for part in range(parts):
            place = slice(part * some, (part + 1) * some)
            dq.ref[:, place] = pieces[3 * part]()[...]
            dk_sum[:, place] = pieces[3 * part + 1]()[...]
            dv_sum[:, place] = pieces[3 * part + 2]()[...]

        def work(n, j, pair):
            cols = pl.ds(pl.multiple_of(pair * PAIR, PAIR), PAIR)
            rows = pl.ds(pl.multiple_of(j * TILE, TILE), TILE)
            one = pl.ds(pair * tiles + j, 1)
            query = stacked_heads(fq_ref[rows, cols]) * SCALE
            grad = stacked_heads(g_ref[rows, cols])
            near = pl.ds(pl.multiple_of(span[j] * TILE, TILE), n * TILE)
            scores = nt(k_ref[near, cols], query) + twice(bias[near, rows])
            weights = jnp.exp(scores - stat[0, one])
            dscore = (weights * (nt(v_ref[near, cols], grad) - stat[1, one])).astype(BF16)
            dk_sum[near, cols] += nn(dscore, query)
            dv_sum[near, cols] += nn(weights.astype(BF16), grad)

        over_tiles(span, tiles, depth // PAIR, 1, work)
        dk.ref[...] = dk_sum[...].astype(BF16)
        dv.ref[...] = dv_sum[...].astype(BF16)
        low_ref = low_in()
        cols = pl.ds(pl.multiple_of((1 - scalars[0][0]) * half, TILE), half)
        for out, ref in zip(halves, (dq.ref, dk.ref, dv.ref, low_ref)):
            out.ref[...] = ref[:, cols]
            out.go()
        vec_out.ref[...] = vec_in()[...]
        vec_out.ref[8:9, :] = jnp.sum(wide(dq.ref), axis=0, keepdims=True)
        vec_out.ref[9:10, :] = jnp.sum(wide(dv.ref), axis=0, keepdims=True)

    flat = [piece for grad in grads for piece in grad]
    low_shape = shape_of((width, depth), BF16)
    return streamed(
        "other_back", kernel, [core, spans, far_spans], [],
        [full(a) for a in (fgout, fq, k, v, lines, low, vec)] + [full(a) for a in flat],
        [shape_of((width, half), BF16)] * 4 + [low_shape] * 3 + [shape_of((16, depth), F32)],
        scratch=[
            VMEM((width, width), F32), SMEM((2 * tiles,), I32), VMEM((2, lots, 2 * TILE), F32),
            VMEM((width, depth), F32), VMEM((width, depth), F32),
        ],
    )


def last_grads(core, bit, normed, far_normed, pack, far_pack, dq, dk, dv, low, got):
    width, depth = dq.shape
    half = depth // 2

    def kernel(scalars, small, fetches, sends, scratch, scalar_outs):
        left, far_left, att, far_att, dq_in, dk_in, dv_in, low_in = fetches[:8]
        gots = fetches[8:]
        send, keep = sends
        turned = scratch[0]
        cols = pl.ds(pl.multiple_of(scalars[0][0] * half, TILE), half)
        for i, ref in enumerate((left, far_left, att, far_att)):
            turned[i // 2, :, (i % 2) * width : (i % 2 + 1) * width] = ref()[...].T
        for out, which in ((send, 1 - scalars[1][0]), (keep, scalars[1][0])):
            rows = pl.ds(pl.multiple_of(which * half, TILE), half)
            for i, part in enumerate((dq_in, dk_in, dv_in, low_in)):
                place = slice(i * half, (i + 1) * half)
                side = 0 if i < 3 else 1
                value = nn(turned[side, rows, 0:width], part()[:, cols])
                value = value + nn(turned[side, rows, width : 2 * width], gots[i]()[...])
                out.ref[:, place] = value.astype(BF16)
            out.go()

    shape = shape_of((half, 2 * depth), BF16)
    return streamed(
        "last_grads", kernel, [core, jnp.reshape(bit, (1,)).astype(I32)], [],
        [full(normed), full(far_normed), row_of(pack, 2), row_of(far_pack, 2)]
        + [full(a) for a in (dq, dk, dv, low) + tuple(got)],
        [shape, shape],
        scratch=[VMEM((2, depth, 2 * width), BF16)],
    )


def scatter(hot_ref, rows, slots_ref):
    hot = hot_ref[...]
    taken = jnp.max(hot.astype(F32), axis=-1, keepdims=True) > 0.0
    return jnp.where(taken, nn(hot, rows).astype(BF16), slots_ref[...])


def token_out(hot, tokens, routed, gate, branch, feed, down_bias, grad_routed, router, mixed, vec):
    slots, depth = tokens.shape
    width = branch.shape[0]

    def kernel(scalars, small, fetches, sends, scratch, scalar_outs):
        branch_in, feed_in, x_in, gate_in, grad_in, mixed_in, vec_in, hot_in, tok_in = fetches
        out, base, vec_out = sends
        total = branch_in()[...] + feed_in()[...] + wide(small[0])
        x = wide(x_in())
        gate = gate_in()[:, 0:1]
        grad = wide(grad_in())
        logit = jnp.sum(grad * total, axis=-1, keepdims=True) * gate * (1.0 - gate)
        base.ref[...] = grad + mixed_in()[...] + logit * wide(small[1])
        base.go()
        vec_out.ref[...] = vec_in()[...]
        vec_out.ref[12:13, :] = jnp.sum(x * logit, axis=0, keepdims=True)
        out.ref[...] = scatter(hot_in(), (x + gate * total).astype(BF16), tok_in())

    return streamed(
        "token_out", kernel, [], [down_bias, router],
        [full(branch), full(feed), head_rows(routed, width)]
        + [full(a) for a in (gate, grad_routed, mixed, vec, hot, tokens)],
        [shape_of((slots, depth), BF16), shape_of((width, depth), F32), shape_of((16, depth), F32)],
    )


def token_grad(dq, dk, dv, hot, cotangent, routed, base, scale, qkv_weight, vec):
    slots, depth = cotangent.shape
    width = base.shape[0]

    def kernel(scalars, small, fetches, sends, scratch, scalar_outs):
        dq_in, weight_q, dk_in, weight_k, dv_in, weight_v, x_in, base_in, vec_in, hot_in, cot_in = fetches
        out, vec_out = sends
        back = nt(dq_in()[...], weight_q()[...]) + nt(dk_in()[...], weight_k()[...])
        back = back + nt(dv_in()[...], weight_v()[...])
        unit, inverse = normalize(wide(x_in()))
        vec_out.ref[...] = vec_in()[...]
        vec_out.ref[10:11, :] = jnp.sum(back * unit, axis=0, keepdims=True)
        vec_out.ref[11:12, :] = jnp.sum(back, axis=0, keepdims=True)
        vec_out.go()
        rows = (base_in()[...] + norm_back(back, wide(small[0]), unit, inverse)).astype(BF16)
        out.ref[...] = scatter(hot_in(), rows, cot_in())

    return streamed(
        "token_grad", kernel, [], [scale],
        [
            full(dq), columns(qkv_weight, 0, depth), full(dk), columns(qkv_weight, depth, depth),
            full(dv), columns(qkv_weight, 2 * depth, depth), head_rows(routed, width),
            full(base), full(vec), full(hot), full(cotangent),
        ],
        [shape_of((slots, depth), BF16), shape_of((16, depth), F32)],
    )


AXES = ("rows", "seq")
SHIFT = {"c": 0, "x": 1, "z1": 2, "z2": 3}
BLOCK = 16
XY_FIRST = (("x", "y"), ("y", "x"), ("z1", "z1"), ("z2", "z2"))
YX_FIRST = (("y", "x"), ("x", "y"), ("z1", "z1"), ("z2", "z2"))


def swap(block, axes):
    route = []
    for row in range(lax.axis_size("rows")):
        axis = axes[row & 1]
        for seq in range(2):
            if axis == "y":
                other = row * 2 + (seq ^ 1)
            else:
                other = (row ^ (1 << SHIFT[axis])) * 2 + seq
            route.append((row * 2 + seq, other))
    return lax.ppermute(block, AXES, route)


def own_bit(axis):
    if axis == "y":
        return lax.axis_index("seq")
    return (lax.axis_index("rows") >> SHIFT[axis]) & 1


def stage_bit(axes, core):
    if axes[0] == axes[1]:
        return own_bit(axes[0])
    return jnp.where(core == 0, own_bit(axes[0]), own_bit(axes[1]))


def half_of(block, which):
    half = block.shape[0] // 2
    return lax.dynamic_slice_in_dim(block, which * half, half, 0)


def add_low(left, right):
    return (left.astype(F32) + right.astype(F32)).astype(BF16)


def after(value, *others):
    return lax.optimization_barrier((value, *others))[0]


def over_blocks(total):
    extra = BLOCK
    size = lax.axis_size("rows")
    while extra < size:
        route = [(i * 2 + j, (i ^ extra) * 2 + j) for i in range(size) for j in range(2)]
        got = lax.ppermute(total, AXES, route)
        total = (total.astype(F32) + got.astype(F32)).astype(total.dtype)
        extra *= 2
    return total


class Order:
    def __init__(self):
        self.tail = None

    def run(self, call, lead, *args):
        if self.tail is not None:
            leaves, tree = jax.tree.flatten(lead)
            leaves = lax.optimization_barrier(tuple(leaves) + (self.tail,))[:-1]
            lead = jax.tree.unflatten(tree, leaves)
        result = call(lead, *args)
        self.tail = jax.tree.leaves(result)[-1]
        return result


def two_parts(block):
    high = block.astype(BF16)
    return jnp.concatenate([high, (block - high.astype(F32)).astype(BF16)], axis=1)


def from_parts(block):
    half = block.shape[1] // 2
    return block[:, :half].astype(F32) + block[:, half:].astype(F32)


class Sum:
    def __init__(self, order, send, keep, stages):
        self.order, self.keep, self.stages, self.at = order, keep, stages, 1
        self.small, self.riding = None, False
        self.got = swap(send, stages[0])

    @classmethod
    def joined(cls, order, parts):
        new = cls.__new__(cls)
        new.order, new.stages, new.at = order, parts[0].stages, parts[0].at
        new.small, new.riding = None, False
        new.keep = tuple(part.keep for part in parts)
        new.got = tuple(part.got for part in parts)
        return new

    def take(self):
        if not self.riding:
            return self.got
        rows = self.got.shape[0] - self.small.shape[0]
        self.small = self.small + from_parts(self.got[rows:])
        self.riding = False
        return self.got[:rows]

    def post(self, send, axes, ride):
        if ride and self.small is not None:
            send = jnp.concatenate([send, two_parts(self.small)], axis=0)
            self.riding = True
        return swap(send, axes)

    def reduce(self):
        if self.at == len(self.stages):
            self.keep = over_blocks(self.order.run(add_low, self.take(), self.keep))
            self.got = swap(self.keep, self.stages[-1])
            return
        axes = self.stages[self.at]
        bit = stage_bit(axes, own_bit("c"))

        def add(got, keep, which):
            if isinstance(got, tuple):
                return jnp.concatenate([add(g, k, which) for g, k in zip(got, keep)], axis=1)
            return add_low(half_of(keep, which), half_of(got, which))

        arrived = self.take()
        send = self.order.run(lambda got, keep: add(got, keep, 1 - bit), arrived, self.keep)
        got = self.post(send, axes, True)
        self.keep = self.order.run(lambda got, keep: add(got, keep, bit), arrived, self.keep)
        self.got = got
        self.at += 1

    def gather(self):
        self.at -= 1
        self.keep = self.order.run(lambda got, keep: jnp.concatenate([keep, got]), self.got, self.keep)
        self.got = self.post(self.keep, self.stages[self.at - 1], self.at == 1)
        if self.at == 1:
            self.blocks = [(self.keep, 0, 0), (swap(self.keep, ("c", "c")), 1, 0)]

    def rest(self):
        self.got = self.order.run(lambda got: got, self.got)
        self.blocks += [(self.got, 0, 1), (swap(self.got, ("c", "c")), 1, 1)]
        self.take()


def shard_of(stages, core):
    index = jnp.int32(0)
    for axes in stages:
        index = index * 2 + stage_bit(axes, core)
    return index


SHARDS = 8


def place_kernel(kind, rows, count, info_ref, *rest):
    blocks = rest[:count]
    first_ref, second_ref, low, full, sems = rest[-5:]
    depth = blocks[0].shape[1]
    lots = [info_ref[3 * i + 2] for i in range(count)]
    tops = [info_ref[3 * i + 1] for i in range(count)]

    def pull(i, s):
        src = pl.ds(pl.multiple_of((s ^ info_ref[3 * i]) * rows, rows), rows)
        return pltpu.make_async_copy(blocks[i].at[src], low.at[i, pl.ds(s * rows, rows)], sems.at[0, i, s])

    def push(i, s, top):
        src = full.at[i, pl.ds(s * rows, rows)]
        lot = lots[i]
        if kind == "feed":
            copies = []
            size = depth // 2
            for t in range(2):
                at = (lot + 2 * t) * size
                if top == 0:
                    to = first_ref.at[pl.ds(s * rows, rows), pl.ds(pl.multiple_of(at, 128), size)]
                else:
                    to = second_ref.at[pl.ds(pl.multiple_of(at + s * rows, rows), rows)]
                copies.append(pltpu.make_async_copy(src.at[:, pl.ds(t * size, size)], to, sems.at[1 + t, i, s]))
            return copies
        part = depth // 4
        row = pl.ds(pl.multiple_of((tops[i] * SHARDS + s) * rows, rows), rows)
        copies = []
        for t in range(4):
            target = first_ref if t < 3 else second_ref
            at = (2 * t + lot) * part if t < 3 else lot * part
            copies.append(
                pltpu.make_async_copy(
                    src.at[:, pl.ds(t * part, part)],
                    target.at[row, pl.ds(pl.multiple_of(at, 128), part)],
                    sems.at[1 + t, i, s],
                )
            )
        return copies

    def start(i, s):
        if kind != "feed":
            for copy in push(i, s, 0):
                copy.start()
            return
        for top in range(2):

            @pl.when(tops[i] == top)
            def _(top=top):
                for copy in push(i, s, top):
                    copy.start()

    for i in range(count):
        for s in range(SHARDS):
            pull(i, s).start()
    for i in range(count):
        for s in range(SHARDS):
            pull(i, s).wait()
            dst = slice(s * rows, (s + 1) * rows)
            full[i, dst] = low[i, dst].astype(F32)
            start(i, s)
    for i in range(count):
        for s in range(SHARDS):
            for copy in push(i, s, 0):
                copy.wait()


def place(kind, rows, blocks, info, targets, shapes):
    hbm = pl.BlockSpec(memory_space=pltpu.HBM)
    targets = targets or ()
    count = len(blocks)
    return pl.pallas_call(
        functools.partial(place_kernel, kind, rows, count),
        out_shape=tuple(jax.ShapeDtypeStruct(s, F32) for s in shapes),
        in_specs=[pl.BlockSpec(memory_space=pltpu.SMEM)] + [hbm] * (count + len(targets)),
        out_specs=(hbm, hbm),
        scratch_shapes=[
            VMEM((count, rows * SHARDS, blocks[0].shape[1]), BF16),
            VMEM((count, rows * SHARDS, blocks[0].shape[1]), F32),
            pltpu.SemaphoreType.DMA((5, count, SHARDS)),
        ],
        input_output_aliases={1 + count: 0, 2 + count: 1} if targets else {},
        compiler_params=pltpu.CompilerParams(vmem_limit_bytes=62 << 20),
        cost_estimate=pl.CostEstimate(flops=int(LENGTH["place"] * RATE), bytes_accessed=0, transcendentals=0),
        name="place",
    )(info, *blocks, *targets)


def body(
    tokens,
    cotangent,
    segment_ids,
    routing,
    qkv_weight,
    query_bias,
    value_bias,
    out_weight,
    out_bias,
    first_scale,
    first_offset,
    second_scale,
    second_offset,
    up_weight,
    up_bias,
    down_weight,
    down_bias,
    router_weight,
):
    row_count, slots, depth = tokens.shape
    hidden = up_weight.shape[1]
    count = slots // 2
    width = -(-count // 128) * 128
    core = own_bit("c")
    seat = jnp.reshape(core, (1,)).astype(jnp.int32)
    pos = jnp.reshape(lax.axis_index("seq"), (1,)).astype(jnp.int32)
    tokens = tokens.reshape(slots, depth)
    cotangent = cotangent.reshape(slots, depth)
    routes = routing.reshape(2, 1, slots)
    segs = segment_ids.reshape(2, 1, slots)
    qb, vb, ob, s1, o1, s2, o2, db, rw = (
        v.reshape(1, depth)
        for v in (query_bias, value_bias, out_bias, first_scale, first_offset, second_scale,
                  second_offset, down_bias, router_weight)
    )
    ub = up_bias.reshape(1, hidden)

    order = Order()
    routed, grad_routed, hot, spans = pick_rows(pos, routes, segs, tokens, cotangent, count, width)
    far = swap(routed, ("y", "y"))
    q, k, v, normed, gate, acc, near_lse = near_attention(spans, routed, qkv_weight, qb, vb, s1, o1, rw)
    far_normed = swap(normed, ("c", "c"))
    fq, fk, fv, pack, lse, branch, lines, *rest, far_spans = order.run(
        far_and_feed, far, spans, seat, routed, qkv_weight, qb, vb, s1, o1, count, q, acc, near_lse,
        out_weight, ob, s2, o2, gate, grad_routed, up_weight, ub, down_weight
    )
    *acts, feed_sum, gout, mixed, low, delta, vec = rest
    fgout = swap(gout, ("y", "y"))
    far_pack = swap(pack, ("c", "c"))
    sends = [swap(send, ("c", "c")) for send in acts[0::2]]

    plans = (XY_FIRST, XY_FIRST, YX_FIRST)
    first_bits = [stage_bit(plan[0], core) for plan in plans]

    def feed_sums(pair):
        send, keep = order.run(feed_grads, sends[pair], first_bits[pair], pack, far_pack, acts[2 * pair + 1])
        return Sum(order, send, keep, plans[pair])

    def own_part(part):
        return order.run(
            lambda q: own_back(part, 2, q, k, v, gout, lse, delta, fk, fv, lines, spans, far_spans), q
        )

    grads = [own_part(0)]
    one = feed_sums(0)
    fgout = order.run(lambda got: got, fgout)
    two = feed_sums(1)
    grads.append(own_part(1))
    one.got = order.run(lambda got: got, one.got)
    *last_sends, dq, dk, dv, vec = order.run(
        other_back, fgout, seat, spans, far_spans, fq, k, v, lines, grads, low, vec
    )
    gots = [swap(send, ("c", "c")) for send in last_sends]
    both = Sum.joined(order, (one, two))
    both.reduce()
    send, keep = order.run(
        lambda got, *rest: last_grads(
            seat, first_bits[2], normed, far_normed, pack, far_pack, dq, dk, dv, low, (got,) + rest
        ), *gots
    )
    three = Sum(order, send, keep, plans[2])
    both.reduce()
    out_tokens, base, vec = order.run(
        token_out, hot, tokens, routed, gate, branch, feed_sum, db, grad_routed, rw, mixed, vec
    )
    grad_tokens, vec = order.run(token_grad, dq, dk, dv, hot, cotangent, routed, base, s1, qkv_weight, vec)
    three.small = vec

    kinds = {
        "feed": ((depth, hidden), (hidden, depth)),
        "last": ((depth, 3 * depth), (depth, depth)),
    }
    targets = {"feed": None, "last": None}
    rows = {"feed": depth // 8, "last": depth // 16}

    def put(kind, some):
        blocks, info = [], []
        for block, other, half in some:
            owner = core if other == 0 else 1 - core
            own = shard_of(plans[0] if kind == "feed" else plans[2], owner)
            blocks.append(block)
            info += [own % 8, own // 8 ^ half, owner]
        info = jnp.stack(info).astype(jnp.int32)
        targets[kind] = order.run(
            lambda block, *rest: place(kind, rows[kind], rest + (block,), info, targets[kind], kinds[kind]),
            blocks[-1], *blocks[:-1]
        )

    both.reduce()
    three.reduce()
    both.reduce()
    both.gather()
    both.gather()
    three.reduce()
    three.reduce()
    both.gather()
    three.reduce()
    three.gather()
    three.gather()
    put("feed", both.blocks[:2])
    both.rest()
    three.gather()
    put("last", three.blocks)
    put("feed", both.blocks[2:])
    three.rest()
    vec = three.small + swap(three.small, ("c", "c"))
    put("last", three.blocks[2:3])
    put("last", three.blocks[3:])
    vec = over_blocks(vec)
    grad_up, grad_down = targets["feed"]
    grad_qkv, grad_out = targets["last"]
    return (
        out_tokens.reshape(row_count, slots, depth),
        grad_tokens.reshape(row_count, slots, depth),
        grad_qkv,
        vec[8],
        vec[9],
        grad_out,
        vec[7],
        vec[10],
        vec[11],
        vec[5],
        vec[6],
        grad_up,
        vec[0:4].reshape(hidden),
        grad_down,
        vec[4],
        vec[12],
    )


def solution(mesh):
    split = P("rows", "seq", None)
    return jax.shard_map(
        body,
        mesh=mesh,
        in_specs=(split, split, P("rows", None), P("rows", None)) + (P(),) * 14,
        out_specs=(split, split) + (P(),) * 14,
        check_vma=False,
    )
```

time: 366 us -> 313 us (0.86)
  Pallas kernels: 175 us -> 151 us
  starting transfers between devices: 43.7 us -> 25 us
  other arithmetic: 32 us -> 23.9 us
  local copies, waits for them, and re-layouts: 21.8 us -> 16.6 us
    pallas_call x14 -> x11, Pallas kernels: 147 us -> 128 us  [streamed(): pl.pallas_call(wrapped, out_shape=tuple(outs) + tuple(scalar_outs), in_sp...]
    ppermute x41 -> x32, starting transfers between devices: 43.7 us -> 25 us  [swap(): return lax.ppermute(block, AXES, route)]
    convert_element_type x18 -> x14, other arithmetic: 24 us -> 12.2 us  [add_low(): return (left.astype(F32) + right.astype(F32)).astype(BF16)]
    pallas_call x6 -> x5, Pallas kernels: 28.3 us -> 23.1 us  [place(): pl.pallas_call(functools.partial(place_kernel, kind, rows, count), out_sh...]
    unnamed x59 -> x47, local copies, waits for them, and re-layouts: 9.74 us -> 5.33 us
    ppermute x41 -> x32, waiting for transfers between devices: 85.5 us -> 88.8 us  [swap(): return lax.ppermute(block, AXES, route)]
  transfers between devices with their start and end apart: 41 -> 32, of which waited for: 12 -> 12; matrix products, arithmetic and copies ran while one was open for 12% -> 10% of each run, Pallas kernels for 39% -> 33%
where the time goes in v2:
time: 313 us; the launch traced here: 307 us
  Pallas kernels  151 us (48%)
  waiting for transfers between devices  88.8 us (28%)
  starting transfers between devices  25 us (8%)
  other arithmetic  23.9 us (8%)
  local copies, waits for them, and re-layouts  16.6 us (5%)
    pallas_call x11, Pallas kernels, streamed(): pl.pallas_call(wrapped, out_shape=tuple(outs) + tuple(scalar_outs), in_sp...  128 us
    ppermute x32, waiting for transfers between devices, swap(): return lax.ppermute(block, AXES, route)  88.8 us
    ppermute x32, starting transfers between devices, swap(): return lax.ppermute(block, AXES, route)  25 us
    pallas_call x5, Pallas kernels, place(): pl.pallas_call(functools.partial(place_kernel, kind, rows, count), out_sh...  23.1 us
    convert_element_type x14, other arithmetic, add_low(): return (left.astype(F32) + right.astype(F32)).astype(BF16)  12.2 us
  transfers between devices with their start and end apart: 32, of which 12 were waited for; matrix products, arithmetic and copies ran while one was open for 10% of the time, Pallas kernels for 33%

profile of v2, /device:TPU:0, one launch (start us, length us, event | category | flops | bytes accessed | tf_op | source)
XLA Modules:
  0.0 306.9 jit_solution(13329237374665268004)
XLA Ops:
  3.5 6.2 %pick_rows.1 = (bf16[528,768]{1,0:T(8,128)(2,1)}, bf16[512,768]{1,0:T(8,128)(2,1)}, bf16[944,512]{1,0:T(8,128)(2,1)}, s32[8]{0:T(128)}) custom-call(s32[1]{0:T(128)} %bitcast.refs_0_, s32[2,1,944]{2,1,0:T(1,128)} %reshape.99.refs_1_, s32[2,1,944]{2,1,0:T(1,128)} %reshape.100.refs_2_, bf16[944,768]{1,0:T(8,128)(2,1)} %bitcast.21, bf16[944,768]{1,0:T(8,128)(2,1)} %bitcast.23), custom_call_target="tpu_custom_call" | custom-call | flops 6899999744 | tf_op jit(solution)/shard_map/pick_rows/pallas_call | solution.py:134
  9.8 3.0 collective-permute-start
  18.1 14.0 %near_attention.1 = (bf16[512,768]{1,0:T(8,128)(2,1)}, bf16[512,768]{1,0:T(8,128)(2,1)}, bf16[512,768]{1,0:T(8,128)(2,1)}, bf16[512,768]{1,0:T(8,128)(2,1)}, f32...) custom-call(s32[8]{0:T(128)} %get-tuple-element.119.refs_0_.refs_1_, ...), custom_call_target="tpu_custom_call" | custom-call | flops 16099999744 | tf_op jit(solution)/shard_map/near_attention/pallas_call | solution.py:134
  33.0 39.4 %far_and_feed.1 = (bf16[512,768]{1,0:T(8,128)(2,1)}, bf16[512,768]{1,0:T(8,128)(2,1)}, bf16[512,768]{1,0:T(8,128)(2,1)}, bf16[3,512,768]{2,1,0:T(8,128)(2,1)}, f...) custom-call(s32[8]{0:T(128)} %get-tuple-element.119.refs_0_.refs_1_,, ...), custom_call_target="tpu_custom_call" | custom-call | flops 41400000512 | tf_op jit(solution)/shard_map/far_and_feed/pallas_call | solution.py:134
  73.1 10.9 %own_back.2 = (bf16[512,384]{1,0:T(8,128)(2,1)}, f32[512,384]{1,0:T(8,128)}, f32[512,384]{1,0:T(8,128)}) custom-call(s32[8]{0:T(128)} %get-tuple-element.119.refs_0_.refs_1_, s32[8]{0:T(128)} %get-tuple-element.129.refs_1_.refs_2_, bf16[512,768]{1,0:T(8,128)(2,1)} %get-tuple-element.151.refs_13_.refs_2_, ...), custom_call_target="tpu_custom_call" | custom-call | flops 5750000128 | tf_op jit(solution)/shard_map/own_back/pallas_call | solution.py:134
  84.0 7.0 %feed_grads.2 = (bf16[768,768]{1,0:T(8,128)(2,1)}, bf16[768,768]{1,0:T(8,128)(2,1)}) custom-call(s32[1]{0:T(128)} %bitcast.4.refs_0_, bf16[3,512,768]{2,1,0:T(8,128)(2,1)} %get-tuple-element.131.refs_1_.refs_4_, bf16[2,512,768]{2,1,0:T(8,128)(2,1)} %get-tuple-element.132.refs_2_, bf16[3,512,768]{2,1,0:T(8,128)(2,1)} %collective-permute-done.2.refs_3_.refs_5_, ...), custom_call_target="tpu_custom_call" | custom-call | flops 3449999872 | tf_op jit(solution)/shard_map/feed_grads/pallas_call | solution.py:134
  91.0 4.2 %collective-permute-done.1.refs_3_ = bf16[576,768]{1,0:T(8,128)(2,1)S(1)} collective-permute-done((bf16[576,768]{1,0:T(8,128)(2,1)}, bf16[576,768]{1,0:T(8,128)(2,1)S(1)}, u32[]{:S(2)}, u32[]{:S(2)}) %collective-permute-start.1) | collective-permute-done | bytes 884768 | tf_op jit(solution)/shard_map/ppermute | solution.py:834
  97.7 7.0 %feed_grads.3 = (bf16[768,768]{1,0:T(8,128)(2,1)}, bf16[768,768]{1,0:T(8,128)(2,1)}) custom-call(s32[1]{0:T(128)} %bitcast.4.refs_0_, bf16[3,512,768]{2,1,0:T(8,128)(2,1)} %get-tuple-element.131.refs_1_.refs_4_, bf16[2,512,768]{2,1,0:T(8,128)(2,1)} %get-tuple-element.147.refs_2_, bf16[3,512,768]{2,1,0:T(8,128)(2,1)} %collective-permute-done.2.refs_3_.refs_5_, ...), custom_call_target="tpu_custom_call" | custom-call | flops 3449999872 | tf_op jit(solution)/shard_map/feed_grads/pallas_call | solution.py:134
  105.3 10.6 %own_back.3 = (bf16[512,384]{1,0:T(8,128)(2,1)}, f32[512,384]{1,0:T(8,128)}, f32[512,384]{1,0:T(8,128)}) custom-call(s32[8]{0:T(128)} %get-tuple-element.119.refs_0_.refs_1_, s32[8]{0:T(128)} %get-tuple-element.129.refs_1_.refs_2_, bf16[512,768]{1,0:T(8,128)(2,1)} %get-tuple-element.151.refs_13_.refs_2_, ...), custom_call_target="tpu_custom_call" | custom-call | flops 5750000128 | tf_op jit(solution)/shard_map/own_back/pallas_call | solution.py:134
  116.9 8.4 %other_back.1 = (bf16[512,384]{1,0:T(8,128)(2,1)}, bf16[512,384]{1,0:T(8,128)(2,1)}, bf16[512,384]{1,0:T(8,128)(2,1)}, bf16[512,384]{1,0:T(8,128)(2,1)}, bf16[51...) custom-call(s32[1]{0:T(128)} %bitcast.3.refs_1_.refs_0_, ...), custom_call_target="tpu_custom_call" | custom-call | flops 1150000000 | tf_op jit(solution)/shard_map/other_back/pallas_call | solution.py:134
  125.3 2.4 collective-permute-start.9
  134.6 8.2 %last_grads.1 = (bf16[384,1536]{1,0:T(8,128)(2,1)}, bf16[384,1536]{1,0:T(8,128)(2,1)}) custom-call(s32[1]{0:T(128)} %bitcast.3.refs_1_.refs_0_, s32[1]{0:T(128)} %bitcast.5.refs_1_, bf16[512,768]{1,0:T(8,128)(2,1)} %get-tuple-element.169.refs_2_, bf16[512,768]{1,0:T(8,128)(2,1)} %collective-permute-done.8.refs_3_, ...), custom_call_target="tpu_custom_call" | custom-call | flops 9200000000 | tf_op jit(solution)/shard_map/last_grads/pallas_call | solution.py:134
  144.6 3.2 %collective-permute-done.7 = bf16[384,1536]{1,0:T(8,128)(2,1)} collective-permute-done((bf16[384,1536]{1,0:T(8,128)(2,1)}, bf16[384,1536]{1,0:T(8,128)(2,1)}, u32[]{:S(2)}, u32[]{:S(2)}) %collective-permute-start.7) | collective-permute-done | bytes 1179680 | tf_op jit(solution)/shard_map/ppermute | solution.py:834
  151.8 6.5 %token_out.1 = (bf16[944,768]{1,0:T(8,128)(2,1)}, f32[512,768]{1,0:T(8,128)}, f32[16,768]{1,0:T(8,128)}) custom-call(bf16[1,768]{1,0:T(2,128)(2,1)} %reshape.96.refs_0_, bf16[1,768]{1,0:T(2,128)(2,1)} %reshape.97.refs_5_.refs_1_, f32[512,768]{1,0:T(8,128)} %get-tuple-element.126.refs_2_, f32[512,768]{1,0:T(8,128)} %get-tuple-element.127.refs_3_, ...), custom_call_target="tpu_custom_call" | custom-call | flops 1150000000 | tf_op jit(solution)/shard_map/token_out/pallas_call | solution.py:134
  158.3 9.8 %token_grad.1 = (bf16[944,768]{1,0:T(8,128)(2,1)}, f32[16,768]{1,0:T(8,128)}) custom-call(bf16[1,768]{1,0:T(2,128)(2,1)} %reshape.106.refs_3_.refs_4_.refs_0_, bf16[512,768]{1,0:T(8,128)(2,1)} %get-tuple-element.184.refs_6_.refs_1_, bf16[768,2304]{1,0:T(8,128)(2,1)} %refs_2_.1, bf16[512,768]{1,0:T(8,128)(2,1)} %get-tuple-element.171.refs_7_.refs_3_, ...), custom_call_target="tpu_custom_call" | custom-call | flops 16099999744 | tf_op jit(solution)/shard_map/token_grad/pallas_call | solution.py:134
  169.2 3.0 collective-permute-start.16
  175.7 9.5 %collective-permute-done.16 = bf16[96,1536]{1,0:T(8,128)(2,1)S(1)} collective-permute-done((bf16[96,1536]{1,0:T(8,128)(2,1)S(1)}, bf16[96,1536]{1,0:T(8,128)(2,1)S(1)}, u32[]{:S(2)}, u32[]{:S(2)}) %collective-permute-start.16) | collective-permute-done | bytes 294944 | tf_op jit(solution)/shard_map/ppermute | solution.py:834
  187.2 13.0 %collective-permute-done.17 = bf16[96,1536]{1,0:T(8,128)(2,1)S(1)} collective-permute-done((bf16[96,1536]{1,0:T(8,128)(2,1)S(1)}, bf16[96,1536]{1,0:T(8,128)(2,1)S(1)}, u32[]{:S(2)}, u32[]{:S(2)}) %collective-permute-start.17) | collective-permute-done | bytes 294944 | tf_op jit(solution)/shard_map/ppermute | solution.py:834
  202.0 14.5 %collective-permute-done.18 = bf16[192,1536]{1,0:T(8,128)(2,1)S(1)} collective-permute-done((bf16[192,1536]{1,0:T(8,128)(2,1)}, bf16[192,1536]{1,0:T(8,128)(2,1)S(1)}, u32[]{:S(2)}, u32[]{:S(2)}) %collective-permute-start.18) | collective-permute-done | bytes 589856 | tf_op jit(solution)/shard_map/ppermute | solution.py:834
  218.1 10.1 %collective-permute-done.19 = bf16[112,1536]{1,0:T(8,128)(2,1)} collective-permute-done((bf16[112,1536]{1,0:T(8,128)(2,1)}, bf16[112,1536]{1,0:T(8,128)(2,1)}, u32[]{:S(2)}, u32[]{:S(2)}) %collective-permute-start.19) | collective-permute-done | bytes 344096 | tf_op jit(solution)/shard_map/ppermute | solution.py:834
  229.3 3.6 %collective-permute-done.21 = bf16[384,1536]{1,0:T(8,128)(2,1)} collective-permute-done((bf16[384,1536]{1,0:T(8,128)(2,1)S(1)}, bf16[384,1536]{1,0:T(8,128)(2,1)}, u32[]{:S(2)}, u32[]{:S(2)}) %collective-permute-start.21) | collective-permute-done | bytes 1179680 | tf_op jit(solution)/shard_map/ppermute | solution.py:834
  232.9 2.8 pad_maximum_fusion.rest_0_
  239.7 9.1 %collective-permute-done.20 = bf16[64,1536]{1,0:T(8,128)(2,1)S(1)} collective-permute-done((bf16[64,1536]{1,0:T(8,128)(2,1)S(1)}, bf16[64,1536]{1,0:T(8,128)(2,1)S(1)}, u32[]{:S(2)}, u32[]{:S(2)}) %collective-permute-start.20) | collective-permute-done | bytes 196640 | tf_op jit(solution)/shard_map/ppermute | solution.py:834
  249.6 9.4 %collective-permute-done.22 = bf16[48,1536]{1,0:T(8,128)(2,1)S(1)} collective-permute-done((bf16[48,1536]{1,0:T(8,128)(2,1)S(1)}, bf16[48,1536]{1,0:T(8,128)(2,1)S(1)}, u32[]{:S(2)}, u32[]{:S(2)}) %collective-permute-start.22) | collective-permute-done | bytes 147488 | tf_op jit(solution)/shard_map/ppermute | solution.py:834
  259.7 8.3 %collective-permute-done.23 = bf16[96,1536]{1,0:T(8,128)(2,1)S(1)} collective-permute-done((bf16[96,1536]{1,0:T(8,128)(2,1)S(1)}, bf16[96,1536]{1,0:T(8,128)(2,1)S(1)}, u32[]{:S(2)}, u32[]{:S(2)}) %collective-permute-start.23) | collective-permute-done | bytes 294944 | tf_op jit(solution)/shard_map/ppermute | solution.py:834
  268.0 2.1 collective-permute-start.24
  270.1 6.0 %place.5 = (f32[768,3072]{1,0:T(8,128)}, f32[3072,768]{1,0:T(8,128)}) custom-call(s32[6]{0:T(128)} %stack.73.info_ref, bf16[768,1536]{1,0:T(8,128)(2,1)} %pad_maximum_fusion.rest_0_, bf16[768,1536]{1,0:T(8,128)(2,1)} %collective-permute-done.26.rest_1_), custom_call_target="tpu_custom_call" | custom-call | flops 1150000000 | tf_op jit(solution)/shard_map/place/pallas_call | solution.py:1040
  283.0 4.5 %place.6 = (f32[768,2304]{1,0:T(8,128)}, f32[768,768]{1,0:T(8,128)}) custom-call(s32[6]{0:T(128)} %stack.80.info_ref, bf16[384,1536]{1,0:T(8,128)(2,1)} %copy-done.1, bf16[384,1536]{1,0:T(8,128)(2,1)} %collective-permute-done.29.rest_1_), custom_call_target="tpu_custom_call" | custom-call | flops 1150000000 | tf_op jit(solution)/shard_map/place/pallas_call | solution.py:1040
  287.5 6.0 %place.7 = (f32[768,3072]{1,0:T(8,128)}, f32[3072,768]{1,0:T(8,128)}) custom-call(s32[6]{0:T(128)} %stack.76.info_ref, bf16[768,1536]{1,0:T(8,128)(2,1)} %collective-permute-done.25.rest_0_, bf16[768,1536]{1,0:T(8,128)(2,1)} %collective-permute-done.28.rest_1_, ...), custom_call_target="tpu_custom_call", output_to_operand_aliasing={{0}: (3, {}), {1}: (4, {})} | custom-call | flops 1150000000 | tf_op jit(solution)/shard_map/place/pallas_call | solution.py:1040
  293.4 3.4 %collective-permute-done.27.rest_0_ = bf16[400,1536]{1,0:T(8,128)(2,1)S(1)} collective-permute-done((bf16[400,1536]{1,0:T(8,128)(2,1)}, bf16[400,1536]{1,0:T(8,128)(2,1)S(1)}, u32[]{:S(2)}, u32[]{:S(2)}) %collective-permute-start.27) | collective-permute-done | bytes 1228832 | tf_op jit(solution)/shard_map/ppermute | solution.py:834
  298.6 3.3 %place.8 = (f32[768,2304]{1,0:T(8,128)}, f32[768,768]{1,0:T(8,128)}) custom-call(s32[3]{0:T(128)} %pad_add_fusion.1.info_ref, bf16[400,1536]{1,0:T(8,128)(2,1)} %copy-done, f32[768,2304]{1,0:T(8,128)} %get-tuple-element.215.rest_1_, f32[768,768]{1,0:T(8,128)} %get-tuple-element.209.rest_2_), custom_call_target="tpu_custom_call", output_to_operand_aliasing={{0}: (2, {}), {1}: (3, {})} | custom-call | flops 1150000000 | tf_op jit(solution)/shard_map/place/pallas_call | solution.py:1040
  303.3 3.3 %place.9 = (f32[768,2304]{1,0:T(8,128)}, f32[768,768]{1,0:T(8,128)}) custom-call(s32[3]{0:T(128)} %pad_add_fusion.info_ref, bf16[400,1536]{1,0:T(8,128)(2,1)} %collective-permute-done.30.rest_0_, f32[768,2304]{1,0:T(8,128)} %get-tuple-element.218.rest_1_, f32[768,768]{1,0:T(8,128)} %get-tuple-element.216.rest_2_), custom_call_target="tpu_custom_call", output_to_operand_aliasing={{0}: (2, {}), {1}: (3, {})} | custom-call | flops 1150000000 | tf_op jit(solution)/shard_map/place/pallas_call | solution.py:1040
  (152 shorter events, 52.5 us)
Async XLA Ops:
  9.8 22.3 %collective-permute-start = (bf16[528,768]{1,0:T(8,128)(2,1)}, bf16[528,768]{1,0:T(8,128)(2,1)S(1)}, u32[]{:S(2)}, u32[]{:S(2)}) collective-permute-start(bf16[528,768]{1,0:T(8,128)(2,1)} %get-tuple-element.120.refs_6_.refs_12_.refs_4_.refs_5_), channel_id=1, source_target_pairs={{0,1},{1,0},{2,3},{3,2},{4,5},{5,4},{6,7},{7,6},{8,9},{9,8},{10,11... | collective-permute-start | bytes 2433032 | tf_op jit(solution)/shard_map/ppermute | solution.py:834
  72.4 11.6 %collective-permute-start.2 = (bf16[3,512,768]{2,1,0:T(8,128)(2,1)}, bf16[3,512,768]{2,1,0:T(8,128)(2,1)}, u32[]{:S(2)}, u32[]{:S(2)}) collective-permute-start(bf16[3,512,768]{2,1,0:T(8,128)(2,1)} %get-tuple-element.131.refs_1_.refs_4_), channel_id=1, source_target_pairs={{0,2},{1,3},{2,0},{3,1},{4,6},{5,7},{6,4},{7,5},{8,10},{9,11},{10,... | collective-permute-start | bytes 7077896 | tf_op jit(solution)/shard_map/ppermute | solution.py:834
  72.5 11.5 %collective-permute-start.3 = (bf16[2,512,768]{2,1,0:T(8,128)(2,1)}, bf16[2,512,768]{2,1,0:T(8,128)(2,1)}, u32[]{:S(2)}, u32[]{:S(2)}) collective-permute-start(bf16[2,512,768]{2,1,0:T(8,128)(2,1)} %get-tuple-element.133), channel_id=1, source_target_pairs={{0,2},{1,3},{2,0},{3,1},{4,6},{5,7},{6,4},{7,5},{8,10},{9,11},{10,... | collective-permute-start | bytes 4718600 | tf_op jit(solution)/shard_map/ppermute | solution.py:834
  73.0 22.3 %collective-permute-start.5 = (bf16[2,512,768]{2,1,0:T(8,128)(2,1)}, bf16[2,512,768]{2,1,0:T(8,128)(2,1)}, u32[]{:S(2)}, u32[]{:S(2)}) collective-permute-start(bf16[2,512,768]{2,1,0:T(8,128)(2,1)} %get-tuple-element.148), channel_id=1, source_target_pairs={{0,2},{1,3},{2,0},{3,1},{4,6},{5,7},{6,4},{7,5},{8,10},{9,11},{10,... | collective-permute-start | bytes 4718600 | tf_op jit(solution)/shard_map/ppermute | solution.py:834
  73.1 22.2 %collective-permute-start.1 = (bf16[576,768]{1,0:T(8,128)(2,1)}, bf16[576,768]{1,0:T(8,128)(2,1)S(1)}, u32[]{:S(2)}, u32[]{:S(2)}) collective-permute-start(bf16[576,768]{1,0:T(8,128)(2,1)} %get-tuple-element.130.refs_5_), channel_id=1, source_target_pairs={{0,1},{1,0},{2,3},{3,2},{4,5},{5,4},{6,7},{7,6},{8,9},{9,8},{10,11... | collective-permute-start | bytes 2654216 | tf_op jit(solution)/shard_map/ppermute | solution.py:834
  96.2 19.7 %collective-permute-start.4 = (bf16[768,768]{1,0:T(8,128)(2,1)}, bf16[768,768]{1,0:T(8,128)(2,1)S(1)}, u32[]{:S(2)}, u32[]{:S(2)}) collective-permute-start(bf16[768,768]{1,0:T(8,128)(2,1)} %get-tuple-element.146), channel_id=1, source_target_pairs={{0,4},{1,5},{2,3},{3,2},{4,0},{5,1},{6,7},{7,6},{8,12},{9,13},{10,... | collective-permute-start | bytes 3538952 | tf_op jit(solution)/shard_map/ppermute | solution.py:834
  104.7 20.6 %collective-permute-start.6 = (bf16[768,768]{1,0:T(8,128)(2,1)}, bf16[768,768]{1,0:T(8,128)(2,1)}, u32[]{:S(2)}, u32[]{:S(2)}) collective-permute-start(bf16[768,768]{1,0:T(8,128)(2,1)} %get-tuple-element.164), channel_id=1, source_target_pairs={{0,4},{1,5},{2,3},{3,2},{4,0},{5,1},{6,7},{7,6},{8,12},{9,13},{10,... | collective-permute-start | bytes 3538952 | tf_op jit(solution)/shard_map/ppermute | solution.py:834
  105.3 29.3 %collective-permute-start.8 = (bf16[512,768]{1,0:T(8,128)(2,1)}, bf16[512,768]{1,0:T(8,128)(2,1)}, u32[]{:S(2)}, u32[]{:S(2)}) collective-permute-start(bf16[512,768]{1,0:T(8,128)(2,1)} %get-tuple-element.169.refs_2_), channel_id=1, source_target_pairs={{0,2},{1,3},{2,0},{3,1},{4,6},{5,7},{6,4},{7,5},{8,10},{9,11},{10,... | collective-permute-start | bytes 2359304 | tf_op jit(solution)/shard_map/ppermute | solution.py:834
  125.3 6.0 %collective-permute-start.9 = (bf16[512,384]{1,0:T(8,128)(2,1)}, bf16[512,384]{1,0:T(8,128)(2,1)}, u32[]{:S(2)}, u32[]{:S(2)}) collective-permute-start(bf16[512,384]{1,0:T(8,128)(2,1)} %get-tuple-element.173), channel_id=1, source_target_pairs={{0,2},{1,3},{2,0},{3,1},{4,6},{5,7},{6,4},{7,5},{8,10},{9,11},{10,... | collective-permute-start | bytes 1179656 | tf_op jit(solution)/shard_map/ppermute | solution.py:834
  127.8 6.8 %collective-permute-start.10 = (bf16[512,384]{1,0:T(8,128)(2,1)}, bf16[512,384]{1,0:T(8,128)(2,1)}, u32[]{:S(2)}, u32[]{:S(2)}) collective-permute-start(bf16[512,384]{1,0:T(8,128)(2,1)} %get-tuple-element.175), channel_id=1, source_target_pairs={{0,2},{1,3},{2,0},{3,1},{4,6},{5,7},{6,4},{7,5},{8,10},{9,11},{10,... | collective-permute-start | bytes 1179656 | tf_op jit(solution)/shard_map/ppermute | solution.py:834
  127.9 6.8 %collective-permute-start.11 = (bf16[512,384]{1,0:T(8,128)(2,1)}, bf16[512,384]{1,0:T(8,128)(2,1)}, u32[]{:S(2)}, u32[]{:S(2)}) collective-permute-start(bf16[512,384]{1,0:T(8,128)(2,1)} %get-tuple-element.176), channel_id=1, source_target_pairs={{0,2},{1,3},{2,0},{3,1},{4,6},{5,7},{6,4},{7,5},{8,10},{9,11},{10,... | collective-permute-start | bytes 1179656 | tf_op jit(solution)/shard_map/ppermute | solution.py:834
  128.3 6.3 %collective-permute-start.12 = (bf16[512,384]{1,0:T(8,128)(2,1)}, bf16[512,384]{1,0:T(8,128)(2,1)}, u32[]{:S(2)}, u32[]{:S(2)}) collective-permute-start(bf16[512,384]{1,0:T(8,128)(2,1)} %get-tuple-element.177), channel_id=1, source_target_pairs={{0,2},{1,3},{2,0},{3,1},{4,6},{5,7},{6,4},{7,5},{8,10},{9,11},{10,... | collective-permute-start | bytes 1179656 | tf_op jit(solution)/shard_map/ppermute | solution.py:834
  131.3 16.5 %collective-permute-start.7 = (bf16[384,1536]{1,0:T(8,128)(2,1)}, bf16[384,1536]{1,0:T(8,128)(2,1)}, u32[]{:S(2)}, u32[]{:S(2)}) collective-permute-start(bf16[384,1536]{1,0:T(8,128)(2,1)} %pad_maximum_fusion.2), channel_id=1, source_target_pairs={{0,1},{1,0},{2,6},{3,7},{4,5},{5,4},{6,2},{7,3},{8,9},{9,8},{10,14... | collective-permute-start | bytes 3538952 | tf_op jit(solution)/shard_map/ppermute | solution.py:834
  142.8 30.4 %collective-permute-start.13 = (bf16[384,1536]{1,0:T(8,128)(2,1)}, bf16[384,1536]{1,0:T(8,128)(2,1)}, u32[]{:S(2)}, u32[]{:S(2)}) collective-permute-start(bf16[384,1536]{1,0:T(8,128)(2,1)} %get-tuple-element.187), channel_id=1, source_target_pairs={{0,1},{1,0},{2,6},{3,7},{4,5},{5,4},{6,2},{7,3},{8,9},{9,8},{10,14... | collective-permute-start | bytes 3538952 | tf_op jit(solution)/shard_map/ppermute | solution.py:834
  149.8 18.2 %collective-permute-start.14 = (bf16[192,1536]{1,0:T(8,128)(2,1)}, bf16[192,1536]{1,0:T(8,128)(2,1)}, u32[]{:S(2)}, u32[]{:S(2)}) collective-permute-start(bf16[192,1536]{1,0:T(8,128)(2,1)} %add_convert_fusion.3), channel_id=1, source_target_pairs={{0,8},{1,9},{2,10},{3,11},{4,12},{5,13},{6,14},{7,15},{8,0},{9,1},... | collective-permute-start | bytes 1769480 | tf_op jit(solution)/shard_map/ppermute | solution.py:834
  169.2 16.0 %collective-permute-start.16 = (bf16[96,1536]{1,0:T(8,128)(2,1)S(1)}, bf16[96,1536]{1,0:T(8,128)(2,1)S(1)}, u32[]{:S(2)}, u32[]{:S(2)}) collective-permute-start(bf16[96,1536]{1,0:T(8,128)(2,1)S(1)} %add_convert_fusion.12), channel_id=1, source_target_pairs={{0,16},{1,17},{2,18},{3,19},{4,20},{5,21},{6,22},{7,23},{8,24},{9,... | collective-permute-start | bytes 884744 | tf_op jit(solution)/shard_map/ppermute | solution.py:834
  185.3 14.9 %collective-permute-start.17 = (bf16[96,1536]{1,0:T(8,128)(2,1)S(1)}, bf16[96,1536]{1,0:T(8,128)(2,1)S(1)}, u32[]{:S(2)}, u32[]{:S(2)}) collective-permute-start(bf16[96,1536]{1,0:T(8,128)(2,1)S(1)} %add_convert_fusion.10), channel_id=1, source_target_pairs={{0,16},{1,17},{2,18},{3,19},{4,20},{5,21},{6,22},{7,23},{8,24},{9,... | collective-permute-start | bytes 884744 | tf_op jit(solution)/shard_map/ppermute | solution.py:834
  185.5 15.6 %collective-permute-start.15 = (bf16[208,1536]{1,0:T(8,128)(2,1)S(1)}, bf16[208,1536]{1,0:T(8,128)(2,1)S(1)}, u32[]{:S(2)}, u32[]{:S(2)}) collective-permute-start(bf16[208,1536]{1,0:T(8,128)(2,1)S(1)} %maximum_maximum_fusion), channel_id=1, source_target_pairs={{0,4},{1,5},{2,3},{3,2},{4,0},{5,1},{6,7},{7,6},{8,12},{9,13},{10,... | collective-permute-start | bytes 1916936 | tf_op jit(solution)/shard_map/ppermute | solution.py:834
  201.0 15.5 %collective-permute-start.18 = (bf16[192,1536]{1,0:T(8,128)(2,1)}, bf16[192,1536]{1,0:T(8,128)(2,1)S(1)}, u32[]{:S(2)}, u32[]{:S(2)}) collective-permute-start(bf16[192,1536]{1,0:T(8,128)(2,1)} %pad_maximum_fusion.5), channel_id=1, source_target_pairs={{0,8},{1,9},{2,10},{3,11},{4,12},{5,13},{6,14},{7,15},{8,0},{9,1},... | collective-permute-start | bytes 1769480 | tf_op jit(solution)/shard_map/ppermute | solution.py:834
  216.6 16.4 %collective-permute-start.21 = (bf16[384,1536]{1,0:T(8,128)(2,1)S(1)}, bf16[384,1536]{1,0:T(8,128)(2,1)}, u32[]{:S(2)}, u32[]{:S(2)}) collective-permute-start(bf16[384,1536]{1,0:T(8,128)(2,1)S(1)} %pad_maximum_fusion.3), channel_id=1, source_target_pairs={{0,1},{1,0},{2,6},{3,7},{4,5},{5,4},{6,2},{7,3},{8,9},{9,8},{10,14... | collective-permute-start | bytes 3538952 | tf_op jit(solution)/shard_map/ppermute | solution.py:834
  217.7 10.5 %collective-permute-start.19 = (bf16[112,1536]{1,0:T(8,128)(2,1)}, bf16[112,1536]{1,0:T(8,128)(2,1)}, u32[]{:S(2)}, u32[]{:S(2)}) collective-permute-start(bf16[112,1536]{1,0:T(8,128)(2,1)} %maximum_maximum_fusion.1), channel_id=1, source_target_pairs={{0,8},{1,9},{2,10},{3,11},{4,12},{5,13},{6,14},{7,15},{8,0},{9,1},... | collective-permute-start | bytes 1032200 | tf_op jit(solution)/shard_map/ppermute | solution.py:834
  235.8 34.3 %collective-permute-start.26 = (bf16[768,1536]{1,0:T(8,128)(2,1)}, bf16[768,1536]{1,0:T(8,128)(2,1)}, u32[]{:S(2)}, u32[]{:S(2)}) collective-permute-start(bf16[768,1536]{1,0:T(8,128)(2,1)} %pad_maximum_fusion.rest_0_), channel_id=1, source_target_pairs={{0,2},{1,3},{2,0},{3,1},{4,6},{5,7},{6,4},{7,5},{8,10},{9,11},{10,... | collective-permute-start | bytes 7077896 | tf_op jit(solution)/shard_map/ppermute | solution.py:834
  235.8 40.3 %collective-permute-start.25 = (bf16[768,1536]{1,0:T(8,128)(2,1)}, bf16[768,1536]{1,0:T(8,128)(2,1)}, u32[]{:S(2)}, u32[]{:S(2)}) collective-permute-start(bf16[768,1536]{1,0:T(8,128)(2,1)} %pad_maximum_fusion.rest_0_), channel_id=1, source_target_pairs={{0,4},{1,5},{2,3},{3,2},{4,0},{5,1},{6,7},{7,6},{8,12},{9,13},{10,... | collective-permute-start | bytes 7077896 | tf_op jit(solution)/shard_map/ppermute | solution.py:834
  238.2 10.6 %collective-permute-start.20 = (bf16[64,1536]{1,0:T(8,128)(2,1)S(1)}, bf16[64,1536]{1,0:T(8,128)(2,1)S(1)}, u32[]{:S(2)}, u32[]{:S(2)}) collective-permute-start(bf16[64,1536]{1,0:T(8,128)(2,1)S(1)} %maximum_maximum_fusion.2), channel_id=1, source_target_pairs={{0,16},{1,17},{2,18},{3,19},{4,20},{5,21},{6,22},{7,23},{8,24},{9,... | collective-permute-start | bytes 589832 | tf_op jit(solution)/shard_map/ppermute | solution.py:834
  249.5 9.4 %collective-permute-start.22 = (bf16[48,1536]{1,0:T(8,128)(2,1)S(1)}, bf16[48,1536]{1,0:T(8,128)(2,1)S(1)}, u32[]{:S(2)}, u32[]{:S(2)}) collective-permute-start(bf16[48,1536]{1,0:T(8,128)(2,1)S(1)} %get-tuple-element.234), channel_id=1, source_target_pairs={{0,16},{1,17},{2,18},{3,19},{4,20},{5,21},{6,22},{7,23},{8,24},{9,... | collective-permute-start | bytes 442376 | tf_op jit(solution)/shard_map/ppermute | solution.py:834
  259.0 9.0 %collective-permute-start.23 = (bf16[96,1536]{1,0:T(8,128)(2,1)S(1)}, bf16[96,1536]{1,0:T(8,128)(2,1)S(1)}, u32[]{:S(2)}, u32[]{:S(2)}) collective-permute-start(bf16[96,1536]{1,0:T(8,128)(2,1)S(1)} %pad_maximum_fusion.7), channel_id=1, source_target_pairs={{0,8},{1,9},{2,10},{3,11},{4,12},{5,13},{6,14},{7,15},{8,0},{9,1},... | collective-permute-start | bytes 884744 | tf_op jit(solution)/shard_map/ppermute | solution.py:834
  268.0 10.0 %collective-permute-start.24 = (bf16[192,1536]{1,0:T(8,128)(2,1)S(1)}, bf16[192,1536]{1,0:T(8,128)(2,1)S(1)}, u32[]{:S(2)}, u32[]{:S(2)}) collective-permute-start(bf16[192,1536]{1,0:T(8,128)(2,1)S(1)} %pad_maximum_fusion.6), channel_id=1, source_target_pairs={{0,4},{1,5},{2,3},{3,2},{4,0},{5,1},{6,7},{7,6},{8,12},{9,13},{10,... | collective-permute-start | bytes 1769480 | tf_op jit(solution)/shard_map/ppermute | solution.py:834
  276.1 11.4 %collective-permute-start.28 = (bf16[768,1536]{1,0:T(8,128)(2,1)}, bf16[768,1536]{1,0:T(8,128)(2,1)}, u32[]{:S(2)}, u32[]{:S(2)}) collective-permute-start(bf16[768,1536]{1,0:T(8,128)(2,1)} %collective-permute-done.25.rest_0_), channel_id=1, source_target_pairs={{0,2},{1,3},{2,0},{3,1},{4,6},{5,7},{6,4},{7,5},{8,10},{9,11},{10,... | collective-permute-start | bytes 7077896 | tf_op jit(solution)/shard_map/ppermute | solution.py:834
  278.1 4.9 %collective-permute-start.29 = (bf16[384,1536]{1,0:T(8,128)(2,1)S(1)}, bf16[384,1536]{1,0:T(8,128)(2,1)}, u32[]{:S(2)}, u32[]{:S(2)}) collective-permute-start(bf16[384,1536]{1,0:T(8,128)(2,1)S(1)} %pad_maximum_fusion.4.rest_0_), channel_id=1, source_target_pairs={{0,2},{1,3},{2,0},{3,1},{4,6},{5,7},{6,4},{7,5},{8,10},{9,11},{10,... | collective-permute-start | bytes 3538952 | tf_op jit(solution)/shard_map/ppermute | solution.py:834
  279.9 16.9 %collective-permute-start.27 = (bf16[400,1536]{1,0:T(8,128)(2,1)}, bf16[400,1536]{1,0:T(8,128)(2,1)S(1)}, u32[]{:S(2)}, u32[]{:S(2)}) collective-permute-start(bf16[400,1536]{1,0:T(8,128)(2,1)} %maximum_dynamic-update-slice_fusion), channel_id=1, source_target_pairs={{0,1},{1,0},{2,6},{3,7},{4,5},{5,4},{6,2},{7,3},{8,9},{9,8},{10,14... | collective-permute-start | bytes 3686408 | tf_op jit(solution)/shard_map/ppermute | solution.py:834
  296.8 6.4 %collective-permute-start.30 = (bf16[400,1536]{1,0:T(8,128)(2,1)S(1)}, bf16[400,1536]{1,0:T(8,128)(2,1)}, u32[]{:S(2)}, u32[]{:S(2)}) collective-permute-start(bf16[400,1536]{1,0:T(8,128)(2,1)S(1)} %collective-permute-done.27.rest_0_), channel_id=1, source_target_pairs={{0,2},{1,3},{2,0},{3,1},{4,6},{5,7},{6,4},{7,5},{8,10},{9,11},{10,... | collective-permute-start | bytes 3686408 | tf_op jit(solution)/shard_map/ppermute | solution.py:834
  298.1 3.8 %collective-permute-start.31 = (f32[16,768]{1,0:T(8,128)S(1)}, f32[16,768]{1,0:T(8,128)S(1)}, u32[]{:S(2)}, u32[]{:S(2)}) collective-permute-start(f32[16,768]{1,0:T(8,128)S(1)} %add_add_fusion), channel_id=1, source_target_pairs={{0,2},{1,3},{2,0},{3,1},{4,6},{5,7},{6,4},{7,5},{8,10},{9,11},{10,... | collective-permute-start | bytes 147464 | tf_op jit(solution)/shard_map/ppermute | solution.py:834
  (22 other events, 152.9 us)
